TPU v7x, 32 devices: a whole 2x2x4 slice. The times are simulated.
32 devices in a mesh: sim: 8 (over z, x), learn: 4 (over y, core).
Axes of the slice: x: 2, y: 2, z: 4, core: 2. Of those that a mesh axis runs over, the one named last changes fastest.
Arguments:
- fields: float32 [8, 64, 32, 128], P(None, 'sim', 'learn'), may hold values from -2.2 to 2.2
- diffusivity: float32 [8], replicated, may hold values from 0.5 to 1.6
- stoich: float32 [8], replicated, may hold values from -1 to 1
- basis: bfloat16 [96, 8, 64, 32, 128], P(None, None, 'sim', 'learn'), may hold values from -0.0124296114 to 0.0124296114
- gram_old: float32 [96, 96], replicated, may hold values from -6 to 6
Outputs:
- final_fields: float32 [8, 64, 32, 128], P(None, 'sim', 'learn')
- reduced: float32 [96, 8], replicated
- pod_gram: float32 [96, 96], replicated
- rhs_block: float32 [4752, 96], P('learn')
All inputs are finite; a program needn't handle non-finite values.
Results may differ from a plain program's by a relative error of at most 0.0077.
Values sent between devices are 32-bit elements; how exact they have to be, the bound alone decides.
No kernel may reach another device: no remote copies, remote signals or barrier semaphores. Data moves between devices by JAX's collectives and lax.ppermute only.
A program may use at most 64 MiB of HBM per device.

v0:
```python
import functools

import jax
import jax.numpy as jnp
import numpy as np
from jax import lax
from jax.experimental import pallas as pl
from jax.experimental.pallas import tpu as pltpu
from jax.sharding import PartitionSpec as P

STEPS = 8

time_step = 0.1
drift_x = 1.2
drift_y = 1.0
drift_z = 0.3
arrhenius = 2.0
activation = 1.0

BOTH = ("sim", "learn")
VMEM = pl.BlockSpec(memory_space=pltpu.VMEM)
WIDE = 56 * 1024 * 1024


def both_ways(pairs):
    return [(a, b) for a, b in pairs] + [(b, a) for a, b in pairs]


def swaps(ns, nl):
    x_even = both_ways([(s * nl + l, (s + 1) * nl + l) for s in range(0, ns, 2) for l in range(nl)])
    x_odd = [(s * nl + l, (s + 1) * nl + l) for s in range(1, ns - 1, 2) for l in range(nl)]
    x_odd += [(s * nl + l, s * nl + l + 1) for s in (0, ns - 1) for l in range(0, nl, 2)]
    y_even = both_ways([(s * nl + l, s * nl + l + 1) for s in range(ns) for l in range(0, nl, 2)])
    y_odd = [(s * nl + l, s * nl + l + 1) for s in range(ns) for l in range(1, nl - 1, 2)]
    y_odd += [(s * nl, s * nl + nl - 1) for s in range(ns)]
    return x_even, both_ways(x_odd), y_even, both_ways(y_odd)


def corner_cells(reach):
    return [(d, e) for d in range(1, reach + 1) for e in range(1, reach + 1 - d)]


def pack_kernel(cx, cy, xa_ref, xb_ref, to_a_ref, to_b_ref):
    nf = to_a_ref.shape[1]
    even_s = lax.rem(lax.axis_index("sim"), 2) == 0
    even_l = lax.rem(lax.axis_index("learn"), 2) == 0
    cells = corner_cells(min(cx, cy))
    for side, brick in enumerate((xa_ref, xb_ref)):
        is_east = even_s if side == 0 else jnp.logical_not(even_s)
        for n, (d, e) in enumerate(cells):
            row = jnp.where(is_east, d - 1, cx - d) * cy
            high, low = row + cy - e, row + e - 1
            for out_ref, north in ((to_a_ref, even_l), (to_b_ref, jnp.logical_not(even_l))):
                start = jnp.where(north, high, low)
                out_ref[side * len(cells) + n] = brick[pl.ds(start, nf, stride=cx * cy), :]


def pack_corners(xa, xb, cx, cy, nf, nz):
    count = 2 * len(corner_cells(min(cx, cy)))
    shape = jax.ShapeDtypeStruct((count, nf, nz), jnp.float32)
    return pl.pallas_call(
        functools.partial(pack_kernel, cx, cy),
        out_shape=(shape, shape),
        in_specs=[VMEM, VMEM],
        out_specs=(VMEM, VMEM),
        name="pack_corners",
    )(xa, xb)


def rows_loop(start, count, group, body):
    main = count // group

    def trip(i, carry):
        for k in range(group):
            body(start + i * group + k)
        return carry

    lax.fori_loop(0, main, trip, 0)
    for k in range(main * group, count):
        body(start + k)


def round_kernel(
    cx, cy, steps, own_ref, xa_ref, xb_ref, ya_ref, yb_ref, ca_ref, cb_ref, dif_ref, sto_ref,
    state_ref, snap_ref, u_ref, m_ref, rate_ref,
):
    nf, nz = dif_ref.shape
    reach = 2 * steps
    wide_x, wide_y = cx + 2 * reach, cy + 2 * reach
    s, l = lax.axis_index("sim"), lax.axis_index("learn")
    ns, nl = lax.axis_size("sim"), lax.axis_size("learn")
    even_s, even_l = lax.rem(s, 2) == 0, lax.rem(l, 2) == 0
    has_west, has_east = s > 0, s < ns - 1
    has_south, has_north = l > 0, l < nl - 1

    def column(x, y):
        return pl.multiple_of((x * wide_y + y) * nf, nf)

    zero = jnp.zeros((nf, nz), jnp.float32)

    def clear(i, carry):
        for k in range(wide_y):
            u_ref[pl.ds(column(i, k), nf), :] = zero
            m_ref[pl.ds(column(i, k), nf), :] = zero
        return carry

    lax.fori_loop(0, wide_x, clear, 0)

    def place(ref, x0, y0, first_x, first_y, size_x, size_y):
        def trip(i, carry):
            for j in range(size_y):
                value = ref[pl.ds((first_x + i) * cy + first_y + j, nf, stride=cx * cy), :]
                u_ref[pl.ds(column(x0 + i, y0 + j), nf), :] = value
            return carry

        lax.fori_loop(0, size_x, trip, 0)

    place(own_ref, reach, reach, 0, 0, cx, cy)
    for ref, is_east in ((xa_ref, even_s), (xb_ref, jnp.logical_not(even_s))):

        @pl.when(jnp.where(is_east, has_east, has_west))
        def _(ref=ref, is_east=is_east):
            place(ref, jnp.where(is_east, reach + cx, 0), reach, jnp.where(is_east, 0, cx - reach), 0, reach, cy)

    for ref, is_north in ((ya_ref, even_l), (yb_ref, jnp.logical_not(even_l))):

        @pl.when(jnp.where(is_north, has_north, has_south))
        def _(ref=ref, is_north=is_north):
            place(ref, reach, jnp.where(is_north, reach + cy, 0), 0, jnp.where(is_north, 0, cy - reach), cx, reach)

    cells = corner_cells(reach)
    for ref, is_north in ((ca_ref, even_l), (cb_ref, jnp.logical_not(even_l))):
        for side, is_east in ((0, even_s), (1, jnp.logical_not(even_s))):
            has_y = jnp.where(is_north, has_north, has_south)
            has_x = jnp.where(is_east, has_east, has_west)

            @pl.when(jnp.logical_and(has_x, has_y))
            def _(ref=ref, is_north=is_north, side=side, is_east=is_east):
                for n, (d, e) in enumerate(cells):
                    x = jnp.where(is_east, reach + cx + d - 1, reach - d)
                    y = jnp.where(is_north, reach + cy + e - 1, reach - e)
                    u_ref[pl.ds(column(x, y), nf), :] = ref[side * len(cells) + n]

    diffusivity, stoich = dif_ref[...], sto_ref[...]
    lane = lax.broadcasted_iota(jnp.int32, (nf, nz), 1)

    def coefficients(dt):
        return (
            1.0 * (dt / time_step) - 6.0 * dt * diffusivity,
            dt * (diffusivity - 0.5 * drift_x),
            dt * (diffusivity + 0.5 * drift_x),
            dt * (diffusivity - 0.5 * drift_y),
            dt * (diffusivity + 0.5 * drift_y),
            jnp.where(lane < nz - 1, dt * (diffusivity - 0.5 * drift_z), 0.0),
            jnp.where(lane > 0, dt * (diffusivity + 0.5 * drift_z), 0.0),
            dt * arrhenius * stoich,
        )

    in_south = jnp.where(has_south, 1.0, 0.0)
    in_north = jnp.where(has_north, 1.0, 0.0)

    def stage(src, dst, old, r, coefs):
        cc, ce, cw, cn, cs, cu, cl, ck = coefs
        y_first, width = reach - r, cy + 2 * r
        packs = -(-width // nf)

        def rate_row(x):
            for p in range(packs):
                base = (x * wide_y + y_first + p * nf) * nf
                u0 = src[pl.ds(base, nf, stride=nf), :]
                u1 = src[pl.ds(base + 1, nf, stride=nf), :]
                u7 = src[pl.ds(base + 7, nf, stride=nf), :]
                rate = jnp.tanh(u0) * jnp.tanh(u1) * jnp.exp(-activation / (1.0 + u7 * u7))
                rate_ref[pl.ds(pl.multiple_of(x * (wide_y + nf) + p * nf, nf), nf), :] = rate

        rows_loop(reach - r, cx + 2 * r, max(1, 12 // packs), rate_row)

        def columns_row(x):
            here = [src[pl.ds(column(x, y_first - 1 + j), nf), :] for j in range(2)]
            for j in range(width):
                y = y_first + j
                south, centre = here
                north = src[pl.ds(column(x, y + 1), nf), :]
                value = cc * centre + cn * north + cs * south
                value += ce * src[pl.ds(column(x + 1, y), nf), :] + cw * src[pl.ds(column(x - 1, y), nf), :]
                value += cu * pltpu.roll(centre, nz - 1, 1) + cl * pltpu.roll(centre, 1, 1)
                value += ck * rate_ref[pl.ds(x * (wide_y + nf) + j, nf, stride=0), :]
                if old is not None:
                    value += 0.5 * old[pl.ds(column(x, y), nf), :]
                if y < reach:
                    value *= in_south
                if y >= reach + cy:
                    value *= in_north
                dst[pl.ds(column(x, y), nf), :] = value
                here = [centre, north]

        low = jnp.where(has_west, reach - r, reach)
        high = jnp.where(has_east, reach + cx + r, reach + cx)

        def trip(x, carry):
            columns_row(x)
            return carry

        lax.fori_loop(low, high, trip, 0)

    whole, half = coefficients(time_step), coefficients(0.5 * time_step)
    for t in range(steps):
        r = reach - 1 - 2 * t
        stage(u_ref, m_ref, None, r, whole)
        stage(m_ref, u_ref, u_ref, r - 1, half)
        for x in range(cx):
            for f in range(nf):
                value = u_ref[pl.ds(((reach + x) * wide_y + reach) * nf + f, cy, stride=nf), :]
                snap_ref[f * cx + x, pl.ds(t * cy, cy), :] = value
                if t == steps - 1:
                    state_ref[pl.ds((f * cx + x) * cy, cy), :] = value


def advance(state, neighbours, corners, dif, sto, steps):
    nf, cx, cy, nz = state.shape
    wide = (cx + 4 * steps) * (cy + 4 * steps)
    flat = [a.reshape(nf * cx * cy, nz) for a in (state, *neighbours)]
    new, snaps = pl.pallas_call(
        functools.partial(round_kernel, cx, cy, steps),
        out_shape=(
            jax.ShapeDtypeStruct((nf * cx * cy, nz), jnp.float32),
            jax.ShapeDtypeStruct((nf * cx, steps * cy, nz), jnp.float32),
        ),
        in_specs=[VMEM] * 9,
        out_specs=(VMEM, VMEM),
        scratch_shapes=[
            pltpu.VMEM((wide * nf + 8 * nf, nz), jnp.float32),
            pltpu.VMEM((wide * nf + 8 * nf, nz), jnp.float32),
            pltpu.VMEM(((cx + 4 * steps) * (cy + 4 * steps + nf), nz), jnp.float32),
        ],
        name="advance",
    )(*flat, *corners, dif, sto)
    return new.reshape(state.shape), snaps


def project_kernel(cy, steps, basis_ref, snap_ref, out_ref, acc_ref):
    modes, pair, cells, nz = basis_ref.shape
    cx = cells // cy
    step = pl.program_id(0)

    @pl.when(step == 0)
    def _():
        acc_ref[...] = jnp.zeros_like(acc_ref)

    total = None
    for p in range(cx // 2):
        left = [basis_ref[:, f, pl.ds(p * 2 * cy, 2 * cy), :].reshape(modes * 2 * cy, nz) for f in range(pair)]
        right = [
            snap_ref[pl.ds(f * cx + 2 * p, 2)].reshape(2 * steps * cy, nz).astype(jnp.bfloat16) for f in range(pair)
        ]
        term = lax.dot_general(
            jnp.concatenate(left, axis=1),
            jnp.concatenate(right, axis=1),
            (((1,), (1,)), ((), ())),
            preferred_element_type=jnp.float32,
        )
        total = term if total is None else total + term
    acc_ref[...] += total

    @pl.when(step == pl.num_programs(0) - 1)
    def _():
        columns = 2 * steps * cy
        row = lax.broadcasted_iota(jnp.int32, (2 * cy, columns), 0)
        column = lax.broadcasted_iota(jnp.int32, (2 * cy, columns), 1)
        same = (row // cy == column // (steps * cy)) & (row % cy == column % cy)
        kept = acc_ref[...].reshape(modes, 2 * cy, columns) * same.astype(jnp.float32)[None]
        kept = jnp.sum(kept, axis=1)
        which = lax.broadcasted_iota(jnp.int32, (steps, columns), 0)
        column = lax.broadcasted_iota(jnp.int32, (steps, columns), 1)
        gather = (column // cy % steps == which).astype(jnp.float32)
        out_ref[...] = lax.dot_general(
            gather, kept, (((1,), (1,)), ((), ())),
            precision=lax.Precision.HIGHEST, preferred_element_type=jnp.float32,
        )


def project(basis, snaps, steps):
    modes, nf, cx, cy, nz = basis.shape
    pair = 2
    return pl.pallas_call(
        functools.partial(project_kernel, cy, steps),
        out_shape=jax.ShapeDtypeStruct((steps, modes), jnp.float32),
        grid=(nf // pair,),
        in_specs=[
            pl.BlockSpec((modes, pair, cx * cy, nz), lambda i: (0, i, 0, 0)),
            pl.BlockSpec((pair * cx, steps * cy, nz), lambda i: (i, 0, 0)),
        ],
        out_specs=pl.BlockSpec((steps, modes), lambda i: (0, 0)),
        scratch_shapes=[pltpu.VMEM((modes * 2 * cy, 2 * steps * cy), jnp.float32)],
        compiler_params=pltpu.CompilerParams(vmem_limit_bytes=WIDE),
        name="project",
    )(basis.reshape(modes, nf, cx * cy, nz), snaps)


def pair_tables(modes):
    upper_pairs = np.triu_indices(modes)
    first_table = np.concatenate([np.zeros(modes), upper_pairs[0] + 1]).astype(np.int32)
    second_table = np.concatenate([np.arange(modes) + 1, upper_pairs[1] + 1]).astype(np.int32)
    return (first_table, second_table)


def body(fields, diffusivity, stoich, basis, gram_old):
    modes = basis.shape[0]
    nf, cx, cy, nz = fields.shape
    ns, nl = lax.axis_size("sim"), lax.axis_size("learn")
    steps = min(cx, cy) // 2
    x_even, x_odd, y_even, y_odd = swaps(ns, nl)
    dif = jnp.broadcast_to(diffusivity[:, None], (nf, nz))
    sto = jnp.broadcast_to(stoich[:, None], (nf, nz))
    state = fields
    parts = []
    for _ in range(STEPS // steps):
        ya = lax.ppermute(state, BOTH, y_even)
        yb = lax.ppermute(state, BOTH, y_odd)
        xa = lax.ppermute(state, BOTH, x_even)
        xb = lax.ppermute(state, BOTH, x_odd)
        to_a, to_b = pack_corners(xa.reshape(-1, nz), xb.reshape(-1, nz), cx, cy, nf, nz)
        ca = lax.ppermute(to_a, BOTH, y_even)
        cb = lax.ppermute(to_b, BOTH, y_odd)
        state, snaps = advance(state, (xa, xb, ya, yb), (ca, cb), dif, sto, steps)
        parts.append(project(basis, snaps, steps))
    local = jnp.concatenate(parts, axis=0)
    sent = jnp.broadcast_to(local[None], (ns * nl, *local.shape))
    reduced_t = jnp.sum(lax.all_to_all(sent, BOTH, 0, 0), axis=0)
    reduced = reduced_t.T
    pod_gram = gram_old + lax.dot_general(
        reduced_t, reduced_t, (((0,), (0,)), ((), ())),
        precision=lax.Precision.HIGHEST, preferred_element_type=jnp.float32,
    )
    widened = jnp.concatenate([jnp.ones((1, STEPS), jnp.float32), reduced], axis=0)
    first_table, second_table = pair_tables(modes)
    block_rows = first_table.shape[0] // nl
    start = lax.axis_index("learn") * block_rows
    first_rows = lax.dynamic_slice_in_dim(jnp.asarray(first_table), start, block_rows)
    second_rows = lax.dynamic_slice_in_dim(jnp.asarray(second_table), start, block_rows)
    columns = jnp.arange(modes + 1, dtype=jnp.int32)
    pick_first = (first_rows[:, None] == columns[None, :]).astype(jnp.float32)
    pick_second = (second_rows[:, None] == columns[None, :]).astype(jnp.float32)
    earlier = widened[:, :-1]
    left_part = jnp.dot(
        pick_first, earlier, precision=lax.Precision.HIGHEST, preferred_element_type=jnp.float32
    )
    right_part = jnp.dot(
        pick_second, earlier, precision=lax.Precision.HIGHEST, preferred_element_type=jnp.float32
    )
    features = left_part * right_part
    changes = reduced[:, 1:] - reduced[:, :-1]
    rhs_block = jnp.dot(
        features, changes.T, precision=lax.Precision.HIGHEST, preferred_element_type=jnp.float32
    )
    return (state, reduced, pod_gram, rhs_block)


def solution(mesh):
    in_specs = (P(None, "sim", "learn", None), P(), P(), P(None, None, "sim", "learn", None), P())
    out_specs = (P(None, "sim", "learn", None), P(), P(), P("learn", None))
    return jax.shard_map(body, mesh=mesh, in_specs=in_specs, out_specs=out_specs, check_vma=False)
```

profile of v0, /device:TPU:0, one launch (start us, length us, event | category | flops | bytes accessed | tf_op | source)
XLA Modules:
  0.0 120.1 jit_solution(3831695597574796694)
XLA Ops:
  0.6 0.6 collective-permute-start.1
  1.2 4.0 %collective-permute-start = (f32[8,8,8,128]{3,2,1,0:T(8,128)}, f32[8,8,8,128]{3,2,1,0:T(8,128)S(1)}, u32[]{:S(2)}, u32[]{:S(2)}) collective-permute-start(f32[8,8,8,128]{3,2,1,0:T(8,128)} %param.7), channel_id=1, source_target_pairs={{0,4},{1,5},{2,6},{3,7},{8,12},{9,13},{10,14},{11,15},{16,20},{17,... | collective-permute-start | bytes 786440 | tf_op jit(solution)/shard_map/ppermute | solution.py:320
  5.2 0.4 collective-permute-start.3
  5.6 1.2 %collective-permute-start.2 = (f32[8,8,8,128]{3,2,1,0:T(8,128)}, f32[8,8,8,128]{3,2,1,0:T(8,128)S(1)}, u32[]{:S(2)}, u32[]{:S(2)}) collective-permute-start(f32[8,8,8,128]{3,2,1,0:T(8,128)} %param.7), channel_id=1, source_target_pairs={{0,1},{2,3},{4,5},{6,7},{8,9},{10,11},{12,13},{14,15},{16,17},{18,... | collective-permute-start | bytes 786440 | tf_op jit(solution)/shard_map/ppermute | solution.py:318
  6.8 0.0 collective-permute-done.1
  6.9 9.2 %collective-permute-done = f32[8,8,8,128]{3,2,1,0:T(8,128)S(1)} collective-permute-done((f32[8,8,8,128]{3,2,1,0:T(8,128)}, f32[8,8,8,128]{3,2,1,0:T(8,128)S(1)}, u32[]{:S(2)}, u32[]{:S(2)}) %collective-permute-start) | collective-permute-done | bytes 262176 | tf_op jit(solution)/shard_map/ppermute | solution.py:320
  16.1 0.7 copy-done.3
  16.8 2.2 %pack_corners.2 = (f32[56,8,128]{2,1,0:T(8,128)}, f32[56,8,128]{2,1,0:T(8,128)}) custom-call(f32[512,128]{1,0:T(8,128)} %bitcast.24, f32[512,128]{1,0:T(8,128)} %bitcast.22), custom_call_target="tpu_custom_call" | custom-call | tf_op jit(solution)/shard_map/pack_corners/pallas_call | solution.py:61
  18.9 0.0 collective-permute-start.4
  19.0 1.6 %collective-permute-start.5 = (f32[56,8,128]{2,1,0:T(8,128)}, f32[56,8,128]{2,1,0:T(8,128)S(1)}, u32[]{:S(2)}, u32[]{:S(2)}) collective-permute-start(f32[56,8,128]{2,1,0:T(8,128)} %get-tuple-element.13), channel_id=1, source_target_pairs={{1,2},{5,6},{9,10},{13,14},{17,18},{21,22},{25,26},{29,30},{0,3},{... | collective-permute-start | bytes 688136 | tf_op jit(solution)/shard_map/ppermute | solution.py:324
  20.6 0.0 collective-permute-done.3
  20.6 0.0 collective-permute-done.2
  20.6 0.0 collective-permute-done.4.ca_ref
  20.6 5.8 %collective-permute-done.5.cb_ref = f32[56,8,128]{2,1,0:T(8,128)S(1)} collective-permute-done((f32[56,8,128]{2,1,0:T(8,128)}, f32[56,8,128]{2,1,0:T(8,128)S(1)}, u32[]{:S(2)}, u32[]{:S(2)}) %collective-permute-start.5) | collective-permute-done | bytes 229408 | tf_op jit(solution)/shard_map/ppermute | solution.py:324
  26.4 1.3 %broadcast_in_dim.6.dif_ref = f32[8,128]{1,0:T(8,128)} broadcast(f32[8]{0:T(128)} %param.8), dimensions={0} | broadcast | bytes 4128 | tf_op jit(solution)/shard_map/broadcast_in_dim | solution.py:313
  27.7 1.3 %broadcast_in_dim.7.sto_ref = f32[8,128]{1,0:T(8,128)} broadcast(f32[8]{0:T(128)} %param.9), dimensions={0} | broadcast | bytes 4128 | tf_op jit(solution)/shard_map/broadcast_in_dim | solution.py:314
  29.1 14.4 %advance.2 = (f32[512,128]{1,0:T(8,128)}, f32[64,32,128]{2,1,0:T(8,128)}) custom-call(f32[512,128]{1,0:T(8,128)} %bitcast.26, f32[512,128]{1,0:T(8,128)} %bitcast.25, f32[512,128]{1,0:T(8,128)} %bitcast.23, f32[512,128]{1,0:T(8,128)} %bitcast.34, f32[512,128]{1,0:T(8,128)} %bitcast.33, f32[56,8,128]{2,1,0:T(8,128)} %copy-done.9, f32[56,8,128]{2,1,0:T(8,128)} %copy-done.11, ...), custom_call_target="tpu_custom_call" | custom-call | tf_op jit(solution)/shard_map/advance/pallas_call | solution.py:223
  43.5 0.7 collective-permute-start.7
  44.2 6.5 %collective-permute-start.6 = (f32[8,8,8,128]{3,2,1,0:T(8,128)}, f32[8,8,8,128]{3,2,1,0:T(8,128)S(1)}, u32[]{:S(2)}, u32[]{:S(2)}) collective-permute-start(f32[8,8,8,128]{3,2,1,0:T(8,128)} %bitcast.28), channel_id=1, source_target_pairs={{0,4},{1,5},{2,6},{3,7},{8,12},{9,13},{10,14},{11,15},{16,20},{17,... | collective-permute-start | bytes 786440 | tf_op jit(solution)/shard_map/ppermute | solution.py:320
  50.7 1.1 collective-permute-start.9
  51.7 0.8 collective-permute-start.8
  52.6 0.0 collective-permute-done.7
  52.6 9.9 %collective-permute-done.6 = f32[8,8,8,128]{3,2,1,0:T(8,128)S(1)} collective-permute-done((f32[8,8,8,128]{3,2,1,0:T(8,128)}, f32[8,8,8,128]{3,2,1,0:T(8,128)S(1)}, u32[]{:S(2)}, u32[]{:S(2)}) %collective-permute-start.6) | collective-permute-done | bytes 262176 | tf_op jit(solution)/shard_map/ppermute | solution.py:320
  62.4 0.7 copy-done.1
  63.1 2.2 %pack_corners.3 = (f32[56,8,128]{2,1,0:T(8,128)}, f32[56,8,128]{2,1,0:T(8,128)}) custom-call(f32[512,128]{1,0:T(8,128)} %bitcast.20, f32[512,128]{1,0:T(8,128)} %bitcast.18), custom_call_target="tpu_custom_call" | custom-call | tf_op jit(solution)/shard_map/pack_corners/pallas_call | solution.py:61
  65.3 0.1 collective-permute-start.10
  65.4 1.3 %collective-permute-start.11 = (f32[56,8,128]{2,1,0:T(8,128)}, f32[56,8,128]{2,1,0:T(8,128)S(1)}, u32[]{:S(2)}, u32[]{:S(2)}) collective-permute-start(f32[56,8,128]{2,1,0:T(8,128)} %get-tuple-element.16), channel_id=1, source_target_pairs={{1,2},{5,6},{9,10},{13,14},{17,18},{21,22},{25,26},{29,30},{0,3},{... | collective-permute-start | bytes 688136 | tf_op jit(solution)/shard_map/ppermute | solution.py:324
  66.7 8.0 %project.2 = f32[4,96]{1,0:T(4,128)} custom-call(bf16[96,8,64,128]{3,2,1,0:T(8,128)(2,1)} %bitcast.16, f32[64,32,128]{2,1,0:T(8,128)} %get-tuple-element.18.snap_ref), custom_call_target="tpu_custom_call" | custom-call | tf_op jit(solution)/shard_map/project/pallas_call | solution.py:285
  74.7 0.0 collective-permute-done.9
  74.7 0.0 collective-permute-done.10.ca_ref
  74.7 0.0 collective-permute-done.11.cb_ref
  74.7 0.6 copy-done.4
  75.4 0.1 copy-done.5
  75.5 0.1 copy-done.8
  75.6 0.1 copy-done.10
  75.6 14.4 %advance.3 = (f32[512,128]{1,0:T(8,128)}, f32[64,32,128]{2,1,0:T(8,128)}) custom-call(f32[512,128]{1,0:T(8,128)} %get-tuple-element.14.own_ref, f32[512,128]{1,0:T(8,128)} %bitcast.21, f32[512,128]{1,0:T(8,128)} %bitcast.19, f32[512,128]{1,0:T(8,128)} %bitcast.32, f32[512,128]{1,0:T(8,128)} %bitcast.31, f32[56,8,128]{2,1,0:T(8,128)} %copy-done.8, ...), custom_call_target="tpu_custom_call" | custom-call | tf_op jit(solution)/shard_map/advance/pallas_call | solution.py:223
  90.0 8.0 %project.3 = f32[4,96]{1,0:T(4,128)} custom-call(bf16[96,8,64,128]{3,2,1,0:T(8,128)(2,1)} %bitcast.17, f32[64,32,128]{2,1,0:T(8,128)} %get-tuple-element.19.snap_ref), custom_call_target="tpu_custom_call" | custom-call | tf_op jit(solution)/shard_map/project/pallas_call | solution.py:285
  98.0 0.7 pad_maximum_fusion
  98.7 0.7 broadcast_in_dim.8
  99.3 8.6 %all-to-all-start = ((f32[32,8,96]{2,1,0:T(8,128)}), f32[32,8,96]{2,1,0:T(8,128)S(1)}, u32[]{:S(2)}, u32[]{:S(2)}) async-start(f32[32,8,96]{2,1,0:T(8,128)} %broadcast_in_dim.8), calls=%async_computation | async-start | bytes 262144 | tf_op jit(solution)/shard_map/all_to_all | solution.py:329
  108.0 0.8 dynamic_slice.6
  108.7 0.8 dynamic_slice.7
  109.5 6.6 %all-to-all-done = f32[32,8,96]{2,1,0:T(8,128)S(1)} async-done(((f32[32,8,96]{2,1,0:T(8,128)}), f32[32,8,96]{2,1,0:T(8,128)S(1)}, u32[]{:S(2)}, u32[]{:S(2)}) %all-to-all-start) | async-done | bytes 98336 | tf_op jit(solution)/shard_map/all_to_all | solution.py:329
  116.2 0.0 copy-start.12
  116.2 0.9 convolution_add_fusion
  117.1 0.7 fusion
  117.8 0.7 convolution_multiply_fusion
  118.5 1.6 %fusion.3 = f32[1188,96]{0,1:T(8,128)} fusion(f32[1188,7]{1,0:T(8,128)S(1)} %convolution_multiply_fusion, f32[96,8]{0,1:T(8,128)S(1)} %bitcast.37), kind=kOutput, calls=%fused_computation.8 | convolution fusion | flops 9580704 | bytes 1074688 | tf_op jit(solution)/shard_map/dot_general | solution.py:353
  (25 shorter events, 0.1 us)
Async XLA Ops:
  0.6 6.2 %collective-permute-start.1 = (f32[8,8,8,128]{3,2,1,0:T(8,128)}, f32[8,8,8,128]{3,2,1,0:T(8,128)S(1)}, u32[]{:S(2)}, u32[]{:S(2)}) collective-permute-start(f32[8,8,8,128]{3,2,1,0:T(8,128)} %param.7), channel_id=1, source_target_pairs={{4,8},{5,9},{6,10},{7,11},{12,16},{13,17},{14,18},{15,19},{20,24},... | collective-permute-start | bytes 786440 | tf_op jit(solution)/shard_map/ppermute | solution.py:321
  1.2 14.9 %collective-permute-start = (f32[8,8,8,128]{3,2,1,0:T(8,128)}, f32[8,8,8,128]{3,2,1,0:T(8,128)S(1)}, u32[]{:S(2)}, u32[]{:S(2)}) collective-permute-start(f32[8,8,8,128]{3,2,1,0:T(8,128)} %param.7), channel_id=1, source_target_pairs={{0,4},{1,5},{2,6},{3,7},{8,12},{9,13},{10,14},{11,15},{16,20},{17,... | collective-permute-start | bytes 786440 | tf_op jit(solution)/shard_map/ppermute | solution.py:320
  5.2 15.4 %collective-permute-start.3 = (f32[8,8,8,128]{3,2,1,0:T(8,128)}, f32[8,8,8,128]{3,2,1,0:T(8,128)S(1)}, u32[]{:S(2)}, u32[]{:S(2)}) collective-permute-start(f32[8,8,8,128]{3,2,1,0:T(8,128)} %param.7), channel_id=1, source_target_pairs={{1,2},{5,6},{9,10},{13,14},{17,18},{21,22},{25,26},{29,30},{0,3},{... | collective-permute-start | bytes 786440 | tf_op jit(solution)/shard_map/ppermute | solution.py:319
  5.6 15.0 %collective-permute-start.2 = (f32[8,8,8,128]{3,2,1,0:T(8,128)}, f32[8,8,8,128]{3,2,1,0:T(8,128)S(1)}, u32[]{:S(2)}, u32[]{:S(2)}) collective-permute-start(f32[8,8,8,128]{3,2,1,0:T(8,128)} %param.7), channel_id=1, source_target_pairs={{0,1},{2,3},{4,5},{6,7},{8,9},{10,11},{12,13},{14,15},{16,17},{18,... | collective-permute-start | bytes 786440 | tf_op jit(solution)/shard_map/ppermute | solution.py:318
  6.8 9.2 %copy-start.2 = (f32[8,8,8,128]{3,2,1,0:T(8,128)}, f32[8,8,8,128]{3,2,1,0:T(8,128)S(1)}, u32[]{:S(2)}) copy-start(f32[8,8,8,128]{3,2,1,0:T(8,128)S(1)} %collective-permute-done.1) | copy-start | bytes 786436
  16.1 0.7 copy-start.3
  18.9 1.7 %collective-permute-start.4 = (f32[56,8,128]{2,1,0:T(8,128)}, f32[56,8,128]{2,1,0:T(8,128)S(1)}, u32[]{:S(2)}, u32[]{:S(2)}) collective-permute-start(f32[56,8,128]{2,1,0:T(8,128)} %get-tuple-element.12), channel_id=1, source_target_pairs={{0,1},{2,3},{4,5},{6,7},{8,9},{10,11},{12,13},{14,15},{16,17},{18,... | collective-permute-start | bytes 688136 | tf_op jit(solution)/shard_map/ppermute | solution.py:323
  19.0 7.4 %collective-permute-start.5 = (f32[56,8,128]{2,1,0:T(8,128)}, f32[56,8,128]{2,1,0:T(8,128)S(1)}, u32[]{:S(2)}, u32[]{:S(2)}) collective-permute-start(f32[56,8,128]{2,1,0:T(8,128)} %get-tuple-element.13), channel_id=1, source_target_pairs={{1,2},{5,6},{9,10},{13,14},{17,18},{21,22},{25,26},{29,30},{0,3},{... | collective-permute-start | bytes 688136 | tf_op jit(solution)/shard_map/ppermute | solution.py:324
  20.6 8.5 %copy-start.6 = (f32[8,8,8,128]{3,2,1,0:T(8,128)}, f32[8,8,8,128]{3,2,1,0:T(8,128)S(1)}, u32[]{:S(2)}) copy-start(f32[8,8,8,128]{3,2,1,0:T(8,128)S(1)} %collective-permute-done.3) | copy-start | bytes 786436
  20.6 8.4 %copy-start.7 = (f32[8,8,8,128]{3,2,1,0:T(8,128)}, f32[8,8,8,128]{3,2,1,0:T(8,128)S(1)}, u32[]{:S(2)}) copy-start(f32[8,8,8,128]{3,2,1,0:T(8,128)S(1)} %collective-permute-done.2) | copy-start | bytes 786436
  20.6 8.4 %copy-start.9 = (f32[56,8,128]{2,1,0:T(8,128)}, f32[56,8,128]{2,1,0:T(8,128)S(1)}, u32[]{:S(2)}) copy-start(f32[56,8,128]{2,1,0:T(8,128)S(1)} %collective-permute-done.4.ca_ref) | copy-start | bytes 688132
  26.4 2.6 %copy-start.11 = (f32[56,8,128]{2,1,0:T(8,128)}, f32[56,8,128]{2,1,0:T(8,128)S(1)}, u32[]{:S(2)}) copy-start(f32[56,8,128]{2,1,0:T(8,128)S(1)} %collective-permute-done.5.cb_ref) | copy-start | bytes 688132
  43.5 9.1 %collective-permute-start.7 = (f32[8,8,8,128]{3,2,1,0:T(8,128)}, f32[8,8,8,128]{3,2,1,0:T(8,128)S(1)}, u32[]{:S(2)}, u32[]{:S(2)}) collective-permute-start(f32[8,8,8,128]{3,2,1,0:T(8,128)} %bitcast.27), channel_id=1, source_target_pairs={{4,8},{5,9},{6,10},{7,11},{12,16},{13,17},{14,18},{15,19},{20,24},... | collective-permute-start | bytes 786440 | tf_op jit(solution)/shard_map/ppermute | solution.py:321
  44.2 18.3 %collective-permute-start.6 = (f32[8,8,8,128]{3,2,1,0:T(8,128)}, f32[8,8,8,128]{3,2,1,0:T(8,128)S(1)}, u32[]{:S(2)}, u32[]{:S(2)}) collective-permute-start(f32[8,8,8,128]{3,2,1,0:T(8,128)} %bitcast.28), channel_id=1, source_target_pairs={{0,4},{1,5},{2,6},{3,7},{8,12},{9,13},{10,14},{11,15},{16,20},{17,... | collective-permute-start | bytes 786440 | tf_op jit(solution)/shard_map/ppermute | solution.py:320
  50.7 24.0 %collective-permute-start.9 = (f32[8,8,8,128]{3,2,1,0:T(8,128)}, f32[8,8,8,128]{3,2,1,0:T(8,128)S(1)}, u32[]{:S(2)}, u32[]{:S(2)}) collective-permute-start(f32[8,8,8,128]{3,2,1,0:T(8,128)} %bitcast.29), channel_id=1, source_target_pairs={{1,2},{5,6},{9,10},{13,14},{17,18},{21,22},{25,26},{29,30},{0,3},{... | collective-permute-start | bytes 786440 | tf_op jit(solution)/shard_map/ppermute | solution.py:319
  51.7 22.9 %collective-permute-start.8 = (f32[8,8,8,128]{3,2,1,0:T(8,128)}, f32[8,8,8,128]{3,2,1,0:T(8,128)S(1)}, u32[]{:S(2)}, u32[]{:S(2)}) collective-permute-start(f32[8,8,8,128]{3,2,1,0:T(8,128)} %bitcast.30), channel_id=1, source_target_pairs={{0,1},{2,3},{4,5},{6,7},{8,9},{10,11},{12,13},{14,15},{16,17},{18,... | collective-permute-start | bytes 786440 | tf_op jit(solution)/shard_map/ppermute | solution.py:318
  52.6 9.9 %copy-start = (f32[8,8,8,128]{3,2,1,0:T(8,128)}, f32[8,8,8,128]{3,2,1,0:T(8,128)S(1)}, u32[]{:S(2)}) copy-start(f32[8,8,8,128]{3,2,1,0:T(8,128)S(1)} %collective-permute-done.7) | copy-start | bytes 786436
  62.4 0.7 copy-start.1
  65.3 9.4 %collective-permute-start.10 = (f32[56,8,128]{2,1,0:T(8,128)}, f32[56,8,128]{2,1,0:T(8,128)S(1)}, u32[]{:S(2)}, u32[]{:S(2)}) collective-permute-start(f32[56,8,128]{2,1,0:T(8,128)} %get-tuple-element.15), channel_id=1, source_target_pairs={{0,1},{2,3},{4,5},{6,7},{8,9},{10,11},{12,13},{14,15},{16,17},{18,... | collective-permute-start | bytes 688136 | tf_op jit(solution)/shard_map/ppermute | solution.py:323
  65.4 9.3 %collective-permute-start.11 = (f32[56,8,128]{2,1,0:T(8,128)}, f32[56,8,128]{2,1,0:T(8,128)S(1)}, u32[]{:S(2)}, u32[]{:S(2)}) collective-permute-start(f32[56,8,128]{2,1,0:T(8,128)} %get-tuple-element.16), channel_id=1, source_target_pairs={{1,2},{5,6},{9,10},{13,14},{17,18},{21,22},{25,26},{29,30},{0,3},{... | collective-permute-start | bytes 688136 | tf_op jit(solution)/shard_map/ppermute | solution.py:324
  66.7 49.5 %copy-start.13 = (f32[96,96]{1,0:T(8,128)S(1)}, f32[96,96]{1,0:T(8,128)}, u32[]{:S(2)}) copy-start(f32[96,96]{1,0:T(8,128)} %param.11) | copy-start | bytes 110596
  74.7 23.3 %copy-start.14 = (f32[4,96]{1,0:T(4,128)S(1)}, f32[4,96]{1,0:T(4,128)}, u32[]{:S(2)}) copy-start(f32[4,96]{1,0:T(4,128)} %project.2) | copy-start | bytes 4612
  74.7 0.7 copy-start.4
  74.7 0.8 copy-start.5
  74.7 0.9 copy-start.8
  74.7 0.9 copy-start.10
  99.3 16.8 %all-to-all-start = ((f32[32,8,96]{2,1,0:T(8,128)}), f32[32,8,96]{2,1,0:T(8,128)S(1)}, u32[]{:S(2)}, u32[]{:S(2)}) async-start(f32[32,8,96]{2,1,0:T(8,128)} %broadcast_in_dim.8), calls=%async_computation | async-start | bytes 262144 | tf_op jit(solution)/shard_map/all_to_all | solution.py:329
  116.2 3.9 %copy-start.12 = (f32[8,96]{1,0:T(8,128)}, f32[8,96]{1,0:T(8,128)S(1)}, u32[]{:S(2)}) copy-start(f32[8,96]{1,0:T(8,128)S(1)} %reduce_sum.9) | copy-start | bytes 9220
where the time goes:
time: 120 us
  Pallas kernels  49.1 us (41%)
  waiting for transfers between devices  31.5 us (26%)
  starting transfers between devices  26.9 us (22%)
  local copies, waits for them, and re-layouts  7.2 us (6%)
  matrix products  3.83 us (3%)
    pallas_call x2, Pallas kernels, advance(): pl.pallas_call(functools.partial(round_kernel, cx, cy, steps), out_shape=...  28.8 us
    ppermute x2, waiting for transfers between devices, body(): xa = lax.ppermute(state, BOTH, x_even)  19.1 us
    pallas_call x2, Pallas kernels, project(): pl.pallas_call(functools.partial(project_kernel, cy, steps), out_shape=ja...  15.9 us
    ppermute x2, starting transfers between devices, body(): xa = lax.ppermute(state, BOTH, x_even)  10.5 us
    all_to_all x1, starting transfers between devices, body(): reduced_t = jnp.sum(lax.all_to_all(sent, BOTH, 0, 0), axis=0)  8.62 us
    all_to_all x1, waiting for transfers between devices, body(): reduced_t = jnp.sum(lax.all_to_all(sent, BOTH, 0, 0), axis=0)  6.63 us
    ppermute x2, waiting for transfers between devices, body(): cb = lax.ppermute(to_b, BOTH, y_odd)  5.76 us
    pallas_call x2, Pallas kernels, pack_corners(): pl.pallas_call(functools.partial(pack_kernel, cx, cy), out_shape=(shape,...  4.34 us
  transfers between devices with their start and end apart: 13, of which 4 were waited for; matrix products, arithmetic and copies ran while one was open for 1% of the time, Pallas kernels for 10%

commit v1 on v0

v1 whole, which is shorter than its diff:
```python
import functools

import jax
import jax.numpy as jnp
import numpy as np
from jax import lax
from jax.experimental import pallas as pl
from jax.experimental.pallas import tpu as pltpu
from jax.sharding import PartitionSpec as P

STEPS = 8

time_step = 0.1
drift_x = 1.2
drift_y = 1.0
drift_z = 0.3
arrhenius = 2.0
activation = 1.0

BOTH = ("sim", "learn")
VMEM = pl.BlockSpec(memory_space=pltpu.VMEM)
WIDE = 56 * 1024 * 1024


def both_ways(pairs):
    return [(a, b) for a, b in pairs] + [(b, a) for a, b in pairs]


def swaps(ns, nl):
    x_even = both_ways([(s * nl + l, (s + 1) * nl + l) for s in range(0, ns, 2) for l in range(nl)])
    x_odd = [(s * nl + l, (s + 1) * nl + l) for s in range(1, ns - 1, 2) for l in range(nl)]
    x_odd += [(s * nl + l, s * nl + l + 1) for s in (0, ns - 1) for l in range(0, nl, 2)]
    y_even = both_ways([(s * nl + l, s * nl + l + 1) for s in range(ns) for l in range(0, nl, 2)])
    y_odd = [(s * nl + l, s * nl + l + 1) for s in range(ns) for l in range(1, nl - 1, 2)]
    y_far = y_odd + [(s * nl + l, (s + 1) * nl + l) for s in range(0, ns, 2) for l in (0, nl - 1)]
    y_odd = y_odd + [(s * nl, s * nl + nl - 1) for s in range(ns)]
    return x_even, both_ways(x_odd), y_even, both_ways(y_odd), both_ways(y_far)


def in_vmem(*arrays):
    return [pltpu.with_memory_space_constraint(a, pltpu.VMEM) for a in arrays]


def corner_runs(reach):
    runs, first = [], 0
    for d in range(1, reach):
        runs.append((d, reach - d, first))
        first += reach - d
    return runs, first


def each_case(first, second, body):
    for a in (True, False):
        for b in (True, False):

            @pl.when(jnp.logical_and(first == a, second == b))
            def _(a=a, b=b):
                body(a, b)


def columns_kernel(cx, cy, native_ref, out_ref):
    nf = native_ref.shape[0] // (cx * cy)
    for c in range(cx * cy):
        out_ref[pl.ds(c * nf, nf), :] = native_ref[pl.ds(c, nf, stride=cx * cy), :]


def to_columns(fields):
    nf, cx, cy, nz = fields.shape
    return pl.pallas_call(
        functools.partial(columns_kernel, cx, cy),
        out_shape=pltpu.VMEM((cx * cy * nf, nz), jnp.float32),
        in_specs=[VMEM],
        out_specs=VMEM,
        name="to_columns",
    )(fields.reshape(nf * cx * cy, nz))


def pack_kernel(cx, cy, nf, xa_ref, xb_ref, to_a_ref, to_b_ref):
    runs, size = corner_runs(min(cx, cy))
    even_s = lax.rem(lax.axis_index("sim"), 2) == 0
    even_l = lax.rem(lax.axis_index("learn"), 2) == 0

    def copy(s_is_even, l_is_even):
        for side, brick in enumerate((xa_ref, xb_ref)):
            is_east = s_is_even == (side == 0)
            for out_ref, north in ((to_a_ref, l_is_even), (to_b_ref, not l_is_even)):
                for d, count, first in runs:
                    x = d - 1 if is_east else cx - d
                    y = cy - count if north else 0
                    rows = brick[pl.ds((x * cy + y) * nf, count * nf), :]
                    out_ref[pl.ds((side * size + first) * nf, count * nf), :] = rows

    each_case(even_s, even_l, copy)


def pack_corners(xa, xb, cx, cy, nf):
    nz = xa.shape[1]
    size = 2 * corner_runs(min(cx, cy))[1]
    shape = pltpu.VMEM((size * nf, nz), jnp.float32)
    return pl.pallas_call(
        functools.partial(pack_kernel, cx, cy, nf),
        out_shape=(shape, shape),
        in_specs=[VMEM, VMEM],
        out_specs=(VMEM, VMEM),
        name="pack_corners",
    )(*in_vmem(xa, xb))


def round_kernel(
    cx, cy, nf, steps, last, own_ref, xa_ref, xb_ref, ya_ref, yb_ref, ca_ref, cb_ref, dif_ref, sto_ref,
    state_ref, snap_ref, u_ref, m_ref, rate_ref,
):
    nz = own_ref.shape[1]
    reach = 2 * steps
    wide_x, wide_y = cx + 2 * reach, cy + 2 * reach
    s, l = lax.axis_index("sim"), lax.axis_index("learn")
    ns, nl = lax.axis_size("sim"), lax.axis_size("learn")
    even_s, even_l = lax.rem(s, 2) == 0, lax.rem(l, 2) == 0
    has_west, has_east = s > 0, s < ns - 1
    has_south, has_north = l > 0, l < nl - 1

    def place(ref, x0, y0):
        for i in range(cx):
            u_ref[pl.ds(((x0 + i) * wide_y + y0) * nf, cy * nf), :] = ref[pl.ds(i * cy * nf, cy * nf), :]

    def clear(x0, x1, y0, y1):
        zeros = jnp.zeros(((y1 - y0) * nf, nz), jnp.float32)

        def trip(x, carry):
            for ref in (u_ref, m_ref):
                ref[pl.ds(pl.multiple_of((x * wide_y + y0) * nf, nf), (y1 - y0) * nf), :] = zeros
            return carry

        lax.fori_loop(x0, x1, trip, 0)

    place(own_ref, reach, reach)
    runs, size = corner_runs(reach)

    def receive(s_is_even, l_is_even):
        for side, brick in enumerate((xa_ref, xb_ref)):
            is_east = s_is_even == (side == 0)

            @pl.when(has_east if is_east else has_west)
            def _(brick=brick, is_east=is_east):
                place(brick, reach + cx if is_east else 0, reach)

        for corner, brick, north in ((ca_ref, ya_ref, l_is_even), (cb_ref, yb_ref, not l_is_even)):

            @pl.when(has_north if north else has_south)
            def _(corner=corner, brick=brick, north=north):
                place(brick, reach, reach + cy if north else 0)
                for side in range(2):
                    is_east = s_is_even == (side == 0)
                    for d, count, first in runs:
                        x = reach + cx + d - 1 if is_east else reach - d
                        y = reach + cy if north else reach - count
                        rows = corner[pl.ds((side * size + first) * nf, count * nf), :]
                        u_ref[pl.ds((x * wide_y + y) * nf, count * nf), :] = rows

    each_case(even_s, even_l, receive)
    pl.when(jnp.logical_not(has_west))(lambda: clear(0, reach, 0, wide_y))
    pl.when(jnp.logical_not(has_east))(lambda: clear(reach + cx, wide_x, 0, wide_y))
    pl.when(jnp.logical_not(has_south))(lambda: clear(0, wide_x, 0, reach))
    pl.when(jnp.logical_not(has_north))(lambda: clear(0, wide_x, reach + cy, wide_y))

    field = lax.broadcasted_iota(jnp.int32, (nf, nz), 0)
    lane = lax.broadcasted_iota(jnp.int32, (nf, nz), 1)
    diffusivity, stoich = jnp.zeros((nf, nz), jnp.float32), jnp.zeros((nf, nz), jnp.float32)
    for f in range(nf):
        diffusivity = jnp.where(field == f, dif_ref[f], diffusivity)
        stoich = jnp.where(field == f, sto_ref[f], stoich)

    def coefficients(dt):
        return (
            1.0 * (dt / time_step) - 6.0 * dt * diffusivity,
            dt * (diffusivity - 0.5 * drift_x),
            dt * (diffusivity + 0.5 * drift_x),
            dt * (diffusivity - 0.5 * drift_y),
            dt * (diffusivity + 0.5 * drift_y),
            jnp.where(lane < nz - 1, dt * (diffusivity - 0.5 * drift_z), 0.0),
            jnp.where(lane > 0, dt * (diffusivity + 0.5 * drift_z), 0.0),
            dt * arrhenius * stoich,
        )

    in_south = jnp.where(has_south, 1.0, 0.0)
    in_north = jnp.where(has_north, 1.0, 0.0)

    def rows_block(src, dst, old, coefs, rows):
        cc, ce, cw, cn, cs, cu, cl, ck = coefs

        def load(x, y):
            return src[pl.ds((x * wide_y + y) * nf, nf), :]

        for k, (x, beyond) in enumerate(rows):
            y_first, width = reach - beyond, cy + 2 * beyond
            for p in range(0, width, nf):
                base = (x * wide_y + y_first + p) * nf
                u0 = src[pl.ds(base, nf, stride=nf), :]
                u1 = src[pl.ds(base + 1, nf, stride=nf), :]
                u7 = src[pl.ds(base + 7, nf, stride=nf), :]
                rate = jnp.tanh(u0) * jnp.tanh(u1) * jnp.exp(-activation / (1.0 + u7 * u7))
                rate_ref[pl.ds(k * (wide_y + nf) + p, nf), :] = rate
        for k, (x, beyond) in enumerate(rows):
            y_first, width = reach - beyond, cy + 2 * beyond
            south, centre = load(x, y_first - 1), load(x, y_first)
            for j in range(width):
                y = y_first + j
                north = load(x, y + 1)
                value = cc * centre + cn * north + cs * south
                value += ce * load(x + 1, y) + cw * load(x - 1, y)
                value += cu * pltpu.roll(centre, nz - 1, 1) + cl * pltpu.roll(centre, 1, 1)
                value += ck * rate_ref[pl.ds(k * (wide_y + nf) + j, nf, stride=0), :]
                if old is not None:
                    value += 0.5 * old[pl.ds((x * wide_y + y) * nf, nf), :]
                if y < reach:
                    value *= in_south
                if y >= reach + cy:
                    value *= in_north
                dst[pl.ds((x * wide_y + y) * nf, nf), :] = value
                south, centre = centre, north

    def stage(src, dst, old, r, coefs):
        group = 4

        def trip(i, carry):
            x0 = reach + i * group
            rows_block(src, dst, old, coefs, [(x0 + k, r) for k in range(group)])
            return carry

        lax.fori_loop(0, cx // group, trip, 0)
        if r:

            @pl.when(has_west)
            def _():
                rows_block(src, dst, old, coefs, [(reach - d, r - d) for d in range(1, r + 1)])

            @pl.when(has_east)
            def _():
                rows_block(src, dst, old, coefs, [(reach + cx - 1 + d, r - d) for d in range(1, r + 1)])

    whole, half = coefficients(time_step), coefficients(0.5 * time_step)
    for t in range(steps):
        r = reach - 1 - 2 * t
        stage(u_ref, m_ref, None, r, whole)
        stage(m_ref, u_ref, u_ref, r - 1, half)
        for x in range(cx):
            for f in range(nf):
                value = u_ref[pl.ds(((reach + x) * wide_y + reach) * nf + f, cy, stride=nf), :]
                snap_ref[f * cx + x, pl.ds(t * cy, cy), :] = value
                if last and t == steps - 1:
                    state_ref[pl.ds((f * cx + x) * cy, cy), :] = value
    if not last:
        for i in range(cx):
            rows = u_ref[pl.ds(((reach + i) * wide_y + reach) * nf, cy * nf), :]
            state_ref[pl.ds(i * cy * nf, cy * nf), :] = rows


def advance(bricks, corners, dif, sto, cx, cy, nf, steps, last):
    nz = bricks[0].shape[1]
    wide = (cx + 4 * steps) * (cy + 4 * steps)
    rows = max(cx, 2 * steps) * (cy + 4 * steps + nf)
    shape = (nf * cx * cy, nz)
    scalars = pl.BlockSpec(memory_space=pltpu.SMEM)
    return pl.pallas_call(
        functools.partial(round_kernel, cx, cy, nf, steps, last),
        out_shape=(
            jax.ShapeDtypeStruct(shape, jnp.float32) if last else pltpu.VMEM(shape, jnp.float32),
            pltpu.VMEM((nf * cx, steps * cy, nz), jnp.float32),
        ),
        in_specs=[VMEM] * 7 + [scalars] * 2,
        out_specs=(VMEM, VMEM),
        scratch_shapes=[
            pltpu.VMEM((wide * nf, nz), jnp.float32),
            pltpu.VMEM((wide * nf, nz), jnp.float32),
            pltpu.VMEM((rows, nz), jnp.float32),
        ],
        name="advance",
    )(*in_vmem(*bricks, *corners), dif, sto)


def project_kernel(cy, steps, basis_ref, snap_ref, out_ref, acc_ref):
    modes, pair, cells, nz = basis_ref.shape
    cx = cells // cy
    step = pl.program_id(0)

    @pl.when(step == 0)
    def _():
        acc_ref[...] = jnp.zeros_like(acc_ref)

    total = None
    for p in range(cx // 2):
        left = [basis_ref[:, f, pl.ds(p * 2 * cy, 2 * cy), :].reshape(modes * 2 * cy, nz) for f in range(pair)]
        right = [
            snap_ref[pl.ds(f * cx + 2 * p, 2)].reshape(2 * steps * cy, nz).astype(jnp.bfloat16) for f in range(pair)
        ]
        term = lax.dot_general(
            jnp.concatenate(left, axis=1),
            jnp.concatenate(right, axis=1),
            (((1,), (1,)), ((), ())),
            preferred_element_type=jnp.float32,
        )
        total = term if total is None else total + term
    acc_ref[...] += total

    @pl.when(step == pl.num_programs(0) - 1)
    def _():
        columns = 2 * steps * cy
        row = lax.broadcasted_iota(jnp.int32, (2 * cy, columns), 0)
        column = lax.broadcasted_iota(jnp.int32, (2 * cy, columns), 1)
        same = (row // cy == column // (steps * cy)) & (row % cy == column % cy)
        kept = acc_ref[...].reshape(modes, 2 * cy, columns) * same.astype(jnp.float32)[None]
        kept = jnp.sum(kept, axis=1)
        which = lax.broadcasted_iota(jnp.int32, (steps, columns), 0)
        column = lax.broadcasted_iota(jnp.int32, (steps, columns), 1)
        gather = (column // cy % steps == which).astype(jnp.float32)
        out_ref[...] = lax.dot_general(
            gather, kept, (((1,), (1,)), ((), ())),
            precision=lax.Precision.HIGHEST, preferred_element_type=jnp.float32,
        )


def project(basis, snaps, steps):
    modes, nf, cx, cy, nz = basis.shape
    pair = 2
    return pl.pallas_call(
        functools.partial(project_kernel, cy, steps),
        out_shape=jax.ShapeDtypeStruct((steps, modes), jnp.float32),
        grid=(nf // pair,),
        in_specs=[
            pl.BlockSpec((modes, pair, cx * cy, nz), lambda i: (0, i, 0, 0)),
            pl.BlockSpec((pair * cx, steps * cy, nz), lambda i: (i, 0, 0)),
        ],
        out_specs=pl.BlockSpec((steps, modes), lambda i: (0, 0)),
        scratch_shapes=[pltpu.VMEM((modes * 2 * cy, 2 * steps * cy), jnp.float32)],
        compiler_params=pltpu.CompilerParams(vmem_limit_bytes=WIDE),
        name="project",
    )(basis.reshape(modes, nf, cx * cy, nz), *in_vmem(snaps))


def pair_tables(modes):
    upper_pairs = np.triu_indices(modes)
    first_table = np.concatenate([np.zeros(modes), upper_pairs[0] + 1]).astype(np.int32)
    second_table = np.concatenate([np.arange(modes) + 1, upper_pairs[1] + 1]).astype(np.int32)
    return (first_table, second_table)


def body(fields, diffusivity, stoich, basis, gram_old):
    modes = basis.shape[0]
    nf, cx, cy, nz = fields.shape
    ns, nl = lax.axis_size("sim"), lax.axis_size("learn")
    steps = min(cx, cy) // 2
    x_even, x_odd, y_even, y_odd, y_far = swaps(ns, nl)
    state = to_columns(fields)
    rounds = STEPS // steps
    parts = []
    for n in range(rounds):
        ya = lax.ppermute(state, BOTH, y_even)
        yb = lax.ppermute(state, BOTH, y_odd)
        xa = lax.ppermute(state, BOTH, x_even)
        xb = lax.ppermute(state, BOTH, x_odd)
        to_a, to_b = pack_corners(xa, xb, cx, cy, nf)
        ca = lax.ppermute(to_a, BOTH, y_even)
        cb = lax.ppermute(to_b, BOTH, y_far)
        bricks = (state, xa, xb, ya, yb)
        state, snaps = advance(bricks, (ca, cb), diffusivity, stoich, cx, cy, nf, steps, n == rounds - 1)
        parts.append(project(basis, snaps, steps))
    state = state.reshape(fields.shape)
    local = jnp.concatenate(parts, axis=0)
    sent = jnp.broadcast_to(local[None], (ns * nl, *local.shape))
    reduced_t = jnp.sum(lax.all_to_all(sent, BOTH, 0, 0), axis=0)
    reduced = reduced_t.T
    pod_gram = gram_old + lax.dot_general(
        reduced_t, reduced_t, (((0,), (0,)), ((), ())),
        precision=lax.Precision.HIGHEST, preferred_element_type=jnp.float32,
    )
    widened = jnp.concatenate([jnp.ones((1, STEPS), jnp.float32), reduced], axis=0)
    first_table, second_table = pair_tables(modes)
    block_rows = first_table.shape[0] // nl
    start = lax.axis_index("learn") * block_rows
    first_rows = lax.dynamic_slice_in_dim(jnp.asarray(first_table), start, block_rows)
    second_rows = lax.dynamic_slice_in_dim(jnp.asarray(second_table), start, block_rows)
    columns = jnp.arange(modes + 1, dtype=jnp.int32)
    pick_first = (first_rows[:, None] == columns[None, :]).astype(jnp.float32)
    pick_second = (second_rows[:, None] == columns[None, :]).astype(jnp.float32)
    earlier = widened[:, :-1]
    left_part = jnp.dot(
        pick_first, earlier, precision=lax.Precision.HIGHEST, preferred_element_type=jnp.float32
    )
    right_part = jnp.dot(
        pick_second, earlier, precision=lax.Precision.HIGHEST, preferred_element_type=jnp.float32
    )
    features = left_part * right_part
    changes = reduced[:, 1:] - reduced[:, :-1]
    rhs_block = jnp.dot(
        features, changes.T, precision=lax.Precision.HIGHEST, preferred_element_type=jnp.float32
    )
    return (state, reduced, pod_gram, rhs_block)


def solution(mesh):
    in_specs = (P(None, "sim", "learn", None), P(), P(), P(None, None, "sim", "learn", None), P())
    out_specs = (P(None, "sim", "learn", None), P(), P(), P("learn", None))
    return jax.shard_map(body, mesh=mesh, in_specs=in_specs, out_specs=out_specs, check_vma=False)
```

time: 120 us -> 97.3 us (0.81)
  Pallas kernels: 49.1 us -> 29.6 us
  local copies, waits for them, and re-layouts: 7.2 us -> 12.4 us
  starting transfers between devices: 26.9 us -> 22.2 us
  waiting for transfers between devices: 31.5 us -> 27.2 us
    pallas_call x4 -> x5, Pallas kernels: 33.1 us -> 13.8 us  [the longest x2 12.6 us: advance(): pl.pallas_call(functools.partial(round_kernel, cx, cy, nf, steps, last),...]
    unnamed x30 -> x34, local copies, waits for them, and re-layouts: 2.33 us -> 10.2 us
    ppermute x2, waiting for transfers between devices: 5.76 us -> 1.88 us  [body(): cb = lax.ppermute(to_b, BOTH, y_far)]
    all_to_all x1, starting transfers between devices: 8.62 us -> 5.04 us  [body(): reduced_t = jnp.sum(lax.all_to_all(sent, BOTH, 0, 0), axis=0)]
    broadcast_in_dim x2 -> x0, local copies, waits for them, and re-layouts: 2.63 us -> none  [the longest x1 1.32 us: body(): dif = jnp.broadcast_to(diffusivity[:, None], (nf, nz))]
    ppermute x2, starting transfers between devices: 2.91 us -> 5.07 us  [body(): cb = lax.ppermute(to_b, BOTH, y_far)]
    ppermute x2, starting transfers between devices: 10.5 us -> 8.73 us  [body(): xa = lax.ppermute(state, BOTH, x_even)]
  transfers between devices with their start and end apart: 13 -> 13, of which waited for: 4 -> 4; matrix products, arithmetic and copies ran while one was open for 1% -> 2% of each run, Pallas kernels for 10% -> 8%
where the time goes in v1:
time: 97.3 us; the launch traced here: 96.7 us
  Pallas kernels  29.6 us (30%)
  waiting for transfers between devices  27.2 us (28%)
  starting transfers between devices  22.2 us (23%)
  local copies, waits for them, and re-layouts  12.4 us (13%)
  matrix products  3.83 us (4%)
    ppermute x2, waiting for transfers between devices, body(): xa = lax.ppermute(state, BOTH, x_even)  18.6 us
    pallas_call x2, Pallas kernels, project(): pl.pallas_call(functools.partial(project_kernel, cy, steps), out_shape=ja...  15.9 us
    pallas_call x2, Pallas kernels, advance(): pl.pallas_call(functools.partial(round_kernel, cx, cy, nf, steps, last),...  12.6 us
    unnamed x34, local copies, waits for them, and re-layouts  10.2 us
    ppermute x2, starting transfers between devices, body(): xa = lax.ppermute(state, BOTH, x_even)  8.73 us
    all_to_all x1, waiting for transfers between devices, body(): reduced_t = jnp.sum(lax.all_to_all(sent, BOTH, 0, 0), axis=0)  6.63 us
    ppermute x2, starting transfers between devices, body(): cb = lax.ppermute(to_b, BOTH, y_far)  5.07 us
    all_to_all x1, starting transfers between devices, body(): reduced_t = jnp.sum(lax.all_to_all(sent, BOTH, 0, 0), axis=0)  5.04 us
  transfers between devices with their start and end apart: 13, of which 4 were waited for; matrix products, arithmetic and copies ran while one was open for 2% of the time, Pallas kernels for 8%

profile of v1, /device:TPU:0, one launch (start us, length us, event | category | flops | bytes accessed | tf_op | source)
XLA Modules:
  0.0 96.7 jit_solution(8821091756730974657)
XLA Ops:
  0.6 1.1 %to_columns.1.own_ref = f32[512,128]{1,0:T(8,128)S(1)} custom-call(f32[512,128]{1,0:T(8,128)} %bitcast.9), custom_call_target="tpu_custom_call" | custom-call | tf_op jit(solution)/shard_map/to_columns/pallas_call | solution.py:69
  1.7 0.6 collective-permute-start.1
  2.3 4.0 %collective-permute-start = (f32[512,128]{1,0:T(8,128)S(1)}, f32[512,128]{1,0:T(8,128)S(1)}, u32[]{:S(2)}, u32[]{:S(2)}) collective-permute-start(f32[512,128]{1,0:T(8,128)S(1)} %to_columns.1.own_ref), channel_id=1, source_target_pairs={{0,4},{1,5},{2,6},{3,7},{8,12},{9,13},{10,14},{11,15},{16,20},{17,... | collective-permute-start | bytes 786440 | tf_op jit(solution)/shard_map/ppermute | solution.py:359
  6.3 0.4 collective-permute-start.3
  6.7 1.2 %collective-permute-start.2 = (f32[512,128]{1,0:T(8,128)S(1)}, f32[512,128]{1,0:T(8,128)S(1)}, u32[]{:S(2)}, u32[]{:S(2)}) collective-permute-start(f32[512,128]{1,0:T(8,128)S(1)} %to_columns.1.own_ref), channel_id=1, source_target_pairs={{0,1},{2,3},{4,5},{6,7},{8,9},{10,11},{12,13},{14,15},{16,17},{18,... | collective-permute-start | bytes 786440 | tf_op jit(solution)/shard_map/ppermute | solution.py:357
  8.0 0.0 collective-permute-done.1.xb_ref
  8.0 8.9 %collective-permute-done.xa_ref = f32[512,128]{1,0:T(8,128)S(1)} collective-permute-done((f32[512,128]{1,0:T(8,128)S(1)}, f32[512,128]{1,0:T(8,128)S(1)}, u32[]{:S(2)}, u32[]{:S(2)}) %collective-permute-start) | collective-permute-done | bytes 262176 | tf_op jit(solution)/shard_map/ppermute | solution.py:359
  16.9 0.1 collective-permute-start.4
  17.0 2.5 %collective-permute-start.5 = (f32[448,128]{1,0:T(8,128)S(1)}, f32[448,128]{1,0:T(8,128)S(1)}, u32[]{:S(2)}, u32[]{:S(2)}) collective-permute-start(f32[448,128]{1,0:T(8,128)S(1)} %get-tuple-element.13), channel_id=1, source_target_pairs={{1,2},{5,6},{9,10},{13,14},{17,18},{21,22},{25,26},{29,30},{0,4},{... | collective-permute-start | bytes 688136 | tf_op jit(solution)/shard_map/ppermute | solution.py:363
  19.5 0.7 copy-done.6
  20.2 0.0 collective-permute-done.2.ya_ref
  20.2 0.7 copy-done.8
  20.9 0.0 collective-permute-done.4.ca_ref
  20.9 0.7 copy-done.10
  21.6 1.9 %collective-permute-done.5.cb_ref = f32[448,128]{1,0:T(8,128)S(1)} collective-permute-done((f32[448,128]{1,0:T(8,128)S(1)}, f32[448,128]{1,0:T(8,128)S(1)}, u32[]{:S(2)}, u32[]{:S(2)}) %collective-permute-start.5) | collective-permute-done | bytes 229408 | tf_op jit(solution)/shard_map/ppermute | solution.py:363
  23.5 0.7 copy-done.12
  24.2 0.9 copy-done.1
  25.2 0.9 copy-done.7
  26.1 0.9 copy-done.9
  27.1 0.9 copy-done.11
  28.0 0.9 copy-done.13
  29.0 5.8 %advance.2 = (f32[512,128]{1,0:T(8,128)S(1)}, f32[64,32,128]{2,1,0:T(8,128)S(1)}) custom-call(f32[512,128]{1,0:T(8,128)S(1)} %to_columns.1.own_ref, f32[512,128]{1,0:T(8,128)S(1)} %collective-permute-done.xa_ref, f32[512,128]{1,0:T(8,128)S(1)} %copy-done.1, f32[512,128]{1,0:T(8,128)S(1)} %copy-done.9, f32[512,128]{1,0:T(8,128)S(1)} %copy-done.7, ...), custom_call_target="tpu_custom_call" | custom-call | tf_op jit(solution)/shard_map/advance/pallas_call | solution.py:264
  34.7 0.0 copy-start.2
  34.8 0.1 collective-permute-start.7
  34.8 4.7 %collective-permute-start.6 = (f32[512,128]{1,0:T(8,128)S(1)}, f32[512,128]{1,0:T(8,128)S(1)}, u32[]{:S(2)}, u32[]{:S(2)}) collective-permute-start(f32[512,128]{1,0:T(8,128)S(1)} %get-tuple-element.14.own_ref), channel_id=1, source_target_pairs={{0,4},{1,5},{2,6},{3,7},{8,12},{9,13},{10,14},{11,15},{16,20},{17,... | collective-permute-start | bytes 786440 | tf_op jit(solution)/shard_map/ppermute | solution.py:359
  39.5 0.1 collective-permute-start.9
  39.6 0.8 collective-permute-start.8
  40.5 9.7 %collective-permute-done.6.xa_ref = f32[512,128]{1,0:T(8,128)S(1)} collective-permute-done((f32[512,128]{1,0:T(8,128)S(1)}, f32[512,128]{1,0:T(8,128)S(1)}, u32[]{:S(2)}, u32[]{:S(2)}) %collective-permute-start.6) | collective-permute-done | bytes 262176 | tf_op jit(solution)/shard_map/ppermute | solution.py:359
  50.3 0.1 collective-permute-start.10
  50.4 2.5 %collective-permute-start.11 = (f32[448,128]{1,0:T(8,128)S(1)}, f32[448,128]{1,0:T(8,128)S(1)}, u32[]{:S(2)}, u32[]{:S(2)}) collective-permute-start(f32[448,128]{1,0:T(8,128)S(1)} %get-tuple-element.16), channel_id=1, source_target_pairs={{1,2},{5,6},{9,10},{13,14},{17,18},{21,22},{25,26},{29,30},{0,4},{... | collective-permute-start | bytes 688136 | tf_op jit(solution)/shard_map/ppermute | solution.py:363
  52.9 7.9 %project.2 = f32[4,96]{1,0:T(4,128)} custom-call(bf16[96,8,64,128]{3,2,1,0:T(8,128)(2,1)} %bitcast.7, f32[64,32,128]{2,1,0:T(8,128)S(1)} %get-tuple-element.18.snap_ref), custom_call_target="tpu_custom_call" | custom-call | tf_op jit(solution)/shard_map/project/pallas_call | solution.py:325
  60.9 0.7 copy-done.4
  61.6 0.0 copy-start.3
  61.6 0.9 copy-done.3
  62.5 0.9 copy-done.5
  63.5 6.8 %advance.3 = (f32[512,128]{1,0:T(8,128)}, f32[64,32,128]{2,1,0:T(8,128)S(1)}) custom-call(f32[512,128]{1,0:T(8,128)S(1)} %copy-done.3, f32[512,128]{1,0:T(8,128)S(1)} %collective-permute-done.6.xa_ref, f32[512,128]{1,0:T(8,128)S(1)} %collective-permute-done.7.xb_ref, f32[512,128]{1,0:T(8,128)S(1)} %collective-permute-done.8.ya_ref, ...), custom_call_target="tpu_custom_call" | custom-call | tf_op jit(solution)/shard_map/advance/pallas_call | solution.py:264
  70.3 7.9 %project.3 = f32[4,96]{1,0:T(4,128)} custom-call(bf16[96,8,64,128]{3,2,1,0:T(8,128)(2,1)} %bitcast.8, f32[64,32,128]{2,1,0:T(8,128)S(1)} %get-tuple-element.19.snap_ref), custom_call_target="tpu_custom_call" | custom-call | tf_op jit(solution)/shard_map/project/pallas_call | solution.py:325
  78.2 0.7 pad_maximum_fusion
  78.9 0.7 broadcast_in_dim.2
  79.6 5.0 %all-to-all-start = ((f32[32,8,96]{2,1,0:T(8,128)}), f32[32,8,96]{2,1,0:T(8,128)S(1)}, u32[]{:S(2)}, u32[]{:S(2)}) async-start(f32[32,8,96]{2,1,0:T(8,128)} %broadcast_in_dim.2), calls=%async_computation | async-start | bytes 262144 | tf_op jit(solution)/shard_map/all_to_all | solution.py:370
  84.6 0.8 dynamic_slice.6
  85.4 0.8 dynamic_slice.7
  86.2 6.6 %all-to-all-done = f32[32,8,96]{2,1,0:T(8,128)S(1)} async-done(((f32[32,8,96]{2,1,0:T(8,128)}), f32[32,8,96]{2,1,0:T(8,128)S(1)}, u32[]{:S(2)}, u32[]{:S(2)}) %all-to-all-start) | async-done | bytes 98336 | tf_op jit(solution)/shard_map/all_to_all | solution.py:370
  92.8 0.0 copy-start.14
  92.9 0.9 convolution_add_fusion
  93.7 0.7 fusion
  94.4 0.7 convolution_multiply_fusion
  95.1 1.6 %fusion.3 = f32[1188,96]{0,1:T(8,128)} fusion(f32[1188,7]{1,0:T(8,128)S(1)} %convolution_multiply_fusion, f32[96,8]{0,1:T(8,128)S(1)} %bitcast.12), kind=kOutput, calls=%fused_computation.8 | convolution fusion | flops 9580704 | bytes 1074688 | tf_op jit(solution)/shard_map/dot_general | solution.py:394
  (28 shorter events, 0.2 us)
Async XLA Ops:
  1.7 6.2 %collective-permute-start.1 = (f32[512,128]{1,0:T(8,128)S(1)}, f32[512,128]{1,0:T(8,128)S(1)}, u32[]{:S(2)}, u32[]{:S(2)}) collective-permute-start(f32[512,128]{1,0:T(8,128)S(1)} %to_columns.1.own_ref), channel_id=1, source_target_pairs={{4,8},{5,9},{6,10},{7,11},{12,16},{13,17},{14,18},{15,19},{20,24},... | collective-permute-start | bytes 786440 | tf_op jit(solution)/shard_map/ppermute | solution.py:360
  2.3 14.6 %collective-permute-start = (f32[512,128]{1,0:T(8,128)S(1)}, f32[512,128]{1,0:T(8,128)S(1)}, u32[]{:S(2)}, u32[]{:S(2)}) collective-permute-start(f32[512,128]{1,0:T(8,128)S(1)} %to_columns.1.own_ref), channel_id=1, source_target_pairs={{0,4},{1,5},{2,6},{3,7},{8,12},{9,13},{10,14},{11,15},{16,20},{17,... | collective-permute-start | bytes 786440 | tf_op jit(solution)/shard_map/ppermute | solution.py:359
  6.3 13.2 %collective-permute-start.3 = (f32[512,128]{1,0:T(8,128)S(1)}, f32[512,128]{1,0:T(8,128)S(1)}, u32[]{:S(2)}, u32[]{:S(2)}) collective-permute-start(f32[512,128]{1,0:T(8,128)S(1)} %to_columns.1.own_ref), channel_id=1, source_target_pairs={{1,2},{5,6},{9,10},{13,14},{17,18},{21,22},{25,26},{29,30},{0,3},{... | collective-permute-start | bytes 786440 | tf_op jit(solution)/shard_map/ppermute | solution.py:358
  6.7 13.5 %collective-permute-start.2 = (f32[512,128]{1,0:T(8,128)S(1)}, f32[512,128]{1,0:T(8,128)S(1)}, u32[]{:S(2)}, u32[]{:S(2)}) collective-permute-start(f32[512,128]{1,0:T(8,128)S(1)} %to_columns.1.own_ref), channel_id=1, source_target_pairs={{0,1},{2,3},{4,5},{6,7},{8,9},{10,11},{12,13},{14,15},{16,17},{18,... | collective-permute-start | bytes 786440 | tf_op jit(solution)/shard_map/ppermute | solution.py:357
  8.0 13.0 %copy-start = (f32[512,128]{1,0:T(8,128)}, f32[512,128]{1,0:T(8,128)S(1)}, u32[]{:S(2)}) copy-start(f32[512,128]{1,0:T(8,128)S(1)} %collective-permute-done.1.xb_ref) | copy-start | bytes 786436
  16.9 4.0 %collective-permute-start.4 = (f32[448,128]{1,0:T(8,128)S(1)}, f32[448,128]{1,0:T(8,128)S(1)}, u32[]{:S(2)}, u32[]{:S(2)}) collective-permute-start(f32[448,128]{1,0:T(8,128)S(1)} %get-tuple-element.12), channel_id=1, source_target_pairs={{0,1},{2,3},{4,5},{6,7},{8,9},{10,11},{12,13},{14,15},{16,17},{18,... | collective-permute-start | bytes 688136 | tf_op jit(solution)/shard_map/ppermute | solution.py:362
  17.0 6.5 %collective-permute-start.5 = (f32[448,128]{1,0:T(8,128)S(1)}, f32[448,128]{1,0:T(8,128)S(1)}, u32[]{:S(2)}, u32[]{:S(2)}) collective-permute-start(f32[448,128]{1,0:T(8,128)S(1)} %get-tuple-element.13), channel_id=1, source_target_pairs={{1,2},{5,6},{9,10},{13,14},{17,18},{21,22},{25,26},{29,30},{0,4},{... | collective-permute-start | bytes 688136 | tf_op jit(solution)/shard_map/ppermute | solution.py:363
  19.5 0.7 copy-start.6
  20.2 0.7 copy-start.8
  20.9 0.7 copy-start.10
  23.5 0.7 copy-start.12
  24.2 0.9 copy-start.1
  25.2 0.9 copy-start.7
  26.1 0.9 copy-start.9
  27.1 0.9 copy-start.11
  28.0 0.9 copy-start.13
  34.7 26.8 %copy-start.2 = (f32[512,128]{1,0:T(8,128)}, f32[512,128]{1,0:T(8,128)S(1)}, u32[]{:S(2)}) copy-start(f32[512,128]{1,0:T(8,128)S(1)} %get-tuple-element.14.own_ref) | copy-start | bytes 786436
  34.8 5.7 %collective-permute-start.7 = (f32[512,128]{1,0:T(8,128)S(1)}, f32[512,128]{1,0:T(8,128)S(1)}, u32[]{:S(2)}, u32[]{:S(2)}) collective-permute-start(f32[512,128]{1,0:T(8,128)S(1)} %get-tuple-element.14.own_ref), channel_id=1, source_target_pairs={{4,8},{5,9},{6,10},{7,11},{12,16},{13,17},{14,18},{15,19},{20,24},... | collective-permute-start | bytes 786440 | tf_op jit(solution)/shard_map/ppermute | solution.py:360
  34.8 15.4 %collective-permute-start.6 = (f32[512,128]{1,0:T(8,128)S(1)}, f32[512,128]{1,0:T(8,128)S(1)}, u32[]{:S(2)}, u32[]{:S(2)}) collective-permute-start(f32[512,128]{1,0:T(8,128)S(1)} %get-tuple-element.14.own_ref), channel_id=1, source_target_pairs={{0,4},{1,5},{2,6},{3,7},{8,12},{9,13},{10,14},{11,15},{16,20},{17,... | collective-permute-start | bytes 786440 | tf_op jit(solution)/shard_map/ppermute | solution.py:359
  39.5 21.3 %collective-permute-start.9 = (f32[512,128]{1,0:T(8,128)S(1)}, f32[512,128]{1,0:T(8,128)S(1)}, u32[]{:S(2)}, u32[]{:S(2)}) collective-permute-start(f32[512,128]{1,0:T(8,128)S(1)} %get-tuple-element.14.own_ref), channel_id=1, source_target_pairs={{1,2},{5,6},{9,10},{13,14},{17,18},{21,22},{25,26},{29,30},{0,3},{... | collective-permute-start | bytes 786440 | tf_op jit(solution)/shard_map/ppermute | solution.py:358
  39.6 21.9 %collective-permute-start.8 = (f32[512,128]{1,0:T(8,128)S(1)}, f32[512,128]{1,0:T(8,128)S(1)}, u32[]{:S(2)}, u32[]{:S(2)}) collective-permute-start(f32[512,128]{1,0:T(8,128)S(1)} %get-tuple-element.14.own_ref), channel_id=1, source_target_pairs={{0,1},{2,3},{4,5},{6,7},{8,9},{10,11},{12,13},{14,15},{16,17},{18,... | collective-permute-start | bytes 786440 | tf_op jit(solution)/shard_map/ppermute | solution.py:357
  50.3 11.3 %collective-permute-start.10 = (f32[448,128]{1,0:T(8,128)S(1)}, f32[448,128]{1,0:T(8,128)S(1)}, u32[]{:S(2)}, u32[]{:S(2)}) collective-permute-start(f32[448,128]{1,0:T(8,128)S(1)} %get-tuple-element.15), channel_id=1, source_target_pairs={{0,1},{2,3},{4,5},{6,7},{8,9},{10,11},{12,13},{14,15},{16,17},{18,... | collective-permute-start | bytes 688136 | tf_op jit(solution)/shard_map/ppermute | solution.py:362
  50.4 11.2 %collective-permute-start.11 = (f32[448,128]{1,0:T(8,128)S(1)}, f32[448,128]{1,0:T(8,128)S(1)}, u32[]{:S(2)}, u32[]{:S(2)}) collective-permute-start(f32[448,128]{1,0:T(8,128)S(1)} %get-tuple-element.16), channel_id=1, source_target_pairs={{1,2},{5,6},{9,10},{13,14},{17,18},{21,22},{25,26},{29,30},{0,4},{... | collective-permute-start | bytes 688136 | tf_op jit(solution)/shard_map/ppermute | solution.py:363
  52.9 40.0 %copy-start.15 = (f32[96,96]{1,0:T(8,128)S(1)}, f32[96,96]{1,0:T(8,128)}, u32[]{:S(2)}) copy-start(f32[96,96]{1,0:T(8,128)} %param.11) | copy-start | bytes 110596
  60.8 0.7 copy-start.4
  61.6 1.0 copy-start.3
  62.5 0.9 copy-start.5
  63.5 14.7 %copy-start.16 = (f32[4,96]{1,0:T(4,128)S(1)}, f32[4,96]{1,0:T(4,128)}, u32[]{:S(2)}) copy-start(f32[4,96]{1,0:T(4,128)} %project.2) | copy-start | bytes 4612
  79.6 13.3 %all-to-all-start = ((f32[32,8,96]{2,1,0:T(8,128)}), f32[32,8,96]{2,1,0:T(8,128)S(1)}, u32[]{:S(2)}, u32[]{:S(2)}) async-start(f32[32,8,96]{2,1,0:T(8,128)} %broadcast_in_dim.2), calls=%async_computation | async-start | bytes 262144 | tf_op jit(solution)/shard_map/all_to_all | solution.py:370
  92.8 3.9 %copy-start.14 = (f32[8,96]{1,0:T(8,128)}, f32[8,96]{1,0:T(8,128)S(1)}, u32[]{:S(2)}) copy-start(f32[8,96]{1,0:T(8,128)S(1)} %reduce_sum.9) | copy-start | bytes 9220

commit v2 on v1

--- a/solution.py
+++ b/solution.py
@@ -19,7 +19,7 @@
 
 BOTH = ("sim", "learn")
 VMEM = pl.BlockSpec(memory_space=pltpu.VMEM)
-WIDE = 56 * 1024 * 1024
+MIB = 1024 * 1024
 
 
 def both_ways(pairs):
@@ -71,6 +71,7 @@
         out_shape=pltpu.VMEM((cx * cy * nf, nz), jnp.float32),
         in_specs=[VMEM],
         out_specs=VMEM,
+        compiler_params=pltpu.CompilerParams(vmem_limit_bytes=2 * MIB),
         name="to_columns",
     )(fields.reshape(nf * cx * cy, nz))
 
@@ -102,6 +103,7 @@
         out_shape=(shape, shape),
         in_specs=[VMEM, VMEM],
         out_specs=(VMEM, VMEM),
+        compiler_params=pltpu.CompilerParams(vmem_limit_bytes=MIB),
         name="pack_corners",
     )(*in_vmem(xa, xb))
 
@@ -274,67 +276,86 @@
             pltpu.VMEM((wide * nf, nz), jnp.float32),
             pltpu.VMEM((rows, nz), jnp.float32),
         ],
+        compiler_params=pltpu.CompilerParams(vmem_limit_bytes=8 * MIB),
         name="advance",
     )(*in_vmem(*bricks, *corners), dif, sto)
 
 
-def project_kernel(cy, steps, basis_ref, snap_ref, out_ref, acc_ref):
-    modes, pair, cells, nz = basis_ref.shape
-    cx = cells // cy
-    step = pl.program_id(0)
-
-    @pl.when(step == 0)
-    def _():
-        acc_ref[...] = jnp.zeros_like(acc_ref)
-
-    total = None
-    for p in range(cx // 2):
-        left = [basis_ref[:, f, pl.ds(p * 2 * cy, 2 * cy), :].reshape(modes * 2 * cy, nz) for f in range(pair)]
-        right = [
-            snap_ref[pl.ds(f * cx + 2 * p, 2)].reshape(2 * steps * cy, nz).astype(jnp.bfloat16) for f in range(pair)
-        ]
-        term = lax.dot_general(
-            jnp.concatenate(left, axis=1),
-            jnp.concatenate(right, axis=1),
-            (((1,), (1,)), ((), ())),
-            preferred_element_type=jnp.float32,
+def split(value):
+    high = value.astype(jnp.bfloat16)
+    rest = value - high.astype(jnp.float32)
+    middle = rest.astype(jnp.bfloat16)
+    return high, middle, (rest - middle.astype(jnp.float32)).astype(jnp.bfloat16)
+
+
+def project_kernel(cx, cy, steps, copies, basis_ref, snap_ref, *refs):
+    earlier_ref, out_ref, acc_ref = refs if copies else (None, *refs)
+    modes, nf, _, nz = basis_ref.shape
+    pair = 2
+    for g in range(nf // pair):
+        total = None
+        for p in range(cx // 2):
+            left, right = [], []
+            for f in range(g * pair, (g + 1) * pair):
+                left.append(basis_ref[:, f, pl.ds(p * 2 * cy, 2 * cy), :].reshape(modes * 2 * cy, nz))
+                rows = snap_ref[pl.ds(f * cx + 2 * p, 2)].reshape(2 * steps * cy, nz)
+                right.append(rows.astype(jnp.bfloat16))
+            term = lax.dot_general(
+                jnp.concatenate(right, axis=1),
+                jnp.concatenate(left, axis=1),
+                (((1,), (1,)), ((), ())),
+                preferred_element_type=jnp.float32,
+            )
+            total = term if total is None else total + term
+        acc_ref[...] = total if g == 0 else acc_ref[...] + total
+
+    lanes = 8 * 2 * cy
+    blocks = modes * 2 * cy // lanes
+    row = lax.broadcasted_iota(jnp.int32, (cy, lanes), 0)
+    column = lax.broadcasted_iota(jnp.int32, (cy, lanes), 1)
+    same_y = row == lax.rem(column, cy)
+    first_x = lax.rem(column // cy, 2) == 0
+    mode_of = lax.broadcasted_iota(jnp.int32, (lanes, modes), 0) // (2 * cy)
+    mode = lax.broadcasted_iota(jnp.int32, (lanes, modes), 1)
+    summed = None
+    for k in range(blocks):
+        kept = []
+        for t in range(steps):
+            west = acc_ref[pl.ds(t * cy, cy), pl.ds(k * lanes, lanes)]
+            east = acc_ref[pl.ds((steps + t) * cy, cy), pl.ds(k * lanes, lanes)]
+            kept.append(jnp.where(same_y, jnp.where(first_x, west, east), 0.0))
+        gather = (mode - 8 * k == mode_of).astype(jnp.bfloat16)
+        term = jnp.dot(
+            jnp.concatenate(split(jnp.concatenate(kept, axis=0)), axis=0), gather, preferred_element_type=jnp.float32
         )
-        total = term if total is None else total + term
-    acc_ref[...] += total
-
-    @pl.when(step == pl.num_programs(0) - 1)
-    def _():
-        columns = 2 * steps * cy
-        row = lax.broadcasted_iota(jnp.int32, (2 * cy, columns), 0)
-        column = lax.broadcasted_iota(jnp.int32, (2 * cy, columns), 1)
-        same = (row // cy == column // (steps * cy)) & (row % cy == column % cy)
-        kept = acc_ref[...].reshape(modes, 2 * cy, columns) * same.astype(jnp.float32)[None]
-        kept = jnp.sum(kept, axis=1)
-        which = lax.broadcasted_iota(jnp.int32, (steps, columns), 0)
-        column = lax.broadcasted_iota(jnp.int32, (steps, columns), 1)
-        gather = (column // cy % steps == which).astype(jnp.float32)
-        out_ref[...] = lax.dot_general(
-            gather, kept, (((1,), (1,)), ((), ())),
-            precision=lax.Precision.HIGHEST, preferred_element_type=jnp.float32,
-        )
-
-
-def project(basis, snaps, steps):
-    modes, nf, cx, cy, nz = basis.shape
-    pair = 2
+        summed = term if summed is None else summed + term
+    count = steps * cy
+    summed = summed[:count] + summed[count : 2 * count] + summed[2 * count :]
+    result = jnp.sum(summed.reshape(steps, cy, modes), axis=1)
+    if copies:
+        both = jnp.concatenate([earlier_ref[...], result], axis=0)
+        for n in range(copies):
+            out_ref[n] = both
+    else:
+        out_ref[...] = result
+
+
+def project(basis, snaps, cx, cy, steps, earlier=None, copies=0):
+    modes = basis.shape[0]
+    shape = (steps, modes)
+    operands = in_vmem(snaps)
+    if copies:
+        shape = (copies, earlier.shape[0] + steps, modes)
+        operands += in_vmem(earlier)
     return pl.pallas_call(
-        functools.partial(project_kernel, cy, steps),
-        out_shape=jax.ShapeDtypeStruct((steps, modes), jnp.float32),
-        grid=(nf // pair,),
-        in_specs=[
-            pl.BlockSpec((modes, pair, cx * cy, nz), lambda i: (0, i, 0, 0)),
-            pl.BlockSpec((pair * cx, steps * cy, nz), lambda i: (i, 0, 0)),
-        ],
-        out_specs=pl.BlockSpec((steps, modes), lambda i: (0, 0)),
-        scratch_shapes=[pltpu.VMEM((modes * 2 * cy, 2 * steps * cy), jnp.float32)],
-        compiler_params=pltpu.CompilerParams(vmem_limit_bytes=WIDE),
+        functools.partial(project_kernel, cx, cy, steps, copies),
+        out_shape=jax.ShapeDtypeStruct(shape, jnp.float32) if copies else pltpu.VMEM(shape, jnp.float32),
+        in_specs=[VMEM] * (1 + len(operands)),
+        out_specs=VMEM,
+        scratch_shapes=[pltpu.VMEM((2 * steps * cy, modes * 2 * cy), jnp.float32)],
+        compiler_params=pltpu.CompilerParams(vmem_limit_bytes=8 * MIB),
         name="project",
-    )(basis.reshape(modes, nf, cx * cy, nz), *in_vmem(snaps))
+    )(basis, *operands)
 
 
 def pair_tables(modes):
@@ -344,57 +365,87 @@
     return (first_table, second_table)
 
 
+def infer_kernel(shares_ref, gram_ref, picks_ref, reduced_ref, pod_ref, rhs_ref):
+    steps, modes = reduced_ref.shape
+    block = rhs_ref.shape[1]
+    reduced = shares_ref[0]
+    for n in range(1, shares_ref.shape[0]):
+        reduced += shares_ref[n]
+    reduced_ref[...] = reduced
+    transposed = (((0,), (0,)), ((), ()))
+    pod_ref[...] = gram_ref[...] + lax.dot_general(
+        reduced, reduced, transposed, precision=lax.Precision.HIGHEST, preferred_element_type=jnp.float32
+    )
+    wide = picks_ref.shape[0]
+    padded = jnp.concatenate([reduced, jnp.zeros((steps, wide - modes), jnp.float32)], axis=1)
+    lane = lax.broadcasted_iota(jnp.int32, (steps, wide), 1)
+    widened = jnp.where(lane == 0, 1.0, pltpu.roll(padded, 1, 1))
+    picked = jnp.dot(jnp.concatenate(split(widened), axis=0), picks_ref[...], preferred_element_type=jnp.float32)
+    picked = picked[:steps] + picked[steps : 2 * steps] + picked[2 * steps :]
+    features = picked[:, :block] * picked[:, picks_ref.shape[1] // 2 :][:, :block]
+    row = lax.broadcasted_iota(jnp.int32, (steps, modes), 0)
+    changes = jnp.where(row < steps - 1, pltpu.roll(reduced, steps - 1, 0) - reduced, 0.0)
+    ch, cm, cl = split(changes)
+    fh, fm, fl = split(features)
+    rhs_ref[...] = lax.dot_general(
+        jnp.concatenate([ch, ch, cm, ch, cm, cl], axis=0),
+        jnp.concatenate([fh, fm, fh, fl, fm, fh], axis=0),
+        transposed,
+        preferred_element_type=jnp.float32,
+    )
+
+
+def infer(shares, gram_old, nl):
+    count, steps, modes = shares.shape
+    tables = np.stack(pair_tables(modes))
+    block = tables.shape[1] // nl
+    lanes = -(-block // 128) * 128
+    wide = -(-(modes + 1) // 128) * 128
+    index = lax.dynamic_slice_in_dim(jnp.asarray(tables), lax.axis_index("learn") * block, block, axis=1)
+    index = jnp.pad(index, ((0, 0), (0, lanes - block)), constant_values=-1).reshape(1, 2 * lanes)
+    picks = (lax.broadcasted_iota(jnp.int32, (wide, 2 * lanes), 0) == index).astype(jnp.bfloat16)
+    reduced, pod_gram, rhs = pl.pallas_call(
+        infer_kernel,
+        out_shape=(
+            jax.ShapeDtypeStruct((steps, modes), jnp.float32),
+            jax.ShapeDtypeStruct((modes, modes), jnp.float32),
+            jax.ShapeDtypeStruct((modes, block), jnp.float32),
+        ),
+        in_specs=[VMEM] * 3,
+        out_specs=(VMEM, VMEM, VMEM),
+        compiler_params=pltpu.CompilerParams(vmem_limit_bytes=8 * MIB),
+        name="infer",
+    )(*in_vmem(shares, gram_old, picks))
+    return reduced.T, pod_gram, rhs.T
+
+
 def body(fields, diffusivity, stoich, basis, gram_old):
-    modes = basis.shape[0]
     nf, cx, cy, nz = fields.shape
     ns, nl = lax.axis_size("sim"), lax.axis_size("learn")
     steps = min(cx, cy) // 2
+    rounds = STEPS // steps
     x_even, x_odd, y_even, y_odd, y_far = swaps(ns, nl)
     state = to_columns(fields)
-    rounds = STEPS // steps
-    parts = []
+    (basis,) = in_vmem(basis.reshape(basis.shape[0], nf, cx * cy, nz))
+    share = None
     for n in range(rounds):
         ya = lax.ppermute(state, BOTH, y_even)
         yb = lax.ppermute(state, BOTH, y_odd)
         xa = lax.ppermute(state, BOTH, x_even)
         xb = lax.ppermute(state, BOTH, x_odd)
+        if n:
+            part = project(basis, snaps, cx, cy, steps)
+            xa, xb, part = lax.optimization_barrier((xa, xb, part))
+            share = part if share is None else jnp.concatenate([share, part], axis=0)
         to_a, to_b = pack_corners(xa, xb, cx, cy, nf)
         ca = lax.ppermute(to_a, BOTH, y_even)
         cb = lax.ppermute(to_b, BOTH, y_far)
         bricks = (state, xa, xb, ya, yb)
         state, snaps = advance(bricks, (ca, cb), diffusivity, stoich, cx, cy, nf, steps, n == rounds - 1)
-        parts.append(project(basis, snaps, steps))
-    state = state.reshape(fields.shape)
-    local = jnp.concatenate(parts, axis=0)
-    sent = jnp.broadcast_to(local[None], (ns * nl, *local.shape))
-    reduced_t = jnp.sum(lax.all_to_all(sent, BOTH, 0, 0), axis=0)
-    reduced = reduced_t.T
-    pod_gram = gram_old + lax.dot_general(
-        reduced_t, reduced_t, (((0,), (0,)), ((), ())),
-        precision=lax.Precision.HIGHEST, preferred_element_type=jnp.float32,
-    )
-    widened = jnp.concatenate([jnp.ones((1, STEPS), jnp.float32), reduced], axis=0)
-    first_table, second_table = pair_tables(modes)
-    block_rows = first_table.shape[0] // nl
-    start = lax.axis_index("learn") * block_rows
-    first_rows = lax.dynamic_slice_in_dim(jnp.asarray(first_table), start, block_rows)
-    second_rows = lax.dynamic_slice_in_dim(jnp.asarray(second_table), start, block_rows)
-    columns = jnp.arange(modes + 1, dtype=jnp.int32)
-    pick_first = (first_rows[:, None] == columns[None, :]).astype(jnp.float32)
-    pick_second = (second_rows[:, None] == columns[None, :]).astype(jnp.float32)
-    earlier = widened[:, :-1]
-    left_part = jnp.dot(
-        pick_first, earlier, precision=lax.Precision.HIGHEST, preferred_element_type=jnp.float32
-    )
-    right_part = jnp.dot(
-        pick_second, earlier, precision=lax.Precision.HIGHEST, preferred_element_type=jnp.float32
-    )
-    features = left_part * right_part
-    changes = reduced[:, 1:] - reduced[:, :-1]
-    rhs_block = jnp.dot(
-        features, changes.T, precision=lax.Precision.HIGHEST, preferred_element_type=jnp.float32
-    )
-    return (state, reduced, pod_gram, rhs_block)
+    sent = project(basis, snaps, cx, cy, steps, share, ns * nl)
+    shares = lax.all_to_all(sent, BOTH, 0, 0)
+    reduced, pod_gram, rhs_block = infer(shares, gram_old, nl)
+    return (state.reshape(fields.shape), reduced, pod_gram, rhs_block)
 
 
 def solution(mesh):

time: 97.3 us -> 82.3 us (0.85)
  Pallas kernels: 29.6 us -> 22.7 us
  matrix products: 3.83 us -> 0 us
  starting transfers between devices: 22.2 us -> 19.7 us
    ppermute x2, waiting for transfers between devices: 18.6 us -> 11.2 us  [body(): xa = lax.ppermute(state, BOTH, x_even)]
    pallas_call x2 -> x3, Pallas kernels: 15.9 us -> 10.3 us  [the longest x2 8.95 us: project(): pl.pallas_call(functools.partial(project_kernel, cx, cy, steps, copies),...]
    ppermute x2, waiting for transfers between devices: 1.88 us -> 7.15 us  [body(): cb = lax.ppermute(to_b, BOTH, y_far)]
    dot_general x4 -> x0, matrix products: 3.83 us -> none  [the longest x1 1.58 us: body(): jnp.dot(features, changes.T, precision=lax.Precision.HIGHEST, preferred_e...]
    ppermute x2, starting transfers between devices: 8.73 us -> 6.25 us  [body(): xa = lax.ppermute(state, BOTH, x_even)]
    all_to_all x1, waiting for transfers between devices: 6.63 us -> 8.08 us  [body(): shares = lax.all_to_all(sent, BOTH, 0, 0)]
    unnamed x34 -> x16, local copies, waits for them, and re-layouts: 10.2 us -> 11.4 us
    ppermute x2, starting transfers between devices: 2.08 us -> 1.01 us  [body(): ya = lax.ppermute(state, BOTH, y_even)]
  transfers between devices with their start and end apart: 13 -> 13, of which waited for: 4 -> 5; matrix products, arithmetic and copies ran while one was open for 2% -> 1% of each run, Pallas kernels for 8% -> 5%
where the time goes in v2:
time: 82.3 us; the launch traced here: 82 us
  waiting for transfers between devices  26.5 us (32%)
  Pallas kernels  22.7 us (28%)
  starting transfers between devices  19.7 us (24%)
  local copies, waits for them, and re-layouts  12.2 us (15%)
    pallas_call x2, Pallas kernels, advance(): pl.pallas_call(functools.partial(round_kernel, cx, cy, nf, steps, last),...  12.2 us
    unnamed x16, local copies, waits for them, and re-layouts  11.4 us
    ppermute x2, waiting for transfers between devices, body(): xa = lax.ppermute(state, BOTH, x_even)  11.2 us
    pallas_call x2, Pallas kernels, project(): pl.pallas_call(functools.partial(project_kernel, cx, cy, steps, copies),...  8.95 us
    all_to_all x1, waiting for transfers between devices, body(): shares = lax.all_to_all(sent, BOTH, 0, 0)  8.08 us
    ppermute x2, waiting for transfers between devices, body(): cb = lax.ppermute(to_b, BOTH, y_far)  7.15 us
    ppermute x2, starting transfers between devices, body(): xa = lax.ppermute(state, BOTH, x_even)  6.25 us
    all_to_all x1, starting transfers between devices, body(): shares = lax.all_to_all(sent, BOTH, 0, 0)  5.65 us
  transfers between devices with their start and end apart: 13, of which 5 were waited for; matrix products, arithmetic and copies ran while one was open for 1% of the time, Pallas kernels for 5%

profile of v2, /device:TPU:0, one launch (start us, length us, event | category | flops | bytes accessed | tf_op | source)
XLA Modules:
  0.0 82.0 jit_solution(17757402789643674193)
XLA Ops:
  0.6 0.0 copy-start.2
  0.6 0.9 %copy-done.2 = f32[8,8,8,128]{3,2,1,0:T(8,128)S(1)} copy-done((f32[8,8,8,128]{3,2,1,0:T(8,128)S(1)}, f32[8,8,8,128]{3,2,1,0:T(8,128)}, u32[]{:S(2)}) %copy-start.2) | copy-done | bytes 262168
  1.6 0.2 to_columns.1.own_ref
  1.7 3.0 %collective-permute-start = (f32[512,128]{1,0:T(8,128)S(1)}, f32[512,128]{1,0:T(8,128)S(1)}, u32[]{:S(2)}, u32[]{:S(2)}) collective-permute-start(f32[512,128]{1,0:T(8,128)S(1)} %to_columns.1.own_ref), channel_id=1, source_target_pairs={{0,4},{1,5},{2,6},{3,7},{8,12},{9,13},{10,14},{11,15},{16,20},{17,... | collective-permute-start | bytes 786440 | tf_op jit(solution)/shard_map/ppermute | solution.py:434
  4.8 0.0 collective-permute-start.1
  4.8 0.5 collective-permute-start.2
  5.3 1.1 %collective-permute-start.3 = (f32[512,128]{1,0:T(8,128)S(1)}, f32[512,128]{1,0:T(8,128)S(1)}, u32[]{:S(2)}, u32[]{:S(2)}) collective-permute-start(f32[512,128]{1,0:T(8,128)S(1)} %to_columns.1.own_ref), channel_id=1, source_target_pairs={{1,2},{5,6},{9,10},{13,14},{17,18},{21,22},{25,26},{29,30},{0,3},{... | collective-permute-start | bytes 786440 | tf_op jit(solution)/shard_map/ppermute | solution.py:433
  6.4 9.5 %collective-permute-done.xa_ref = f32[512,128]{1,0:T(8,128)S(1)} collective-permute-done((f32[512,128]{1,0:T(8,128)S(1)}, f32[512,128]{1,0:T(8,128)S(1)}, u32[]{:S(2)}, u32[]{:S(2)}) %collective-permute-start) | collective-permute-done | bytes 262176 | tf_op jit(solution)/shard_map/ppermute | solution.py:434
  16.0 0.0 collective-permute-done.1.xb_ref
  16.0 0.1 collective-permute-start.4
  16.1 2.5 %collective-permute-start.5 = (f32[448,128]{1,0:T(8,128)S(1)}, f32[448,128]{1,0:T(8,128)S(1)}, u32[]{:S(2)}, u32[]{:S(2)}) collective-permute-start(f32[448,128]{1,0:T(8,128)S(1)} %get-tuple-element.19), channel_id=1, source_target_pairs={{1,2},{5,6},{9,10},{13,14},{17,18},{21,22},{25,26},{29,30},{0,4},{... | collective-permute-start | bytes 688136 | tf_op jit(solution)/shard_map/ppermute | solution.py:442
  18.6 0.0 collective-permute-done.2.ya_ref
  18.6 0.0 collective-permute-done.3.yb_ref
  18.6 0.0 collective-permute-done.4.ca_ref
  18.6 4.0 %collective-permute-done.5.cb_ref = f32[448,128]{1,0:T(8,128)S(1)} collective-permute-done((f32[448,128]{1,0:T(8,128)S(1)}, f32[448,128]{1,0:T(8,128)S(1)}, u32[]{:S(2)}, u32[]{:S(2)}) %collective-permute-start.5) | collective-permute-done | bytes 229408 | tf_op jit(solution)/shard_map/ppermute | solution.py:442
  22.6 0.0 copy-start.4
  22.6 0.7 copy-done.4
  23.3 0.0 copy-start.6
  23.3 0.7 copy-done.6
  23.9 5.7 %advance.2 = (f32[512,128]{1,0:T(8,128)S(1)}, f32[64,32,128]{2,1,0:T(8,128)S(1)}) custom-call(f32[512,128]{1,0:T(8,128)S(1)} %to_columns.1.own_ref, f32[512,128]{1,0:T(8,128)S(1)} %collective-permute-done.xa_ref, f32[512,128]{1,0:T(8,128)S(1)} %collective-permute-done.1.xb_ref, f32[512,128]{1,0:T(8,128)S(1)} %collective-permute-done.2.ya_ref, ...), custom_call_target="tpu_custom_call" | custom-call | tf_op jit(solution)/shard_map/advance/pallas_call | solution.py:266
  29.6 3.2 %collective-permute-start.6 = (f32[512,128]{1,0:T(8,128)S(1)}, f32[512,128]{1,0:T(8,128)S(1)}, u32[]{:S(2)}, u32[]{:S(2)}) collective-permute-start(f32[512,128]{1,0:T(8,128)S(1)} %get-tuple-element.20.own_ref), channel_id=1, source_target_pairs={{0,4},{1,5},{2,6},{3,7},{8,12},{9,13},{10,14},{11,15},{16,20},{17,... | collective-permute-start | bytes 786440 | tf_op jit(solution)/shard_map/ppermute | solution.py:434
  32.8 0.0 collective-permute-start.7
  32.8 0.5 collective-permute-start.8
  33.3 0.4 collective-permute-start.9
  33.8 0.0 copy-start
  33.8 4.6 %copy-done = bf16[96,8,8,8,128]{4,3,2,1,0:T(8,128)(2,1)S(1)} copy-done((bf16[96,8,8,8,128]{4,3,2,1,0:T(8,128)(2,1)S(1)}, bf16[96,8,8,8,128]{4,3,2,1,0:T(8,128)(2,1)}, u32[]{:S(2)}) %copy-start) | copy-done | bytes 12582936
  38.4 0.0 copy-start.5
  38.4 0.0 copy-start.7
  38.4 4.1 %project.2.refs_0_ = f32[4,96]{1,0:T(4,128)S(1)} custom-call(bf16[96,8,64,128]{3,2,1,0:T(8,128)(2,1)S(1)} %bitcast.5, f32[64,32,128]{2,1,0:T(8,128)S(1)} %get-tuple-element.21.snap_ref), custom_call_target="tpu_custom_call" | custom-call | tf_op jit(solution)/shard_map/project/pallas_call | solution.py:350
  42.5 1.7 %collective-permute-done.6.xa_ref = f32[512,128]{1,0:T(8,128)S(1)} collective-permute-done((f32[512,128]{1,0:T(8,128)S(1)}, f32[512,128]{1,0:T(8,128)S(1)}, u32[]{:S(2)}, u32[]{:S(2)}) %collective-permute-start.6) | collective-permute-done | bytes 262176 | tf_op jit(solution)/shard_map/ppermute | solution.py:434
  44.2 0.0 collective-permute-done.7.xb_ref
  44.2 0.1 collective-permute-start.10
  44.3 2.5 %collective-permute-start.11 = (f32[448,128]{1,0:T(8,128)S(1)}, f32[448,128]{1,0:T(8,128)S(1)}, u32[]{:S(2)}, u32[]{:S(2)}) collective-permute-start(f32[448,128]{1,0:T(8,128)S(1)} %get-tuple-element.25), channel_id=1, source_target_pairs={{1,2},{5,6},{9,10},{13,14},{17,18},{21,22},{25,26},{29,30},{0,4},{... | collective-permute-start | bytes 688136 | tf_op jit(solution)/shard_map/ppermute | solution.py:442
  46.8 0.8 constant_dynamic-slice_fusion
  47.7 0.0 collective-permute-done.8.ya_ref
  47.7 0.0 collective-permute-done.9.yb_ref
  47.7 0.0 collective-permute-done.10.ca_ref
  47.7 3.2 %collective-permute-done.11.cb_ref = f32[448,128]{1,0:T(8,128)S(1)} collective-permute-done((f32[448,128]{1,0:T(8,128)S(1)}, f32[448,128]{1,0:T(8,128)S(1)}, u32[]{:S(2)}, u32[]{:S(2)}) %collective-permute-start.11) | collective-permute-done | bytes 229408 | tf_op jit(solution)/shard_map/ppermute | solution.py:442
  50.8 0.0 copy-done.5
  50.8 0.0 copy-done.7
  50.9 6.5 %advance.3 = (f32[512,128]{1,0:T(8,128)}, f32[64,32,128]{2,1,0:T(8,128)S(1)}) custom-call(f32[512,128]{1,0:T(8,128)S(1)} %get-tuple-element.20.own_ref, f32[512,128]{1,0:T(8,128)S(1)} %collective-permute-done.6.xa_ref, f32[512,128]{1,0:T(8,128)S(1)} %collective-permute-done.7.xb_ref, f32[512,128]{1,0:T(8,128)S(1)} %collective-permute-done.8.ya_ref, ...), custom_call_target="tpu_custom_call" | custom-call | tf_op jit(solution)/shard_map/advance/pallas_call | solution.py:266
  57.4 4.6 %copy-done.1 = bf16[96,8,8,8,128]{4,3,2,1,0:T(8,128)(2,1)S(1)} copy-done((bf16[96,8,8,8,128]{4,3,2,1,0:T(8,128)(2,1)S(1)}, bf16[96,8,8,8,128]{4,3,2,1,0:T(8,128)(2,1)}, u32[]{:S(2)}) %copy-start.1) | copy-done | bytes 12582936
  62.0 4.8 %project.3 = f32[32,8,96]{2,1,0:T(8,128)} custom-call(bf16[96,8,64,128]{3,2,1,0:T(8,128)(2,1)S(1)} %bitcast.6, f32[64,32,128]{2,1,0:T(8,128)S(1)} %get-tuple-element.27.snap_ref, f32[4,96]{1,0:T(4,128)S(1)} %project.2.refs_0_), custom_call_target="tpu_custom_call" | custom-call | tf_op jit(solution)/shard_map/project/pallas_call | solution.py:350
  66.8 5.7 %all-to-all-start = ((f32[32,8,96]{2,1,0:T(8,128)}), f32[32,8,96]{2,1,0:T(8,128)S(1)}, u32[]{:S(2)}, u32[]{:S(2)}) async-start(f32[32,8,96]{2,1,0:T(8,128)} %project.3), calls=%async_computation | async-start | bytes 262144 | tf_op jit(solution)/shard_map/all_to_all | solution.py:446
  72.4 0.1 fusion.picks_ref
  72.5 8.1 %all-to-all-done.shares_ref = f32[32,8,96]{2,1,0:T(8,128)S(1)} async-done(((f32[32,8,96]{2,1,0:T(8,128)}), f32[32,8,96]{2,1,0:T(8,128)S(1)}, u32[]{:S(2)}, u32[]{:S(2)}) %all-to-all-start) | async-done | bytes 98336 | tf_op jit(solution)/shard_map/all_to_all | solution.py:446
  80.6 0.0 copy-done.3
  80.6 1.3 %infer.1 = (f32[8,96]{1,0:T(8,128)}, f32[96,96]{1,0:T(8,128)}, f32[96,1188]{1,0:T(8,128)}) custom-call(f32[32,8,96]{2,1,0:T(8,128)S(1)} %all-to-all-done.shares_ref, f32[96,96]{1,0:T(8,128)S(1)} %copy-done.3, bf16[128,2560]{1,0:T(8,128)(2,1)S(1)} %fusion.picks_ref), custom_call_target="tpu_custom_call" | custom-call | tf_op jit(solution)/shard_map/infer/pallas_call | solution.py:407
  (6 shorter events, 0.1 us)
Async XLA Ops:
  0.6 1.0 %copy-start.2 = (f32[8,8,8,128]{3,2,1,0:T(8,128)S(1)}, f32[8,8,8,128]{3,2,1,0:T(8,128)}, u32[]{:S(2)}) copy-start(f32[8,8,8,128]{3,2,1,0:T(8,128)} %param.6) | copy-start | bytes 786436
  1.7 14.2 %collective-permute-start = (f32[512,128]{1,0:T(8,128)S(1)}, f32[512,128]{1,0:T(8,128)S(1)}, u32[]{:S(2)}, u32[]{:S(2)}) collective-permute-start(f32[512,128]{1,0:T(8,128)S(1)} %to_columns.1.own_ref), channel_id=1, source_target_pairs={{0,4},{1,5},{2,6},{3,7},{8,12},{9,13},{10,14},{11,15},{16,20},{17,... | collective-permute-start | bytes 786440 | tf_op jit(solution)/shard_map/ppermute | solution.py:434
  4.8 11.2 %collective-permute-start.1 = (f32[512,128]{1,0:T(8,128)S(1)}, f32[512,128]{1,0:T(8,128)S(1)}, u32[]{:S(2)}, u32[]{:S(2)}) collective-permute-start(f32[512,128]{1,0:T(8,128)S(1)} %to_columns.1.own_ref), channel_id=1, source_target_pairs={{4,8},{5,9},{6,10},{7,11},{12,16},{13,17},{14,18},{15,19},{20,24},... | collective-permute-start | bytes 786440 | tf_op jit(solution)/shard_map/ppermute | solution.py:435
  4.8 13.9 %collective-permute-start.2 = (f32[512,128]{1,0:T(8,128)S(1)}, f32[512,128]{1,0:T(8,128)S(1)}, u32[]{:S(2)}, u32[]{:S(2)}) collective-permute-start(f32[512,128]{1,0:T(8,128)S(1)} %to_columns.1.own_ref), channel_id=1, source_target_pairs={{0,1},{2,3},{4,5},{6,7},{8,9},{10,11},{12,13},{14,15},{16,17},{18,... | collective-permute-start | bytes 786440 | tf_op jit(solution)/shard_map/ppermute | solution.py:432
  5.3 13.3 %collective-permute-start.3 = (f32[512,128]{1,0:T(8,128)S(1)}, f32[512,128]{1,0:T(8,128)S(1)}, u32[]{:S(2)}, u32[]{:S(2)}) collective-permute-start(f32[512,128]{1,0:T(8,128)S(1)} %to_columns.1.own_ref), channel_id=1, source_target_pairs={{1,2},{5,6},{9,10},{13,14},{17,18},{21,22},{25,26},{29,30},{0,3},{... | collective-permute-start | bytes 786440 | tf_op jit(solution)/shard_map/ppermute | solution.py:433
  16.0 2.6 %collective-permute-start.4 = (f32[448,128]{1,0:T(8,128)S(1)}, f32[448,128]{1,0:T(8,128)S(1)}, u32[]{:S(2)}, u32[]{:S(2)}) collective-permute-start(f32[448,128]{1,0:T(8,128)S(1)} %get-tuple-element.18), channel_id=1, source_target_pairs={{0,1},{2,3},{4,5},{6,7},{8,9},{10,11},{12,13},{14,15},{16,17},{18,... | collective-permute-start | bytes 688136 | tf_op jit(solution)/shard_map/ppermute | solution.py:441
  16.1 6.5 %collective-permute-start.5 = (f32[448,128]{1,0:T(8,128)S(1)}, f32[448,128]{1,0:T(8,128)S(1)}, u32[]{:S(2)}, u32[]{:S(2)}) collective-permute-start(f32[448,128]{1,0:T(8,128)S(1)} %get-tuple-element.19), channel_id=1, source_target_pairs={{1,2},{5,6},{9,10},{13,14},{17,18},{21,22},{25,26},{29,30},{0,4},{... | collective-permute-start | bytes 688136 | tf_op jit(solution)/shard_map/ppermute | solution.py:442
  22.6 0.7 copy-start.4
  23.3 0.7 copy-start.6
  29.6 14.6 %collective-permute-start.6 = (f32[512,128]{1,0:T(8,128)S(1)}, f32[512,128]{1,0:T(8,128)S(1)}, u32[]{:S(2)}, u32[]{:S(2)}) collective-permute-start(f32[512,128]{1,0:T(8,128)S(1)} %get-tuple-element.20.own_ref), channel_id=1, source_target_pairs={{0,4},{1,5},{2,6},{3,7},{8,12},{9,13},{10,14},{11,15},{16,20},{17,... | collective-permute-start | bytes 786440 | tf_op jit(solution)/shard_map/ppermute | solution.py:434
  32.8 11.4 %collective-permute-start.7 = (f32[512,128]{1,0:T(8,128)S(1)}, f32[512,128]{1,0:T(8,128)S(1)}, u32[]{:S(2)}, u32[]{:S(2)}) collective-permute-start(f32[512,128]{1,0:T(8,128)S(1)} %get-tuple-element.20.own_ref), channel_id=1, source_target_pairs={{4,8},{5,9},{6,10},{7,11},{12,16},{13,17},{14,18},{15,19},{20,24},... | collective-permute-start | bytes 786440 | tf_op jit(solution)/shard_map/ppermute | solution.py:435
  32.8 14.8 %collective-permute-start.8 = (f32[512,128]{1,0:T(8,128)S(1)}, f32[512,128]{1,0:T(8,128)S(1)}, u32[]{:S(2)}, u32[]{:S(2)}) collective-permute-start(f32[512,128]{1,0:T(8,128)S(1)} %get-tuple-element.20.own_ref), channel_id=1, source_target_pairs={{0,1},{2,3},{4,5},{6,7},{8,9},{10,11},{12,13},{14,15},{16,17},{18,... | collective-permute-start | bytes 786440 | tf_op jit(solution)/shard_map/ppermute | solution.py:432
  33.3 14.3 %collective-permute-start.9 = (f32[512,128]{1,0:T(8,128)S(1)}, f32[512,128]{1,0:T(8,128)S(1)}, u32[]{:S(2)}, u32[]{:S(2)}) collective-permute-start(f32[512,128]{1,0:T(8,128)S(1)} %get-tuple-element.20.own_ref), channel_id=1, source_target_pairs={{1,2},{5,6},{9,10},{13,14},{17,18},{21,22},{25,26},{29,30},{0,3},{... | collective-permute-start | bytes 786440 | tf_op jit(solution)/shard_map/ppermute | solution.py:433
  33.8 4.6 %copy-start = (bf16[96,8,8,8,128]{4,3,2,1,0:T(8,128)(2,1)S(1)}, bf16[96,8,8,8,128]{4,3,2,1,0:T(8,128)(2,1)}, u32[]{:S(2)}) copy-start(bf16[96,8,8,8,128]{4,3,2,1,0:T(8,128)(2,1)} %param.9) | copy-start | bytes 37748740
  38.4 12.5 %copy-start.5 = (f32[8]{0:T(128)S(1)}, f32[8]{0:T(128)}, u32[]{:S(2)}) copy-start(f32[8]{0:T(128)} %dif_ref.3) | copy-start | bytes 100
  38.4 12.5 %copy-start.7 = (f32[8]{0:T(128)S(1)}, f32[8]{0:T(128)}, u32[]{:S(2)}) copy-start(f32[8]{0:T(128)} %sto_ref.3) | copy-start | bytes 100
  44.2 3.4 %collective-permute-start.10 = (f32[448,128]{1,0:T(8,128)S(1)}, f32[448,128]{1,0:T(8,128)S(1)}, u32[]{:S(2)}, u32[]{:S(2)}) collective-permute-start(f32[448,128]{1,0:T(8,128)S(1)} %get-tuple-element.24), channel_id=1, source_target_pairs={{0,1},{2,3},{4,5},{6,7},{8,9},{10,11},{12,13},{14,15},{16,17},{18,... | collective-permute-start | bytes 688136 | tf_op jit(solution)/shard_map/ppermute | solution.py:441
  44.3 6.5 %collective-permute-start.11 = (f32[448,128]{1,0:T(8,128)S(1)}, f32[448,128]{1,0:T(8,128)S(1)}, u32[]{:S(2)}, u32[]{:S(2)}) collective-permute-start(f32[448,128]{1,0:T(8,128)S(1)} %get-tuple-element.25), channel_id=1, source_target_pairs={{1,2},{5,6},{9,10},{13,14},{17,18},{21,22},{25,26},{29,30},{0,4},{... | collective-permute-start | bytes 688136 | tf_op jit(solution)/shard_map/ppermute | solution.py:442
  57.4 4.6 %copy-start.1 = (bf16[96,8,8,8,128]{4,3,2,1,0:T(8,128)(2,1)S(1)}, bf16[96,8,8,8,128]{4,3,2,1,0:T(8,128)(2,1)}, u32[]{:S(2)}) copy-start(bf16[96,8,8,8,128]{4,3,2,1,0:T(8,128)(2,1)} %param.9) | copy-start | bytes 37748740
  61.9 18.7 %copy-start.3 = (f32[96,96]{1,0:T(8,128)S(1)}, f32[96,96]{1,0:T(8,128)}, u32[]{:S(2)}) copy-start(f32[96,96]{1,0:T(8,128)} %gram_ref.1) | copy-start | bytes 110596
  66.8 13.9 %all-to-all-start = ((f32[32,8,96]{2,1,0:T(8,128)}), f32[32,8,96]{2,1,0:T(8,128)S(1)}, u32[]{:S(2)}, u32[]{:S(2)}) async-start(f32[32,8,96]{2,1,0:T(8,128)} %project.3), calls=%async_computation | async-start | bytes 262144 | tf_op jit(solution)/shard_map/all_to_all | solution.py:446

commit v3 on v2

--- a/solution.py
+++ b/solution.py
@@ -19,6 +19,7 @@
 
 BOTH = ("sim", "learn")
 VMEM = pl.BlockSpec(memory_space=pltpu.VMEM)
+SMEM = pl.BlockSpec(memory_space=pltpu.SMEM)
 MIB = 1024 * 1024
 
 
@@ -58,22 +59,28 @@
                 body(a, b)
 
 
-def columns_kernel(cx, cy, native_ref, out_ref):
+def columns_kernel(cx, cy, dif_ref, sto_ref, native_ref, out_ref, factors_ref):
     nf = native_ref.shape[0] // (cx * cy)
+    field = lax.broadcasted_iota(jnp.int32, (nf, native_ref.shape[1]), 0)
+    for n, ref in enumerate((dif_ref, sto_ref)):
+        value = jnp.zeros(field.shape, jnp.float32)
+        for f in range(nf):
+            value = jnp.where(field == f, ref[f], value)
+        factors_ref[n] = value
     for c in range(cx * cy):
         out_ref[pl.ds(c * nf, nf), :] = native_ref[pl.ds(c, nf, stride=cx * cy), :]
 
 
-def to_columns(fields):
+def to_columns(fields, diffusivity, stoich):
     nf, cx, cy, nz = fields.shape
     return pl.pallas_call(
         functools.partial(columns_kernel, cx, cy),
-        out_shape=pltpu.VMEM((cx * cy * nf, nz), jnp.float32),
-        in_specs=[VMEM],
-        out_specs=VMEM,
+        out_shape=(pltpu.VMEM((cx * cy * nf, nz), jnp.float32), pltpu.VMEM((2, nf, nz), jnp.float32)),
+        in_specs=[SMEM, SMEM, VMEM],
+        out_specs=(VMEM, VMEM),
         compiler_params=pltpu.CompilerParams(vmem_limit_bytes=2 * MIB),
         name="to_columns",
-    )(fields.reshape(nf * cx * cy, nz))
+    )(diffusivity, stoich, fields.reshape(nf * cx * cy, nz))
 
 
 def pack_kernel(cx, cy, nf, xa_ref, xb_ref, to_a_ref, to_b_ref):
@@ -109,7 +116,7 @@
 
 
 def round_kernel(
-    cx, cy, nf, steps, last, own_ref, xa_ref, xb_ref, ya_ref, yb_ref, ca_ref, cb_ref, dif_ref, sto_ref,
+    cx, cy, nf, steps, last, own_ref, xa_ref, xb_ref, ya_ref, yb_ref, ca_ref, cb_ref, factors_ref,
     state_ref, snap_ref, u_ref, m_ref, rate_ref,
 ):
     nz = own_ref.shape[1]
@@ -165,12 +172,8 @@
     pl.when(jnp.logical_not(has_south))(lambda: clear(0, wide_x, 0, reach))
     pl.when(jnp.logical_not(has_north))(lambda: clear(0, wide_x, reach + cy, wide_y))
 
-    field = lax.broadcasted_iota(jnp.int32, (nf, nz), 0)
     lane = lax.broadcasted_iota(jnp.int32, (nf, nz), 1)
-    diffusivity, stoich = jnp.zeros((nf, nz), jnp.float32), jnp.zeros((nf, nz), jnp.float32)
-    for f in range(nf):
-        diffusivity = jnp.where(field == f, dif_ref[f], diffusivity)
-        stoich = jnp.where(field == f, sto_ref[f], stoich)
+    diffusivity, stoich = factors_ref[0], factors_ref[1]
 
     def coefficients(dt):
         return (
@@ -257,19 +260,18 @@
             state_ref[pl.ds(i * cy * nf, cy * nf), :] = rows
 
 
-def advance(bricks, corners, dif, sto, cx, cy, nf, steps, last):
+def advance(bricks, corners, factors, cx, cy, nf, steps, last):
     nz = bricks[0].shape[1]
     wide = (cx + 4 * steps) * (cy + 4 * steps)
     rows = max(cx, 2 * steps) * (cy + 4 * steps + nf)
     shape = (nf * cx * cy, nz)
-    scalars = pl.BlockSpec(memory_space=pltpu.SMEM)
     return pl.pallas_call(
         functools.partial(round_kernel, cx, cy, nf, steps, last),
         out_shape=(
-            jax.ShapeDtypeStruct(shape, jnp.float32) if last else pltpu.VMEM(shape, jnp.float32),
+            pltpu.VMEM(shape, jnp.float32),
             pltpu.VMEM((nf * cx, steps * cy, nz), jnp.float32),
         ),
-        in_specs=[VMEM] * 7 + [scalars] * 2,
+        in_specs=[VMEM] * 8,
         out_specs=(VMEM, VMEM),
         scratch_shapes=[
             pltpu.VMEM((wide * nf, nz), jnp.float32),
@@ -278,7 +280,7 @@
         ],
         compiler_params=pltpu.CompilerParams(vmem_limit_bytes=8 * MIB),
         name="advance",
-    )(*in_vmem(*bricks, *corners), dif, sto)
+    )(*in_vmem(*bricks, *corners, factors))
 
 
 def split(value):
@@ -395,15 +397,32 @@
     )
 
 
-def infer(shares, gram_old, nl):
-    count, steps, modes = shares.shape
+def picks_kernel(tables_ref, after_ref, out_ref):
+    del after_ref
+    index = tables_ref[pl.ds(lax.axis_index("learn"), 1), :]
+    place = lax.broadcasted_iota(jnp.int32, out_ref.shape, 0)
+    out_ref[...] = jnp.where(place == index, 1.0, 0.0).astype(jnp.bfloat16)
+
+
+def pick_matrices(modes, nl, after):
     tables = np.stack(pair_tables(modes))
     block = tables.shape[1] // nl
     lanes = -(-block // 128) * 128
+    tables = tables.reshape(2, nl, block).transpose(1, 0, 2)
+    tables = np.pad(tables, ((0, 0), (0, 0), (0, lanes - block)), constant_values=-1).reshape(nl, 2 * lanes)
     wide = -(-(modes + 1) // 128) * 128
-    index = lax.dynamic_slice_in_dim(jnp.asarray(tables), lax.axis_index("learn") * block, block, axis=1)
-    index = jnp.pad(index, ((0, 0), (0, lanes - block)), constant_values=-1).reshape(1, 2 * lanes)
-    picks = (lax.broadcasted_iota(jnp.int32, (wide, 2 * lanes), 0) == index).astype(jnp.bfloat16)
+    return block, pl.pallas_call(
+        picks_kernel,
+        out_shape=pltpu.VMEM((wide, 2 * lanes), jnp.bfloat16),
+        in_specs=[VMEM, pl.BlockSpec(memory_space=pl.ANY)],
+        out_specs=VMEM,
+        compiler_params=pltpu.CompilerParams(vmem_limit_bytes=4 * MIB),
+        name="pick_matrices",
+    )(jnp.asarray(tables), after)
+
+
+def infer(shares, gram_old, picks, block):
+    count, steps, modes = shares.shape
     reduced, pod_gram, rhs = pl.pallas_call(
         infer_kernel,
         out_shape=(
@@ -425,7 +444,7 @@
     steps = min(cx, cy) // 2
     rounds = STEPS // steps
     x_even, x_odd, y_even, y_odd, y_far = swaps(ns, nl)
-    state = to_columns(fields)
+    state, factors = to_columns(fields, diffusivity, stoich)
     (basis,) = in_vmem(basis.reshape(basis.shape[0], nf, cx * cy, nz))
     share = None
     for n in range(rounds):
@@ -441,10 +460,11 @@
         ca = lax.ppermute(to_a, BOTH, y_even)
         cb = lax.ppermute(to_b, BOTH, y_far)
         bricks = (state, xa, xb, ya, yb)
-        state, snaps = advance(bricks, (ca, cb), diffusivity, stoich, cx, cy, nf, steps, n == rounds - 1)
+        state, snaps = advance(bricks, (ca, cb), factors, cx, cy, nf, steps, n == rounds - 1)
     sent = project(basis, snaps, cx, cy, steps, share, ns * nl)
     shares = lax.all_to_all(sent, BOTH, 0, 0)
-    reduced, pod_gram, rhs_block = infer(shares, gram_old, nl)
+    block, picks = pick_matrices(gram_old.shape[0], nl, sent)
+    reduced, pod_gram, rhs_block = infer(shares, gram_old, picks, block)
     return (state.reshape(fields.shape), reduced, pod_gram, rhs_block)
 
 

time: 82.3 us -> 78.2 us (0.950)
  local copies, waits for them, and re-layouts: 12.2 us -> 7.54 us
  starting transfers between devices: 19.7 us -> 22.8 us
  Pallas kernels: 22.7 us -> 21.5 us
  waiting for transfers between devices: 26.5 us -> 25.3 us
    unnamed x16 -> x15, local copies, waits for them, and re-layouts: 11.4 us -> 7.54 us
    ppermute x2, starting transfers between devices: 6.25 us -> 8.73 us  [body(): xa = lax.ppermute(state, BOTH, x_even)]
    pallas_call x2, Pallas kernels: 12.2 us -> 10.4 us  [advance(): pl.pallas_call(functools.partial(round_kernel, cx, cy, nf, steps, last),...]
    ppermute x2, waiting for transfers between devices: 11.2 us -> 9.89 us  [body(): xa = lax.ppermute(state, BOTH, x_even)]
    ppermute x2, starting transfers between devices: 1.01 us -> 2.08 us  [body(): ya = lax.ppermute(state, BOTH, y_even)]
    ppermute x2, starting transfers between devices: 1.57 us -> 0.5 us  [body(): yb = lax.ppermute(state, BOTH, y_odd)]
    ppermute x2, waiting for transfers between devices: 7.15 us -> 7.98 us  [body(): cb = lax.ppermute(to_b, BOTH, y_far)]
  transfers between devices with their start and end apart: 13 -> 13, of which waited for: 5 -> 5; matrix products, arithmetic and copies ran while one was open for 1% -> 1% of each run, Pallas kernels for 5% -> 6%
where the time goes in v3:
time: 78.2 us; the launch traced here: 77.9 us
  waiting for transfers between devices  25.3 us (32%)
  starting transfers between devices  22.8 us (29%)
  Pallas kernels  21.5 us (27%)
  local copies, waits for them, and re-layouts  7.54 us (10%)
    pallas_call x2, Pallas kernels, advance(): pl.pallas_call(functools.partial(round_kernel, cx, cy, nf, steps, last),...  10.4 us
    ppermute x2, waiting for transfers between devices, body(): xa = lax.ppermute(state, BOTH, x_even)  9.89 us
    pallas_call x2, Pallas kernels, project(): pl.pallas_call(functools.partial(project_kernel, cx, cy, steps, copies),...  8.95 us
    ppermute x2, starting transfers between devices, body(): xa = lax.ppermute(state, BOTH, x_even)  8.73 us
    ppermute x2, waiting for transfers between devices, body(): cb = lax.ppermute(to_b, BOTH, y_far)  7.98 us
    unnamed x15, local copies, waits for them, and re-layouts  7.54 us
    all_to_all x1, waiting for transfers between devices, body(): shares = lax.all_to_all(sent, BOTH, 0, 0)  7.38 us
    all_to_all x1, starting transfers between devices, body(): shares = lax.all_to_all(sent, BOTH, 0, 0)  5.66 us
  transfers between devices with their start and end apart: 13, of which 5 were waited for; matrix products, arithmetic and copies ran while one was open for 1% of the time, Pallas kernels for 6%

profile of v3, /device:TPU:0, one launch (start us, length us, event | category | flops | bytes accessed | tf_op | source)
XLA Modules:
  0.0 77.9 jit_solution(16035417366414125904)
XLA Ops:
  0.6 0.0 copy-start.2
  0.6 0.9 %copy-done.2 = f32[8,8,8,128]{3,2,1,0:T(8,128)S(1)} copy-done((f32[8,8,8,128]{3,2,1,0:T(8,128)S(1)}, f32[8,8,8,128]{3,2,1,0:T(8,128)}, u32[]{:S(2)}) %copy-start.2) | copy-done | bytes 262168
  1.6 0.0 copy-start.5
  1.6 0.7 copy-done.5
  2.2 0.0 copy-start.6
  2.2 0.7 copy-done.6
  2.9 0.7 to_columns.1
  3.6 0.6 collective-permute-start.1
  4.2 4.0 %collective-permute-start = (f32[512,128]{1,0:T(8,128)S(1)}, f32[512,128]{1,0:T(8,128)S(1)}, u32[]{:S(2)}, u32[]{:S(2)}) collective-permute-start(f32[512,128]{1,0:T(8,128)S(1)} %get-tuple-element.20.own_ref), channel_id=1, source_target_pairs={{0,4},{1,5},{2,6},{3,7},{8,12},{9,13},{10,14},{11,15},{16,20},{17,... | collective-permute-start | bytes 786440 | tf_op jit(solution)/shard_map/ppermute | solution.py:453
  8.2 0.4 collective-permute-start.3
  8.6 1.2 %collective-permute-start.2 = (f32[512,128]{1,0:T(8,128)S(1)}, f32[512,128]{1,0:T(8,128)S(1)}, u32[]{:S(2)}, u32[]{:S(2)}) collective-permute-start(f32[512,128]{1,0:T(8,128)S(1)} %get-tuple-element.20.own_ref), channel_id=1, source_target_pairs={{0,1},{2,3},{4,5},{6,7},{8,9},{10,11},{12,13},{14,15},{16,17},{18,... | collective-permute-start | bytes 786440 | tf_op jit(solution)/shard_map/ppermute | solution.py:451
  9.8 0.0 collective-permute-done.1.xb_ref
  9.8 8.9 %collective-permute-done.xa_ref = f32[512,128]{1,0:T(8,128)S(1)} collective-permute-done((f32[512,128]{1,0:T(8,128)S(1)}, f32[512,128]{1,0:T(8,128)S(1)}, u32[]{:S(2)}, u32[]{:S(2)}) %collective-permute-start) | collective-permute-done | bytes 262176 | tf_op jit(solution)/shard_map/ppermute | solution.py:453
  18.8 0.1 collective-permute-start.4
  18.8 2.5 %collective-permute-start.5 = (f32[448,128]{1,0:T(8,128)S(1)}, f32[448,128]{1,0:T(8,128)S(1)}, u32[]{:S(2)}, u32[]{:S(2)}) collective-permute-start(f32[448,128]{1,0:T(8,128)S(1)} %get-tuple-element.22), channel_id=1, source_target_pairs={{1,2},{5,6},{9,10},{13,14},{17,18},{21,22},{25,26},{29,30},{0,4},{... | collective-permute-start | bytes 688136 | tf_op jit(solution)/shard_map/ppermute | solution.py:461
  21.4 0.0 collective-permute-done.3.yb_ref
  21.4 0.0 collective-permute-done.2.ya_ref
  21.4 0.0 collective-permute-done.4.ca_ref
  21.4 4.0 %collective-permute-done.5.cb_ref = f32[448,128]{1,0:T(8,128)S(1)} collective-permute-done((f32[448,128]{1,0:T(8,128)S(1)}, f32[448,128]{1,0:T(8,128)S(1)}, u32[]{:S(2)}, u32[]{:S(2)}) %collective-permute-start.5) | collective-permute-done | bytes 229408 | tf_op jit(solution)/shard_map/ppermute | solution.py:461
  25.4 5.1 %advance.2 = (f32[512,128]{1,0:T(8,128)S(1)}, f32[64,32,128]{2,1,0:T(8,128)S(1)}) custom-call(f32[512,128]{1,0:T(8,128)S(1)} %get-tuple-element.20.own_ref, f32[512,128]{1,0:T(8,128)S(1)} %collective-permute-done.xa_ref, f32[512,128]{1,0:T(8,128)S(1)} %collective-permute-done.1.xb_ref, f32[512,128]{1,0:T(8,128)S(1)} %collective-permute-done.2.ya_ref, ...), custom_call_target="tpu_custom_call" | custom-call | tf_op jit(solution)/shard_map/advance/pallas_call | solution.py:268
  30.5 0.1 collective-permute-start.7
  30.6 4.7 %collective-permute-start.6 = (f32[512,128]{1,0:T(8,128)S(1)}, f32[512,128]{1,0:T(8,128)S(1)}, u32[]{:S(2)}, u32[]{:S(2)}) collective-permute-start(f32[512,128]{1,0:T(8,128)S(1)} %get-tuple-element.24.own_ref), channel_id=1, source_target_pairs={{0,4},{1,5},{2,6},{3,7},{8,12},{9,13},{10,14},{11,15},{16,20},{17,... | collective-permute-start | bytes 786440 | tf_op jit(solution)/shard_map/ppermute | solution.py:453
  35.3 0.1 collective-permute-start.9
  35.4 0.8 %collective-permute-start.8 = (f32[512,128]{1,0:T(8,128)S(1)}, f32[512,128]{1,0:T(8,128)S(1)}, u32[]{:S(2)}, u32[]{:S(2)}) collective-permute-start(f32[512,128]{1,0:T(8,128)S(1)} %get-tuple-element.24.own_ref), channel_id=1, source_target_pairs={{0,1},{2,3},{4,5},{6,7},{8,9},{10,11},{12,13},{14,15},{16,17},{18,... | collective-permute-start | bytes 786440 | tf_op jit(solution)/shard_map/ppermute | solution.py:451
  36.2 0.0 copy-start
  36.2 4.6 %copy-done = bf16[96,8,8,8,128]{4,3,2,1,0:T(8,128)(2,1)S(1)} copy-done((bf16[96,8,8,8,128]{4,3,2,1,0:T(8,128)(2,1)S(1)}, bf16[96,8,8,8,128]{4,3,2,1,0:T(8,128)(2,1)}, u32[]{:S(2)}) %copy-start) | copy-done | bytes 12582936
  40.8 0.0 copy-start.1
  40.8 0.0 copy-start.4
  40.8 0.0 copy-start.3
  40.8 4.1 %project.2.refs_0_ = f32[4,96]{1,0:T(4,128)S(1)} custom-call(bf16[96,8,64,128]{3,2,1,0:T(8,128)(2,1)S(1)} %bitcast.6, f32[64,32,128]{2,1,0:T(8,128)S(1)} %get-tuple-element.25.snap_ref), custom_call_target="tpu_custom_call" | custom-call | tf_op jit(solution)/shard_map/project/pallas_call | solution.py:352
  45.0 0.0 collective-permute-done.7.xb_ref
  45.0 1.0 %collective-permute-done.6.xa_ref = f32[512,128]{1,0:T(8,128)S(1)} collective-permute-done((f32[512,128]{1,0:T(8,128)S(1)}, f32[512,128]{1,0:T(8,128)S(1)}, u32[]{:S(2)}, u32[]{:S(2)}) %collective-permute-start.6) | collective-permute-done | bytes 262176 | tf_op jit(solution)/shard_map/ppermute | solution.py:453
  46.0 0.1 collective-permute-start.10
  46.1 2.5 %collective-permute-start.11 = (f32[448,128]{1,0:T(8,128)S(1)}, f32[448,128]{1,0:T(8,128)S(1)}, u32[]{:S(2)}, u32[]{:S(2)}) collective-permute-start(f32[448,128]{1,0:T(8,128)S(1)} %get-tuple-element.29), channel_id=1, source_target_pairs={{1,2},{5,6},{9,10},{13,14},{17,18},{21,22},{25,26},{29,30},{0,4},{... | collective-permute-start | bytes 688136 | tf_op jit(solution)/shard_map/ppermute | solution.py:461
  48.6 0.0 collective-permute-done.9.yb_ref
  48.6 0.0 collective-permute-done.8.ya_ref
  48.6 0.0 collective-permute-done.10.ca_ref
  48.6 4.0 %collective-permute-done.11.cb_ref = f32[448,128]{1,0:T(8,128)S(1)} collective-permute-done((f32[448,128]{1,0:T(8,128)S(1)}, f32[448,128]{1,0:T(8,128)S(1)}, u32[]{:S(2)}, u32[]{:S(2)}) %collective-permute-start.11) | collective-permute-done | bytes 229408 | tf_op jit(solution)/shard_map/ppermute | solution.py:461
  52.6 5.3 %advance.3 = (f32[512,128]{1,0:T(8,128)S(1)}, f32[64,32,128]{2,1,0:T(8,128)S(1)}) custom-call(f32[512,128]{1,0:T(8,128)S(1)} %get-tuple-element.24.own_ref, f32[512,128]{1,0:T(8,128)S(1)} %collective-permute-done.6.xa_ref, f32[512,128]{1,0:T(8,128)S(1)} %collective-permute-done.7.xb_ref, f32[512,128]{1,0:T(8,128)S(1)} %collective-permute-done.8.ya_ref, ...), custom_call_target="tpu_custom_call" | custom-call | tf_op jit(solution)/shard_map/advance/pallas_call | solution.py:268
  57.9 0.0 copy-done.1
  57.9 4.8 %project.3.after_ref = f32[32,8,96]{2,1,0:T(8,128)} custom-call(bf16[96,8,64,128]{3,2,1,0:T(8,128)(2,1)S(1)} %bitcast.7, f32[64,32,128]{2,1,0:T(8,128)S(1)} %get-tuple-element.31.snap_ref, f32[4,96]{1,0:T(4,128)S(1)} %project.2.refs_0_), custom_call_target="tpu_custom_call" | custom-call | tf_op jit(solution)/shard_map/project/pallas_call | solution.py:352
  62.7 5.7 %all-to-all-start = ((f32[32,8,96]{2,1,0:T(8,128)}), f32[32,8,96]{2,1,0:T(8,128)S(1)}, u32[]{:S(2)}, u32[]{:S(2)}) async-start(f32[32,8,96]{2,1,0:T(8,128)} %project.3.after_ref), calls=%async_computation | async-start | bytes 262144 | tf_op jit(solution)/shard_map/all_to_all | solution.py:465
  68.4 0.7 copy.10
  69.1 0.0 copy-done.4
  69.1 0.1 pick_matrices.1.picks_ref
  69.2 7.4 %all-to-all-done.shares_ref = f32[32,8,96]{2,1,0:T(8,128)S(1)} async-done(((f32[32,8,96]{2,1,0:T(8,128)}), f32[32,8,96]{2,1,0:T(8,128)S(1)}, u32[]{:S(2)}, u32[]{:S(2)}) %all-to-all-start) | async-done | bytes 98336 | tf_op jit(solution)/shard_map/all_to_all | solution.py:465
  76.6 0.0 copy-done.3
  76.6 1.3 %infer.1 = (f32[8,96]{1,0:T(8,128)}, f32[96,96]{1,0:T(8,128)}, f32[96,1188]{1,0:T(8,128)}) custom-call(f32[32,8,96]{2,1,0:T(8,128)S(1)} %all-to-all-done.shares_ref, f32[96,96]{1,0:T(8,128)S(1)} %copy-done.3, bf16[128,2560]{1,0:T(8,128)(2,1)S(1)} %pick_matrices.1.picks_ref), custom_call_target="tpu_custom_call" | custom-call | tf_op jit(solution)/shard_map/infer/pallas_call | solution.py:426
  (2 shorter events, 0.1 us)
Async XLA Ops:
  0.6 1.0 %copy-start.2 = (f32[8,8,8,128]{3,2,1,0:T(8,128)S(1)}, f32[8,8,8,128]{3,2,1,0:T(8,128)}, u32[]{:S(2)}) copy-start(f32[8,8,8,128]{3,2,1,0:T(8,128)} %param.6) | copy-start | bytes 786436
  1.6 0.7 copy-start.5
  2.2 0.7 copy-start.6
  3.6 6.2 %collective-permute-start.1 = (f32[512,128]{1,0:T(8,128)S(1)}, f32[512,128]{1,0:T(8,128)S(1)}, u32[]{:S(2)}, u32[]{:S(2)}) collective-permute-start(f32[512,128]{1,0:T(8,128)S(1)} %get-tuple-element.20.own_ref), channel_id=1, source_target_pairs={{4,8},{5,9},{6,10},{7,11},{12,16},{13,17},{14,18},{15,19},{20,24},... | collective-permute-start | bytes 786440 | tf_op jit(solution)/shard_map/ppermute | solution.py:454
  4.2 14.6 %collective-permute-start = (f32[512,128]{1,0:T(8,128)S(1)}, f32[512,128]{1,0:T(8,128)S(1)}, u32[]{:S(2)}, u32[]{:S(2)}) collective-permute-start(f32[512,128]{1,0:T(8,128)S(1)} %get-tuple-element.20.own_ref), channel_id=1, source_target_pairs={{0,4},{1,5},{2,6},{3,7},{8,12},{9,13},{10,14},{11,15},{16,20},{17,... | collective-permute-start | bytes 786440 | tf_op jit(solution)/shard_map/ppermute | solution.py:453
  8.2 13.2 %collective-permute-start.3 = (f32[512,128]{1,0:T(8,128)S(1)}, f32[512,128]{1,0:T(8,128)S(1)}, u32[]{:S(2)}, u32[]{:S(2)}) collective-permute-start(f32[512,128]{1,0:T(8,128)S(1)} %get-tuple-element.20.own_ref), channel_id=1, source_target_pairs={{1,2},{5,6},{9,10},{13,14},{17,18},{21,22},{25,26},{29,30},{0,3},{... | collective-permute-start | bytes 786440 | tf_op jit(solution)/shard_map/ppermute | solution.py:452
  8.6 12.8 %collective-permute-start.2 = (f32[512,128]{1,0:T(8,128)S(1)}, f32[512,128]{1,0:T(8,128)S(1)}, u32[]{:S(2)}, u32[]{:S(2)}) collective-permute-start(f32[512,128]{1,0:T(8,128)S(1)} %get-tuple-element.20.own_ref), channel_id=1, source_target_pairs={{0,1},{2,3},{4,5},{6,7},{8,9},{10,11},{12,13},{14,15},{16,17},{18,... | collective-permute-start | bytes 786440 | tf_op jit(solution)/shard_map/ppermute | solution.py:451
  18.8 2.6 %collective-permute-start.4 = (f32[448,128]{1,0:T(8,128)S(1)}, f32[448,128]{1,0:T(8,128)S(1)}, u32[]{:S(2)}, u32[]{:S(2)}) collective-permute-start(f32[448,128]{1,0:T(8,128)S(1)} %get-tuple-element.21), channel_id=1, source_target_pairs={{0,1},{2,3},{4,5},{6,7},{8,9},{10,11},{12,13},{14,15},{16,17},{18,... | collective-permute-start | bytes 688136 | tf_op jit(solution)/shard_map/ppermute | solution.py:460
  18.8 6.5 %collective-permute-start.5 = (f32[448,128]{1,0:T(8,128)S(1)}, f32[448,128]{1,0:T(8,128)S(1)}, u32[]{:S(2)}, u32[]{:S(2)}) collective-permute-start(f32[448,128]{1,0:T(8,128)S(1)} %get-tuple-element.22), channel_id=1, source_target_pairs={{1,2},{5,6},{9,10},{13,14},{17,18},{21,22},{25,26},{29,30},{0,4},{... | collective-permute-start | bytes 688136 | tf_op jit(solution)/shard_map/ppermute | solution.py:461
  30.5 14.5 %collective-permute-start.7 = (f32[512,128]{1,0:T(8,128)S(1)}, f32[512,128]{1,0:T(8,128)S(1)}, u32[]{:S(2)}, u32[]{:S(2)}) collective-permute-start(f32[512,128]{1,0:T(8,128)S(1)} %get-tuple-element.24.own_ref), channel_id=1, source_target_pairs={{4,8},{5,9},{6,10},{7,11},{12,16},{13,17},{14,18},{15,19},{20,24},... | collective-permute-start | bytes 786440 | tf_op jit(solution)/shard_map/ppermute | solution.py:454
  30.6 15.4 %collective-permute-start.6 = (f32[512,128]{1,0:T(8,128)S(1)}, f32[512,128]{1,0:T(8,128)S(1)}, u32[]{:S(2)}, u32[]{:S(2)}) collective-permute-start(f32[512,128]{1,0:T(8,128)S(1)} %get-tuple-element.24.own_ref), channel_id=1, source_target_pairs={{0,4},{1,5},{2,6},{3,7},{8,12},{9,13},{10,14},{11,15},{16,20},{17,... | collective-permute-start | bytes 786440 | tf_op jit(solution)/shard_map/ppermute | solution.py:453
  35.3 13.4 %collective-permute-start.9 = (f32[512,128]{1,0:T(8,128)S(1)}, f32[512,128]{1,0:T(8,128)S(1)}, u32[]{:S(2)}, u32[]{:S(2)}) collective-permute-start(f32[512,128]{1,0:T(8,128)S(1)} %get-tuple-element.24.own_ref), channel_id=1, source_target_pairs={{1,2},{5,6},{9,10},{13,14},{17,18},{21,22},{25,26},{29,30},{0,3},{... | collective-permute-start | bytes 786440 | tf_op jit(solution)/shard_map/ppermute | solution.py:452
  35.4 13.3 %collective-permute-start.8 = (f32[512,128]{1,0:T(8,128)S(1)}, f32[512,128]{1,0:T(8,128)S(1)}, u32[]{:S(2)}, u32[]{:S(2)}) collective-permute-start(f32[512,128]{1,0:T(8,128)S(1)} %get-tuple-element.24.own_ref), channel_id=1, source_target_pairs={{0,1},{2,3},{4,5},{6,7},{8,9},{10,11},{12,13},{14,15},{16,17},{18,... | collective-permute-start | bytes 786440 | tf_op jit(solution)/shard_map/ppermute | solution.py:451
  36.2 4.6 %copy-start = (bf16[96,8,8,8,128]{4,3,2,1,0:T(8,128)(2,1)S(1)}, bf16[96,8,8,8,128]{4,3,2,1,0:T(8,128)(2,1)}, u32[]{:S(2)}) copy-start(bf16[96,8,8,8,128]{4,3,2,1,0:T(8,128)(2,1)} %param.9) | copy-start | bytes 37748740
  40.8 17.1 %copy-start.1 = (bf16[96,8,8,8,128]{4,3,2,1,0:T(8,128)(2,1)S(1)}, bf16[96,8,8,8,128]{4,3,2,1,0:T(8,128)(2,1)}, u32[]{:S(2)}) copy-start(bf16[96,8,8,8,128]{4,3,2,1,0:T(8,128)(2,1)} %param.9) | copy-start | bytes 37748740
  40.8 28.3 %copy-start.4 = (s32[4,2560]{1,0:T(4,128)S(1)}, s32[4,2560]{1,0:T(4,128)}, u32[]{:S(2)}) copy-start(s32[4,2560]{1,0:T(4,128)} %constant.2.clone.tables_ref) | copy-start | bytes 122884
  40.8 35.8 %copy-start.3 = (f32[96,96]{1,0:T(8,128)S(1)}, f32[96,96]{1,0:T(8,128)}, u32[]{:S(2)}) copy-start(f32[96,96]{1,0:T(8,128)} %gram_ref.1) | copy-start | bytes 110596
  46.0 2.6 %collective-permute-start.10 = (f32[448,128]{1,0:T(8,128)S(1)}, f32[448,128]{1,0:T(8,128)S(1)}, u32[]{:S(2)}, u32[]{:S(2)}) collective-permute-start(f32[448,128]{1,0:T(8,128)S(1)} %get-tuple-element.28), channel_id=1, source_target_pairs={{0,1},{2,3},{4,5},{6,7},{8,9},{10,11},{12,13},{14,15},{16,17},{18,... | collective-permute-start | bytes 688136 | tf_op jit(solution)/shard_map/ppermute | solution.py:460
  46.1 6.5 %collective-permute-start.11 = (f32[448,128]{1,0:T(8,128)S(1)}, f32[448,128]{1,0:T(8,128)S(1)}, u32[]{:S(2)}, u32[]{:S(2)}) collective-permute-start(f32[448,128]{1,0:T(8,128)S(1)} %get-tuple-element.29), channel_id=1, source_target_pairs={{1,2},{5,6},{9,10},{13,14},{17,18},{21,22},{25,26},{29,30},{0,4},{... | collective-permute-start | bytes 688136 | tf_op jit(solution)/shard_map/ppermute | solution.py:461
  62.7 13.9 %all-to-all-start = ((f32[32,8,96]{2,1,0:T(8,128)}), f32[32,8,96]{2,1,0:T(8,128)S(1)}, u32[]{:S(2)}, u32[]{:S(2)}) async-start(f32[32,8,96]{2,1,0:T(8,128)} %project.3.after_ref), calls=%async_computation | async-start | bytes 262144 | tf_op jit(solution)/shard_map/all_to_all | solution.py:465

commit v4 on v3

--- a/solution.py
+++ b/solution.py
@@ -33,9 +33,9 @@
     x_odd += [(s * nl + l, s * nl + l + 1) for s in (0, ns - 1) for l in range(0, nl, 2)]
     y_even = both_ways([(s * nl + l, s * nl + l + 1) for s in range(ns) for l in range(0, nl, 2)])
     y_odd = [(s * nl + l, s * nl + l + 1) for s in range(ns) for l in range(1, nl - 1, 2)]
-    y_far = y_odd + [(s * nl + l, (s + 1) * nl + l) for s in range(0, ns, 2) for l in (0, nl - 1)]
-    y_odd = y_odd + [(s * nl, s * nl + nl - 1) for s in range(ns)]
-    return x_even, both_ways(x_odd), y_even, both_ways(y_odd), both_ways(y_far)
+    far = 2 if ns % 4 == 0 else 1
+    y_odd += [(s * nl + l, (s + far) * nl + l) for s in range(ns) if s // far % 2 == 0 for l in (0, nl - 1)]
+    return x_even, both_ways(x_odd), y_even, both_ways(y_odd)
 
 
 def in_vmem(*arrays):
@@ -50,75 +50,128 @@
     return runs, first
 
 
-def each_case(first, second, body):
-    for a in (True, False):
-        for b in (True, False):
-
-            @pl.when(jnp.logical_and(first == a, second == b))
-            def _(a=a, b=b):
-                body(a, b)
-
-
-def columns_kernel(cx, cy, dif_ref, sto_ref, native_ref, out_ref, factors_ref):
+def x_runs(reach, cy):
+    parts, sizes = ([], []), [0, 0]
+    for d in range(1, reach + 1):
+        count = min(reach - d, cy)
+        if 2 * count >= cy:
+            cuts = ((0, 0, cy),)
+        else:
+            cuts = ((0, 0, count), (1, count, cy - count), (0, cy - count, cy))
+        for part, low, high in cuts:
+            if high > low:
+                parts[part].append((d, low, high - low, sizes[part]))
+                sizes[part] += high - low
+    return parts, sizes
+
+
+def in_first_part(reach, cy, d, y):
+    for e, low, count, first in x_runs(reach, cy)[0][0]:
+        if e == d and low <= y < low + count:
+            return first + y - low
+    raise ValueError((d, y))
+
+
+def each_case(cond, body):
+    pl.when(cond)(lambda: body(True))
+    pl.when(jnp.logical_not(cond))(lambda: body(False))
+
+
+def cut_bricks(cx, cy, nf, load, a1_ref, b1_ref, a2_ref, b2_ref):
+    parts, _ = x_runs(cx, cy)
+
+    def cut(s_is_even):
+        for part, a_ref, b_ref in ((0, a1_ref, b1_ref), (1, a2_ref, b2_ref)):
+            for out_ref, is_east in ((a_ref, s_is_even), (b_ref, not s_is_even)):
+                for d, y, count, first in parts[part]:
+                    out_ref[pl.ds(first * nf, count * nf), :] = load(cx - d if is_east else d - 1, y, count)
+
+    each_case(lax.rem(lax.axis_index("sim"), 2) == 0, cut)
+
+
+def cut_shapes(cx, cy, nf, nz):
+    sizes = x_runs(cx, cy)[1]
+    return [pltpu.VMEM((size * nf, nz), jnp.float32) for size in (sizes[0], sizes[0], sizes[1], sizes[1])]
+
+
+def columns_kernel(cx, cy, native_ref, out_ref, *cut_refs):
     nf = native_ref.shape[0] // (cx * cy)
-    field = lax.broadcasted_iota(jnp.int32, (nf, native_ref.shape[1]), 0)
-    for n, ref in enumerate((dif_ref, sto_ref)):
-        value = jnp.zeros(field.shape, jnp.float32)
-        for f in range(nf):
-            value = jnp.where(field == f, ref[f], value)
-        factors_ref[n] = value
     for c in range(cx * cy):
         out_ref[pl.ds(c * nf, nf), :] = native_ref[pl.ds(c, nf, stride=cx * cy), :]
-
-
-def to_columns(fields, diffusivity, stoich):
+    cut_bricks(cx, cy, nf, lambda x, y, n: out_ref[pl.ds((x * cy + y) * nf, n * nf), :], *cut_refs)
+
+
+def to_columns(fields):
     nf, cx, cy, nz = fields.shape
     return pl.pallas_call(
         functools.partial(columns_kernel, cx, cy),
-        out_shape=(pltpu.VMEM((cx * cy * nf, nz), jnp.float32), pltpu.VMEM((2, nf, nz), jnp.float32)),
-        in_specs=[SMEM, SMEM, VMEM],
-        out_specs=(VMEM, VMEM),
+        out_shape=[pltpu.VMEM((cx * cy * nf, nz), jnp.float32), *cut_shapes(cx, cy, nf, nz)],
+        in_specs=[VMEM],
+        out_specs=[VMEM] * 5,
         compiler_params=pltpu.CompilerParams(vmem_limit_bytes=2 * MIB),
         name="to_columns",
-    )(diffusivity, stoich, fields.reshape(nf * cx * cy, nz))
-
-
-def pack_kernel(cx, cy, nf, xa_ref, xb_ref, to_a_ref, to_b_ref):
-    runs, size = corner_runs(min(cx, cy))
-    even_s = lax.rem(lax.axis_index("sim"), 2) == 0
-    even_l = lax.rem(lax.axis_index("learn"), 2) == 0
-
-    def copy(s_is_even, l_is_even):
-        for side, brick in enumerate((xa_ref, xb_ref)):
-            is_east = s_is_even == (side == 0)
-            for out_ref, north in ((to_a_ref, l_is_even), (to_b_ref, not l_is_even)):
+    )(*in_vmem(fields.reshape(nf * cx * cy, nz)))
+
+
+def factors_kernel(dif_ref, sto_ref, after_ref, out_ref):
+    del after_ref
+    _, nf, nz = out_ref.shape
+    field = lax.broadcasted_iota(jnp.int32, (nf, nz), 0)
+    for n, ref in enumerate((dif_ref, sto_ref)):
+        value = jnp.zeros((nf, nz), jnp.float32)
+        for f in range(nf):
+            value = jnp.where(field == f, ref[f], value)
+        out_ref[n] = value
+
+
+def field_factors(diffusivity, stoich, nz, after):
+    return pl.pallas_call(
+        factors_kernel,
+        out_shape=pltpu.VMEM((2, diffusivity.shape[0], nz), jnp.float32),
+        in_specs=[SMEM, SMEM, pl.BlockSpec(memory_space=pl.ANY)],
+        out_specs=VMEM,
+        compiler_params=pltpu.CompilerParams(vmem_limit_bytes=MIB),
+        name="field_factors",
+    )(diffusivity, stoich, after)
+
+
+def pack_kernel(cx, cy, nf, own_ref, xa_ref, xb_ref, to_a_ref, to_b_ref):
+    runs, size = corner_runs(cx)
+
+    def copy(l_is_even):
+        for out_ref, north in ((to_a_ref, l_is_even), (to_b_ref, not l_is_even)):
+            for side, brick in enumerate((xa_ref, xb_ref)):
                 for d, count, first in runs:
-                    x = d - 1 if is_east else cx - d
-                    y = cy - count if north else 0
-                    rows = brick[pl.ds((x * cy + y) * nf, count * nf), :]
+                    row = in_first_part(cx, cy, d, cy - count if north else 0)
+                    rows = brick[pl.ds(row * nf, count * nf), :]
                     out_ref[pl.ds((side * size + first) * nf, count * nf), :] = rows
 
-    each_case(even_s, even_l, copy)
-
-
-def pack_corners(xa, xb, cx, cy, nf):
-    nz = xa.shape[1]
-    size = 2 * corner_runs(min(cx, cy))[1]
+    each_case(lax.rem(lax.axis_index("learn"), 2) == 0, copy)
+    for x in range(cx):
+        rows = own_ref[pl.ds(x * cy * nf, cy * nf), :]
+        for out_ref in (to_a_ref, to_b_ref):
+            out_ref[pl.ds((2 * size + x * cy) * nf, cy * nf), :] = rows
+
+
+def pack_for_y(own, xa, xb, cx, cy, nf):
+    nz = own.shape[1]
+    size = 2 * corner_runs(cx)[1] + cx * cy
     shape = pltpu.VMEM((size * nf, nz), jnp.float32)
     return pl.pallas_call(
         functools.partial(pack_kernel, cx, cy, nf),
         out_shape=(shape, shape),
-        in_specs=[VMEM, VMEM],
+        in_specs=[VMEM] * 3,
         out_specs=(VMEM, VMEM),
         compiler_params=pltpu.CompilerParams(vmem_limit_bytes=MIB),
-        name="pack_corners",
-    )(*in_vmem(xa, xb))
+        name="pack_for_y",
+    )(*in_vmem(own, xa, xb))
 
 
 def round_kernel(
-    cx, cy, nf, steps, last, own_ref, xa_ref, xb_ref, ya_ref, yb_ref, ca_ref, cb_ref, factors_ref,
-    state_ref, snap_ref, u_ref, m_ref, rate_ref,
+    cx, cy, nf, steps, last, own_ref, a1_ref, b1_ref, a2_ref, b2_ref, ya_ref, yb_ref, factors_ref,
+    state_ref, snap_ref, *refs,
 ):
+    cut_refs, (u_ref, m_ref, rate_ref) = refs[:-3], refs[-3:]
     nz = own_ref.shape[1]
     reach = 2 * steps
     wide_x, wide_y = cx + 2 * reach, cy + 2 * reach
@@ -128,9 +181,13 @@
     has_west, has_east = s > 0, s < ns - 1
     has_south, has_north = l > 0, l < nl - 1
 
-    def place(ref, x0, y0):
+    def place(ref, row, x0, y0):
         for i in range(cx):
-            u_ref[pl.ds(((x0 + i) * wide_y + y0) * nf, cy * nf), :] = ref[pl.ds(i * cy * nf, cy * nf), :]
+            rows = ref[pl.ds((row + i * cy) * nf, cy * nf), :]
+            u_ref[pl.ds(((x0 + i) * wide_y + y0) * nf, cy * nf), :] = rows
+
+    def halo_x(is_east, d):
+        return reach + cx + d - 1 if is_east else reach - d
 
     def clear(x0, x1, y0, y1):
         zeros = jnp.zeros(((y1 - y0) * nf, nz), jnp.float32)
@@ -142,31 +199,39 @@
 
         lax.fori_loop(x0, x1, trip, 0)
 
-    place(own_ref, reach, reach)
-    runs, size = corner_runs(reach)
-
-    def receive(s_is_even, l_is_even):
-        for side, brick in enumerate((xa_ref, xb_ref)):
-            is_east = s_is_even == (side == 0)
+    place(own_ref, 0, reach, reach)
+    corners, size = corner_runs(reach)
+    parts, _ = x_runs(reach, cy)
+
+    def receive_x(s_is_even):
+        for first_ref, rest_ref, is_east in ((a1_ref, a2_ref, s_is_even), (b1_ref, b2_ref, not s_is_even)):
 
             @pl.when(has_east if is_east else has_west)
-            def _(brick=brick, is_east=is_east):
-                place(brick, reach + cx if is_east else 0, reach)
-
-        for corner, brick, north in ((ca_ref, ya_ref, l_is_even), (cb_ref, yb_ref, not l_is_even)):
+            def _(first_ref=first_ref, rest_ref=rest_ref, is_east=is_east):
+                for ref, runs in ((first_ref, parts[0]), (rest_ref, parts[1])):
+                    for d, y, count, first in runs:
+                        rows = ref[pl.ds(first * nf, count * nf), :]
+                        u_ref[pl.ds((halo_x(is_east, d) * wide_y + reach + y) * nf, count * nf), :] = rows
+
+    def receive_y(l_is_even):
+        for ref, north in ((ya_ref, l_is_even), (yb_ref, not l_is_even)):
 
             @pl.when(has_north if north else has_south)
-            def _(corner=corner, brick=brick, north=north):
-                place(brick, reach, reach + cy if north else 0)
-                for side in range(2):
-                    is_east = s_is_even == (side == 0)
-                    for d, count, first in runs:
-                        x = reach + cx + d - 1 if is_east else reach - d
-                        y = reach + cy if north else reach - count
-                        rows = corner[pl.ds((side * size + first) * nf, count * nf), :]
-                        u_ref[pl.ds((x * wide_y + y) * nf, count * nf), :] = rows
-
-    each_case(even_s, even_l, receive)
+            def _(ref=ref, north=north):
+                place(ref, 2 * size, reach, reach + cy if north else 0)
+
+                def receive_corners(s_is_even):
+                    for side in range(2):
+                        for d, count, first in corners:
+                            x = halo_x(s_is_even == (side == 0), d)
+                            y = reach + cy if north else reach - count
+                            rows = ref[pl.ds((side * size + first) * nf, count * nf), :]
+                            u_ref[pl.ds((x * wide_y + y) * nf, count * nf), :] = rows
+
+                each_case(even_s, receive_corners)
+
+    each_case(even_s, receive_x)
+    each_case(even_l, receive_y)
     pl.when(jnp.logical_not(has_west))(lambda: clear(0, reach, 0, wide_y))
     pl.when(jnp.logical_not(has_east))(lambda: clear(reach + cx, wide_x, 0, wide_y))
     pl.when(jnp.logical_not(has_south))(lambda: clear(0, wide_x, 0, reach))
@@ -259,20 +324,27 @@
             rows = u_ref[pl.ds(((reach + i) * wide_y + reach) * nf, cy * nf), :]
             state_ref[pl.ds(i * cy * nf, cy * nf), :] = rows
 
-
-def advance(bricks, corners, factors, cx, cy, nf, steps, last):
-    nz = bricks[0].shape[1]
+        def brick(x, y, count):
+            return u_ref[pl.ds(((reach + x) * wide_y + reach + y) * nf, count * nf), :]
+
+        cut_bricks(cx, cy, nf, brick, *cut_refs)
+
+
+def advance(operands, cx, cy, nf, steps, last):
+    nz = operands[0].shape[1]
     wide = (cx + 4 * steps) * (cy + 4 * steps)
     rows = max(cx, 2 * steps) * (cy + 4 * steps + nf)
     shape = (nf * cx * cy, nz)
+    cuts = [] if last else cut_shapes(cx, cy, nf, nz)
     return pl.pallas_call(
         functools.partial(round_kernel, cx, cy, nf, steps, last),
-        out_shape=(
+        out_shape=[
             pltpu.VMEM(shape, jnp.float32),
             pltpu.VMEM((nf * cx, steps * cy, nz), jnp.float32),
-        ),
+            *cuts,
+        ],
         in_specs=[VMEM] * 8,
-        out_specs=(VMEM, VMEM),
+        out_specs=[VMEM] * (2 + len(cuts)),
         scratch_shapes=[
             pltpu.VMEM((wide * nf, nz), jnp.float32),
             pltpu.VMEM((wide * nf, nz), jnp.float32),
@@ -280,7 +352,7 @@
         ],
         compiler_params=pltpu.CompilerParams(vmem_limit_bytes=8 * MIB),
         name="advance",
-    )(*in_vmem(*bricks, *corners, factors))
+    )(*in_vmem(*operands))
 
 
 def split(value):
@@ -443,24 +515,26 @@
     ns, nl = lax.axis_size("sim"), lax.axis_size("learn")
     steps = min(cx, cy) // 2
     rounds = STEPS // steps
-    x_even, x_odd, y_even, y_odd, y_far = swaps(ns, nl)
-    state, factors = to_columns(fields, diffusivity, stoich)
+    x_even, x_odd, y_even, y_odd = swaps(ns, nl)
+    state, *cuts = to_columns(fields)
+    factors = field_factors(diffusivity, stoich, nz, state)
     (basis,) = in_vmem(basis.reshape(basis.shape[0], nf, cx * cy, nz))
     share = None
     for n in range(rounds):
-        ya = lax.ppermute(state, BOTH, y_even)
-        yb = lax.ppermute(state, BOTH, y_odd)
-        xa = lax.ppermute(state, BOTH, x_even)
-        xb = lax.ppermute(state, BOTH, x_odd)
+        a1 = lax.ppermute(cuts[0], BOTH, x_even)
+        b1 = lax.ppermute(cuts[1], BOTH, x_odd)
         if n:
             part = project(basis, snaps, cx, cy, steps)
-            xa, xb, part = lax.optimization_barrier((xa, xb, part))
+            a1, b1, part = lax.optimization_barrier((a1, b1, part))
             share = part if share is None else jnp.concatenate([share, part], axis=0)
-        to_a, to_b = pack_corners(xa, xb, cx, cy, nf)
-        ca = lax.ppermute(to_a, BOTH, y_even)
-        cb = lax.ppermute(to_b, BOTH, y_far)
-        bricks = (state, xa, xb, ya, yb)
-        state, snaps = advance(bricks, (ca, cb), factors, cx, cy, nf, steps, n == rounds - 1)
+        to_a, to_b = pack_for_y(state, a1, b1, cx, cy, nf)
+        to_a, to_b, *rest = lax.optimization_barrier((to_a, to_b, *cuts[2:]))
+        ya = lax.ppermute(to_a, BOTH, y_even)
+        yb = lax.ppermute(to_b, BOTH, y_odd)
+        a2 = lax.ppermute(rest[0], BOTH, x_even)
+        b2 = lax.ppermute(rest[1], BOTH, x_odd)
+        operands = (state, a1, b1, a2, b2, ya, yb, factors)
+        state, snaps, *cuts = advance(operands, cx, cy, nf, steps, n == rounds - 1)
     sent = project(basis, snaps, cx, cy, steps, share, ns * nl)
     shares = lax.all_to_all(sent, BOTH, 0, 0)
     block, picks = pick_matrices(gram_old.shape[0], nl, sent)

time: 78.2 us -> 77.9 us (level)
  waiting for transfers between devices: 25.3 us -> 24.4 us
    all_to_all x1, starting transfers between devices: 5.66 us -> 7.26 us  [body(): shares = lax.all_to_all(sent, BOTH, 0, 0)]
    ppermute x12, starting transfers between devices: 17.2 us -> 16 us  [the longest x2 6.58 us: body(): a1 = lax.ppermute(cuts[0], BOTH, x_even)]
    ppermute x12, waiting for transfers between devices: 17.9 us -> 17.1 us  [the longest x2 7.67 us: body(): a1 = lax.ppermute(cuts[0], BOTH, x_even)]
  transfers between devices with their start and end apart: 13 -> 13, of which waited for: 5 -> 6; matrix products, arithmetic and copies ran while one was open for 1% -> 1% of each run, Pallas kernels for 6% -> 6%
where the time goes in v4:
time: 77.9 us; the launch traced here: 77.7 us
  waiting for transfers between devices  24.4 us (31%)
  starting transfers between devices  23.2 us (30%)
  Pallas kernels  21.7 us (28%)
  local copies, waits for them, and re-layouts  7.55 us (10%)
    pallas_call x2, Pallas kernels, advance(): pl.pallas_call(functools.partial(round_kernel, cx, cy, nf, steps, last),...  10.4 us
    pallas_call x2, Pallas kernels, project(): pl.pallas_call(functools.partial(project_kernel, cx, cy, steps, copies),...  8.95 us
    ppermute x2, waiting for transfers between devices, body(): a1 = lax.ppermute(cuts[0], BOTH, x_even)  7.67 us
    unnamed x15, local copies, waits for them, and re-layouts  7.55 us
    all_to_all x1, waiting for transfers between devices, body(): shares = lax.all_to_all(sent, BOTH, 0, 0)  7.38 us
    all_to_all x1, starting transfers between devices, body(): shares = lax.all_to_all(sent, BOTH, 0, 0)  7.26 us
    ppermute x2, starting transfers between devices, body(): a1 = lax.ppermute(cuts[0], BOTH, x_even)  6.58 us
    ppermute x2, waiting for transfers between devices, body(): yb = lax.ppermute(to_b, BOTH, y_odd)  5.89 us
  transfers between devices with their start and end apart: 13, of which 6 were waited for; matrix products, arithmetic and copies ran while one was open for 1% of the time, Pallas kernels for 6%

profile of v4, /device:TPU:0, one launch (start us, length us, event | category | flops | bytes accessed | tf_op | source)
XLA Modules:
  0.0 77.7 jit_solution(4580099921007207028)
XLA Ops:
  0.6 0.0 copy-start.2
  0.6 0.9 %copy-done.2 = f32[8,8,8,128]{3,2,1,0:T(8,128)S(1)} copy-done((f32[8,8,8,128]{3,2,1,0:T(8,128)S(1)}, f32[8,8,8,128]{3,2,1,0:T(8,128)}, u32[]{:S(2)}) %copy-start.2) | copy-done | bytes 262168
  1.6 0.2 to_columns.1
  1.8 3.0 %collective-permute-start = (f32[352,128]{1,0:T(8,128)S(1)}, f32[352,128]{1,0:T(8,128)S(1)}, u32[]{:S(2)}, u32[]{:S(2)}) collective-permute-start(f32[352,128]{1,0:T(8,128)S(1)} %get-tuple-element.36), channel_id=1, source_target_pairs={{0,4},{1,5},{2,6},{3,7},{8,12},{9,13},{10,14},{11,15},{16,20},{17,... | collective-permute-start | bytes 540680 | tf_op jit(solution)/shard_map/ppermute | solution.py:524
  4.8 0.0 collective-permute-start.1
  4.8 7.7 %collective-permute-done.xa_ref.a1_ref = f32[352,128]{1,0:T(8,128)S(1)} collective-permute-done((f32[352,128]{1,0:T(8,128)S(1)}, f32[352,128]{1,0:T(8,128)S(1)}, u32[]{:S(2)}, u32[]{:S(2)}) %collective-permute-start) | collective-permute-done | bytes 180256 | tf_op jit(solution)/shard_map/ppermute | solution.py:524
  12.5 0.0 collective-permute-done.1.xb_ref.b1_ref
  12.5 0.1 pack_for_y.2
  12.6 0.1 collective-permute-start.4
  12.6 2.6 %collective-permute-start.5 = (f32[960,128]{1,0:T(8,128)S(1)}, f32[960,128]{1,0:T(8,128)S(1)}, u32[]{:S(2)}, u32[]{:S(2)}) collective-permute-start(f32[960,128]{1,0:T(8,128)S(1)} %get-tuple-element.45), channel_id=1, source_target_pairs={{1,2},{5,6},{9,10},{13,14},{17,18},{21,22},{25,26},{29,30},{0,8},{... | collective-permute-start | bytes 1474568 | tf_op jit(solution)/shard_map/ppermute | solution.py:533
  15.3 1.5 %collective-permute-start.2 = (f32[160,128]{1,0:T(8,128)S(1)}, f32[160,128]{1,0:T(8,128)S(1)}, u32[]{:S(2)}, u32[]{:S(2)}) collective-permute-start(f32[160,128]{1,0:T(8,128)S(1)} %get-tuple-element.42), channel_id=1, source_target_pairs={{0,4},{1,5},{2,6},{3,7},{8,12},{9,13},{10,14},{11,15},{16,20},{17,... | collective-permute-start | bytes 245768 | tf_op jit(solution)/shard_map/ppermute | solution.py:534
  16.8 0.0 collective-permute-start.3
  16.8 0.0 copy-start.5
  16.8 0.7 copy-done.5
  17.4 0.0 copy-start.6
  17.4 0.7 copy-done.6
  18.1 0.6 field_factors.1.factors_ref
  18.6 1.1 %collective-permute-done.2.a2_ref = f32[160,128]{1,0:T(8,128)S(1)} collective-permute-done((f32[160,128]{1,0:T(8,128)S(1)}, f32[160,128]{1,0:T(8,128)S(1)}, u32[]{:S(2)}, u32[]{:S(2)}) %collective-permute-start.2) | collective-permute-done | bytes 81952 | tf_op jit(solution)/shard_map/ppermute | solution.py:534
  19.7 0.0 collective-permute-done.3.b2_ref
  19.7 0.0 collective-permute-done.4.ya_ref
  19.7 3.2 %collective-permute-done.5.yb_ref = f32[960,128]{1,0:T(8,128)S(1)} collective-permute-done((f32[960,128]{1,0:T(8,128)S(1)}, f32[960,128]{1,0:T(8,128)S(1)}, u32[]{:S(2)}, u32[]{:S(2)}) %collective-permute-start.5) | collective-permute-done | bytes 491552 | tf_op jit(solution)/shard_map/ppermute | solution.py:533
  23.0 5.1 %advance.2 = (f32[512,128]{1,0:T(8,128)S(1)}, f32[64,32,128]{2,1,0:T(8,128)S(1)}, f32[352,128]{1,0:T(8,128)S(1)}, f32[352,128]{1,0:T(8,128)S(1)}, f32[160,128]{1,0:T(8,128)S(1)}, /*index=5*/f32[160,128]{1,0:T(8,128)S(1)}) custom-call(f32[512,128]{1,0:T(8,128)S(1)} %get-tuple-element.35.own_ref.after_ref, f32[352,128]{1,0:T(8,128)S(1)} %collective-permute-done.xa_ref.a1_ref, ...), custom_call_target="tpu_custom_call" | custom-call | tf_op jit(solution)/shard_map/advance/pallas_call | solution.py:339
  28.1 3.5 %collective-permute-start.6 = (f32[352,128]{1,0:T(8,128)S(1)}, f32[352,128]{1,0:T(8,128)S(1)}, u32[]{:S(2)}, u32[]{:S(2)}) collective-permute-start(f32[352,128]{1,0:T(8,128)S(1)} %get-tuple-element.47), channel_id=1, source_target_pairs={{0,4},{1,5},{2,6},{3,7},{8,12},{9,13},{10,14},{11,15},{16,20},{17,... | collective-permute-start | bytes 540680 | tf_op jit(solution)/shard_map/ppermute | solution.py:524
  31.6 0.0 collective-permute-start.7
  31.7 0.0 copy-start
  31.7 4.6 %copy-done = bf16[96,8,8,8,128]{4,3,2,1,0:T(8,128)(2,1)S(1)} copy-done((bf16[96,8,8,8,128]{4,3,2,1,0:T(8,128)(2,1)S(1)}, bf16[96,8,8,8,128]{4,3,2,1,0:T(8,128)(2,1)}, u32[]{:S(2)}) %copy-start) | copy-done | bytes 12582936
  36.2 4.1 %project.2.refs_0_ = f32[4,96]{1,0:T(4,128)S(1)} custom-call(bf16[96,8,64,128]{3,2,1,0:T(8,128)(2,1)S(1)} %bitcast.6, f32[64,32,128]{2,1,0:T(8,128)S(1)} %get-tuple-element.49.snap_ref), custom_call_target="tpu_custom_call" | custom-call | tf_op jit(solution)/shard_map/project/pallas_call | solution.py:424
  40.4 0.0 collective-permute-done.6.xa_ref.a1_ref
  40.4 0.0 collective-permute-done.7.xb_ref.b1_ref
  40.4 0.1 pack_for_y.3
  40.5 0.6 collective-permute-start.10
  41.1 1.2 %collective-permute-start.11 = (f32[960,128]{1,0:T(8,128)S(1)}, f32[960,128]{1,0:T(8,128)S(1)}, u32[]{:S(2)}, u32[]{:S(2)}) collective-permute-start(f32[960,128]{1,0:T(8,128)S(1)} %get-tuple-element.59), channel_id=1, source_target_pairs={{1,2},{5,6},{9,10},{13,14},{17,18},{21,22},{25,26},{29,30},{0,8},{... | collective-permute-start | bytes 1474568 | tf_op jit(solution)/shard_map/ppermute | solution.py:533
  42.2 3.5 %collective-permute-start.8 = (f32[160,128]{1,0:T(8,128)S(1)}, f32[160,128]{1,0:T(8,128)S(1)}, u32[]{:S(2)}, u32[]{:S(2)}) collective-permute-start(f32[160,128]{1,0:T(8,128)S(1)} %get-tuple-element.56), channel_id=1, source_target_pairs={{0,4},{1,5},{2,6},{3,7},{8,12},{9,13},{10,14},{11,15},{16,20},{17,... | collective-permute-start | bytes 245768 | tf_op jit(solution)/shard_map/ppermute | solution.py:534
  45.7 0.0 collective-permute-start.9
  45.7 2.4 %collective-permute-done.8.a2_ref = f32[160,128]{1,0:T(8,128)S(1)} collective-permute-done((f32[160,128]{1,0:T(8,128)S(1)}, f32[160,128]{1,0:T(8,128)S(1)}, u32[]{:S(2)}, u32[]{:S(2)}) %collective-permute-start.8) | collective-permute-done | bytes 81952 | tf_op jit(solution)/shard_map/ppermute | solution.py:534
  48.1 0.0 collective-permute-done.9.b2_ref
  48.1 0.0 collective-permute-done.10.ya_ref
  48.1 2.7 %collective-permute-done.11.yb_ref = f32[960,128]{1,0:T(8,128)S(1)} collective-permute-done((f32[960,128]{1,0:T(8,128)S(1)}, f32[960,128]{1,0:T(8,128)S(1)}, u32[]{:S(2)}, u32[]{:S(2)}) %collective-permute-start.11) | collective-permute-done | bytes 491552 | tf_op jit(solution)/shard_map/ppermute | solution.py:533
  50.8 5.3 %advance.3 = (f32[512,128]{1,0:T(8,128)S(1)}, f32[64,32,128]{2,1,0:T(8,128)S(1)}) custom-call(f32[512,128]{1,0:T(8,128)S(1)} %get-tuple-element.46.own_ref, f32[352,128]{1,0:T(8,128)S(1)} %collective-permute-done.6.xa_ref.a1_ref, f32[352,128]{1,0:T(8,128)S(1)} %collective-permute-done.7.xb_ref.b1_ref, f32[160,128]{1,0:T(8,128)S(1)} %collective-permute-done.8.a2_ref, ...), custom_call_target="tpu_custom_call" | custom-call | tf_op jit(solution)/shard_map/advance/pallas_call | solution.py:339
  56.0 0.0 copy-done.1
  56.1 4.8 %project.3.after_ref = f32[32,8,96]{2,1,0:T(8,128)} custom-call(bf16[96,8,64,128]{3,2,1,0:T(8,128)(2,1)S(1)} %bitcast.7, f32[64,32,128]{2,1,0:T(8,128)S(1)} %get-tuple-element.61.snap_ref, f32[4,96]{1,0:T(4,128)S(1)} %project.2.refs_0_), custom_call_target="tpu_custom_call" | custom-call | tf_op jit(solution)/shard_map/project/pallas_call | solution.py:424
  60.9 7.3 %all-to-all-start = ((f32[32,8,96]{2,1,0:T(8,128)}), f32[32,8,96]{2,1,0:T(8,128)S(1)}, u32[]{:S(2)}, u32[]{:S(2)}) async-start(f32[32,8,96]{2,1,0:T(8,128)} %project.3.after_ref), calls=%async_computation | async-start | bytes 262144 | tf_op jit(solution)/shard_map/all_to_all | solution.py:539
  68.1 0.7 copy.10
  68.8 0.0 copy-done.4
  68.8 0.1 pick_matrices.1.picks_ref
  69.0 7.4 %all-to-all-done.shares_ref = f32[32,8,96]{2,1,0:T(8,128)S(1)} async-done(((f32[32,8,96]{2,1,0:T(8,128)}), f32[32,8,96]{2,1,0:T(8,128)S(1)}, u32[]{:S(2)}, u32[]{:S(2)}) %all-to-all-start) | async-done | bytes 98336 | tf_op jit(solution)/shard_map/all_to_all | solution.py:539
  76.3 0.0 copy-done.3
  76.3 1.3 %infer.1 = (f32[8,96]{1,0:T(8,128)}, f32[96,96]{1,0:T(8,128)}, f32[96,1188]{1,0:T(8,128)}) custom-call(f32[32,8,96]{2,1,0:T(8,128)S(1)} %all-to-all-done.shares_ref, f32[96,96]{1,0:T(8,128)S(1)} %copy-done.3, bf16[128,2560]{1,0:T(8,128)(2,1)S(1)} %pick_matrices.1.picks_ref), custom_call_target="tpu_custom_call" | custom-call | tf_op jit(solution)/shard_map/infer/pallas_call | solution.py:498
  (3 shorter events, 0.0 us)
Async XLA Ops:
  0.6 1.0 %copy-start.2 = (f32[8,8,8,128]{3,2,1,0:T(8,128)S(1)}, f32[8,8,8,128]{3,2,1,0:T(8,128)}, u32[]{:S(2)}) copy-start(f32[8,8,8,128]{3,2,1,0:T(8,128)} %param.6) | copy-start | bytes 786436
  1.8 10.7 %collective-permute-start = (f32[352,128]{1,0:T(8,128)S(1)}, f32[352,128]{1,0:T(8,128)S(1)}, u32[]{:S(2)}, u32[]{:S(2)}) collective-permute-start(f32[352,128]{1,0:T(8,128)S(1)} %get-tuple-element.36), channel_id=1, source_target_pairs={{0,4},{1,5},{2,6},{3,7},{8,12},{9,13},{10,14},{11,15},{16,20},{17,... | collective-permute-start | bytes 540680 | tf_op jit(solution)/shard_map/ppermute | solution.py:524
  4.8 7.7 %collective-permute-start.1 = (f32[352,128]{1,0:T(8,128)S(1)}, f32[352,128]{1,0:T(8,128)S(1)}, u32[]{:S(2)}, u32[]{:S(2)}) collective-permute-start(f32[352,128]{1,0:T(8,128)S(1)} %get-tuple-element.37), channel_id=1, source_target_pairs={{4,8},{5,9},{6,10},{7,11},{12,16},{13,17},{14,18},{15,19},{20,24},... | collective-permute-start | bytes 540680 | tf_op jit(solution)/shard_map/ppermute | solution.py:525
  12.6 7.2 %collective-permute-start.4 = (f32[960,128]{1,0:T(8,128)S(1)}, f32[960,128]{1,0:T(8,128)S(1)}, u32[]{:S(2)}, u32[]{:S(2)}) collective-permute-start(f32[960,128]{1,0:T(8,128)S(1)} %get-tuple-element.44), channel_id=1, source_target_pairs={{0,1},{2,3},{4,5},{6,7},{8,9},{10,11},{12,13},{14,15},{16,17},{18,... | collective-permute-start | bytes 1474568 | tf_op jit(solution)/shard_map/ppermute | solution.py:532
  12.6 10.3 %collective-permute-start.5 = (f32[960,128]{1,0:T(8,128)S(1)}, f32[960,128]{1,0:T(8,128)S(1)}, u32[]{:S(2)}, u32[]{:S(2)}) collective-permute-start(f32[960,128]{1,0:T(8,128)S(1)} %get-tuple-element.45), channel_id=1, source_target_pairs={{1,2},{5,6},{9,10},{13,14},{17,18},{21,22},{25,26},{29,30},{0,8},{... | collective-permute-start | bytes 1474568 | tf_op jit(solution)/shard_map/ppermute | solution.py:533
  15.3 4.4 %collective-permute-start.2 = (f32[160,128]{1,0:T(8,128)S(1)}, f32[160,128]{1,0:T(8,128)S(1)}, u32[]{:S(2)}, u32[]{:S(2)}) collective-permute-start(f32[160,128]{1,0:T(8,128)S(1)} %get-tuple-element.42), channel_id=1, source_target_pairs={{0,4},{1,5},{2,6},{3,7},{8,12},{9,13},{10,14},{11,15},{16,20},{17,... | collective-permute-start | bytes 245768 | tf_op jit(solution)/shard_map/ppermute | solution.py:534
  16.8 3.0 %collective-permute-start.3 = (f32[160,128]{1,0:T(8,128)S(1)}, f32[160,128]{1,0:T(8,128)S(1)}, u32[]{:S(2)}, u32[]{:S(2)}) collective-permute-start(f32[160,128]{1,0:T(8,128)S(1)} %get-tuple-element.43), channel_id=1, source_target_pairs={{4,8},{5,9},{6,10},{7,11},{12,16},{13,17},{14,18},{15,19},{20,24},... | collective-permute-start | bytes 245768 | tf_op jit(solution)/shard_map/ppermute | solution.py:535
  16.8 0.7 copy-start.5
  17.4 0.7 copy-start.6
  28.1 12.3 %collective-permute-start.6 = (f32[352,128]{1,0:T(8,128)S(1)}, f32[352,128]{1,0:T(8,128)S(1)}, u32[]{:S(2)}, u32[]{:S(2)}) collective-permute-start(f32[352,128]{1,0:T(8,128)S(1)} %get-tuple-element.47), channel_id=1, source_target_pairs={{0,4},{1,5},{2,6},{3,7},{8,12},{9,13},{10,14},{11,15},{16,20},{17,... | collective-permute-start | bytes 540680 | tf_op jit(solution)/shard_map/ppermute | solution.py:524
  31.6 8.7 %collective-permute-start.7 = (f32[352,128]{1,0:T(8,128)S(1)}, f32[352,128]{1,0:T(8,128)S(1)}, u32[]{:S(2)}, u32[]{:S(2)}) collective-permute-start(f32[352,128]{1,0:T(8,128)S(1)} %get-tuple-element.48), channel_id=1, source_target_pairs={{4,8},{5,9},{6,10},{7,11},{12,16},{13,17},{14,18},{15,19},{20,24},... | collective-permute-start | bytes 540680 | tf_op jit(solution)/shard_map/ppermute | solution.py:525
  31.7 4.6 %copy-start = (bf16[96,8,8,8,128]{4,3,2,1,0:T(8,128)(2,1)S(1)}, bf16[96,8,8,8,128]{4,3,2,1,0:T(8,128)(2,1)}, u32[]{:S(2)}) copy-start(bf16[96,8,8,8,128]{4,3,2,1,0:T(8,128)(2,1)} %param.9) | copy-start | bytes 37748740
  36.2 19.8 %copy-start.1 = (bf16[96,8,8,8,128]{4,3,2,1,0:T(8,128)(2,1)S(1)}, bf16[96,8,8,8,128]{4,3,2,1,0:T(8,128)(2,1)}, u32[]{:S(2)}) copy-start(bf16[96,8,8,8,128]{4,3,2,1,0:T(8,128)(2,1)} %param.9) | copy-start | bytes 37748740
  36.2 32.6 %copy-start.4 = (s32[4,2560]{1,0:T(4,128)S(1)}, s32[4,2560]{1,0:T(4,128)}, u32[]{:S(2)}) copy-start(s32[4,2560]{1,0:T(4,128)} %constant.2.clone.tables_ref) | copy-start | bytes 122884
  36.2 40.1 %copy-start.3 = (f32[96,96]{1,0:T(8,128)S(1)}, f32[96,96]{1,0:T(8,128)}, u32[]{:S(2)}) copy-start(f32[96,96]{1,0:T(8,128)} %gram_ref.1) | copy-start | bytes 110596
  40.5 7.6 %collective-permute-start.10 = (f32[960,128]{1,0:T(8,128)S(1)}, f32[960,128]{1,0:T(8,128)S(1)}, u32[]{:S(2)}, u32[]{:S(2)}) collective-permute-start(f32[960,128]{1,0:T(8,128)S(1)} %get-tuple-element.58), channel_id=1, source_target_pairs={{0,1},{2,3},{4,5},{6,7},{8,9},{10,11},{12,13},{14,15},{16,17},{18,... | collective-permute-start | bytes 1474568 | tf_op jit(solution)/shard_map/ppermute | solution.py:532
  41.1 9.7 %collective-permute-start.11 = (f32[960,128]{1,0:T(8,128)S(1)}, f32[960,128]{1,0:T(8,128)S(1)}, u32[]{:S(2)}, u32[]{:S(2)}) collective-permute-start(f32[960,128]{1,0:T(8,128)S(1)} %get-tuple-element.59), channel_id=1, source_target_pairs={{1,2},{5,6},{9,10},{13,14},{17,18},{21,22},{25,26},{29,30},{0,8},{... | collective-permute-start | bytes 1474568 | tf_op jit(solution)/shard_map/ppermute | solution.py:533
  42.2 5.9 %collective-permute-start.8 = (f32[160,128]{1,0:T(8,128)S(1)}, f32[160,128]{1,0:T(8,128)S(1)}, u32[]{:S(2)}, u32[]{:S(2)}) collective-permute-start(f32[160,128]{1,0:T(8,128)S(1)} %get-tuple-element.56), channel_id=1, source_target_pairs={{0,4},{1,5},{2,6},{3,7},{8,12},{9,13},{10,14},{11,15},{16,20},{17,... | collective-permute-start | bytes 245768 | tf_op jit(solution)/shard_map/ppermute | solution.py:534
  45.7 2.4 %collective-permute-start.9 = (f32[160,128]{1,0:T(8,128)S(1)}, f32[160,128]{1,0:T(8,128)S(1)}, u32[]{:S(2)}, u32[]{:S(2)}) collective-permute-start(f32[160,128]{1,0:T(8,128)S(1)} %get-tuple-element.57), channel_id=1, source_target_pairs={{4,8},{5,9},{6,10},{7,11},{12,16},{13,17},{14,18},{15,19},{20,24},... | collective-permute-start | bytes 245768 | tf_op jit(solution)/shard_map/ppermute | solution.py:535
  60.9 15.5 %all-to-all-start = ((f32[32,8,96]{2,1,0:T(8,128)}), f32[32,8,96]{2,1,0:T(8,128)S(1)}, u32[]{:S(2)}, u32[]{:S(2)}) async-start(f32[32,8,96]{2,1,0:T(8,128)} %project.3.after_ref), calls=%async_computation | async-start | bytes 262144 | tf_op jit(solution)/shard_map/all_to_all | solution.py:539

commit v5 on v4

--- a/solution.py
+++ b/solution.py
@@ -8,6 +8,7 @@
 from jax.experimental.pallas import tpu as pltpu
 from jax.sharding import PartitionSpec as P
 
+
 STEPS = 8
 
 time_step = 0.1
@@ -34,8 +35,9 @@
     y_even = both_ways([(s * nl + l, s * nl + l + 1) for s in range(ns) for l in range(0, nl, 2)])
     y_odd = [(s * nl + l, s * nl + l + 1) for s in range(ns) for l in range(1, nl - 1, 2)]
     far = 2 if ns % 4 == 0 else 1
-    y_odd += [(s * nl + l, (s + far) * nl + l) for s in range(ns) if s // far % 2 == 0 for l in (0, nl - 1)]
-    return x_even, both_ways(x_odd), y_even, both_ways(y_odd)
+    y_far = y_odd + [(s * nl + l, (s + far) * nl + l) for s in range(ns) if s // far % 2 == 0 for l in (0, nl - 1)]
+    y_odd = y_odd + [(s * nl, s * nl + nl - 1) for s in range(ns)]
+    return x_even, both_ways(x_odd), y_even, both_ways(y_odd), both_ways(y_far)
 
 
 def in_vmem(*arrays):
@@ -135,7 +137,7 @@
     )(diffusivity, stoich, after)
 
 
-def pack_kernel(cx, cy, nf, own_ref, xa_ref, xb_ref, to_a_ref, to_b_ref):
+def pack_kernel(cx, cy, nf, xa_ref, xb_ref, to_a_ref, to_b_ref):
     runs, size = corner_runs(cx)
 
     def copy(l_is_even):
@@ -147,28 +149,42 @@
                     out_ref[pl.ds((side * size + first) * nf, count * nf), :] = rows
 
     each_case(lax.rem(lax.axis_index("learn"), 2) == 0, copy)
-    for x in range(cx):
-        rows = own_ref[pl.ds(x * cy * nf, cy * nf), :]
-        for out_ref in (to_a_ref, to_b_ref):
-            out_ref[pl.ds((2 * size + x * cy) * nf, cy * nf), :] = rows
-
-
-def pack_for_y(own, xa, xb, cx, cy, nf):
-    nz = own.shape[1]
-    size = 2 * corner_runs(cx)[1] + cx * cy
+
+
+def pack_corners(xa, xb, cx, cy, nf):
+    nz = xa.shape[1]
+    size = 2 * corner_runs(cx)[1]
     shape = pltpu.VMEM((size * nf, nz), jnp.float32)
     return pl.pallas_call(
         functools.partial(pack_kernel, cx, cy, nf),
         out_shape=(shape, shape),
-        in_specs=[VMEM] * 3,
+        in_specs=[VMEM] * 2,
         out_specs=(VMEM, VMEM),
         compiler_params=pltpu.CompilerParams(vmem_limit_bytes=MIB),
-        name="pack_for_y",
-    )(*in_vmem(own, xa, xb))
+        name="pack_corners",
+    )(*in_vmem(xa, xb))
+
+
+def load_kernel(source_ref, out_ref, sem):
+    copy = pltpu.make_async_copy(source_ref, out_ref, sem)
+    copy.start()
+    copy.wait()
+
+
+def load_basis(basis):
+    return pl.pallas_call(
+        load_kernel,
+        out_shape=pltpu.VMEM(basis.shape, basis.dtype),
+        in_specs=[pl.BlockSpec(memory_space=pltpu.HBM)],
+        out_specs=VMEM,
+        scratch_shapes=[pltpu.SemaphoreType.DMA],
+        compiler_params=pltpu.CompilerParams(vmem_limit_bytes=MIB),
+        name="load_basis",
+    )(pltpu.with_memory_space_constraint(basis, pltpu.HBM))
 
 
 def round_kernel(
-    cx, cy, nf, steps, last, own_ref, a1_ref, b1_ref, a2_ref, b2_ref, ya_ref, yb_ref, factors_ref,
+    cx, cy, nf, steps, last, own_ref, a1_ref, b1_ref, a2_ref, b2_ref, ya_ref, yb_ref, ca_ref, cb_ref, factors_ref,
     state_ref, snap_ref, *refs,
 ):
     cut_refs, (u_ref, m_ref, rate_ref) = refs[:-3], refs[-3:]
@@ -181,9 +197,9 @@
     has_west, has_east = s > 0, s < ns - 1
     has_south, has_north = l > 0, l < nl - 1
 
-    def place(ref, row, x0, y0):
+    def place(ref, x0, y0):
         for i in range(cx):
-            rows = ref[pl.ds((row + i * cy) * nf, cy * nf), :]
+            rows = ref[pl.ds(i * cy * nf, cy * nf), :]
             u_ref[pl.ds(((x0 + i) * wide_y + y0) * nf, cy * nf), :] = rows
 
     def halo_x(is_east, d):
@@ -199,7 +215,7 @@
 
         lax.fori_loop(x0, x1, trip, 0)
 
-    place(own_ref, 0, reach, reach)
+    place(own_ref, reach, reach)
     corners, size = corner_runs(reach)
     parts, _ = x_runs(reach, cy)
 
@@ -214,18 +230,18 @@
                         u_ref[pl.ds((halo_x(is_east, d) * wide_y + reach + y) * nf, count * nf), :] = rows
 
     def receive_y(l_is_even):
-        for ref, north in ((ya_ref, l_is_even), (yb_ref, not l_is_even)):
+        for ref, corner, north in ((ya_ref, ca_ref, l_is_even), (yb_ref, cb_ref, not l_is_even)):
 
             @pl.when(has_north if north else has_south)
-            def _(ref=ref, north=north):
-                place(ref, 2 * size, reach, reach + cy if north else 0)
+            def _(ref=ref, corner=corner, north=north):
+                place(ref, reach, reach + cy if north else 0)
 
                 def receive_corners(s_is_even):
                     for side in range(2):
                         for d, count, first in corners:
                             x = halo_x(s_is_even == (side == 0), d)
                             y = reach + cy if north else reach - count
-                            rows = ref[pl.ds((side * size + first) * nf, count * nf), :]
+                            rows = corner[pl.ds((side * size + first) * nf, count * nf), :]
                             u_ref[pl.ds((x * wide_y + y) * nf, count * nf), :] = rows
 
                 each_case(even_s, receive_corners)
@@ -343,7 +359,7 @@
             pltpu.VMEM((nf * cx, steps * cy, nz), jnp.float32),
             *cuts,
         ],
-        in_specs=[VMEM] * 8,
+        in_specs=[VMEM] * 10,
         out_specs=[VMEM] * (2 + len(cuts)),
         scratch_shapes=[
             pltpu.VMEM((wide * nf, nz), jnp.float32),
@@ -494,7 +510,7 @@
 
 
 def infer(shares, gram_old, picks, block):
-    count, steps, modes = shares.shape
+    _, steps, modes = shares.shape
     reduced, pod_gram, rhs = pl.pallas_call(
         infer_kernel,
         out_shape=(
@@ -510,30 +526,33 @@
     return reduced.T, pod_gram, rhs.T
 
 
+def swap(value, pairs):
+    return lax.ppermute(value, BOTH, pairs)
+
+
 def body(fields, diffusivity, stoich, basis, gram_old):
     nf, cx, cy, nz = fields.shape
     ns, nl = lax.axis_size("sim"), lax.axis_size("learn")
     steps = min(cx, cy) // 2
     rounds = STEPS // steps
-    x_even, x_odd, y_even, y_odd = swaps(ns, nl)
+    x_even, x_odd, y_even, y_odd, y_far = swaps(ns, nl)
     state, *cuts = to_columns(fields)
     factors = field_factors(diffusivity, stoich, nz, state)
-    (basis,) = in_vmem(basis.reshape(basis.shape[0], nf, cx * cy, nz))
     share = None
     for n in range(rounds):
-        a1 = lax.ppermute(cuts[0], BOTH, x_even)
-        b1 = lax.ppermute(cuts[1], BOTH, x_odd)
-        if n:
+        a1, b1 = swap(cuts[0], x_even), swap(cuts[1], x_odd)
+        ya, yb = swap(state, y_even), swap(state, y_odd)
+        a2, b2 = swap(cuts[2], x_even), swap(cuts[3], x_odd)
+        if n == 0:
+            basis = load_basis(basis.reshape(basis.shape[0], nf, cx * cy, nz))
+            a1, b1, basis, factors = lax.optimization_barrier((a1, b1, basis, factors))
+        else:
             part = project(basis, snaps, cx, cy, steps)
             a1, b1, part = lax.optimization_barrier((a1, b1, part))
             share = part if share is None else jnp.concatenate([share, part], axis=0)
-        to_a, to_b = pack_for_y(state, a1, b1, cx, cy, nf)
-        to_a, to_b, *rest = lax.optimization_barrier((to_a, to_b, *cuts[2:]))
-        ya = lax.ppermute(to_a, BOTH, y_even)
-        yb = lax.ppermute(to_b, BOTH, y_odd)
-        a2 = lax.ppermute(rest[0], BOTH, x_even)
-        b2 = lax.ppermute(rest[1], BOTH, x_odd)
-        operands = (state, a1, b1, a2, b2, ya, yb, factors)
+        to_a, to_b = pack_corners(a1, b1, cx, cy, nf)
+        ca, cb = swap(to_a, y_even), swap(to_b, y_far)
+        operands = (state, a1, b1, a2, b2, ya, yb, ca, cb, factors)
         state, snaps, *cuts = advance(operands, cx, cy, nf, steps, n == rounds - 1)
     sent = project(basis, snaps, cx, cy, steps, share, ns * nl)
     shares = lax.all_to_all(sent, BOTH, 0, 0)

time: 77.9 us -> 77.2 us (level)
  starting transfers between devices: 23.2 us -> 30.9 us
  waiting for transfers between devices: 24.4 us -> 17.4 us
  local copies, waits for them, and re-layouts: 7.55 us -> 1.66 us
  Pallas kernels: 21.7 us -> 26.2 us
    ppermute x12 -> x16, waiting for transfers between devices: 17.1 us -> 10 us  [swap(): return lax.ppermute(value, BOTH, pairs)]
    ppermute x12 -> x16, starting transfers between devices: 16 us -> 21.9 us  [swap(): return lax.ppermute(value, BOTH, pairs)]
    unnamed x15 -> x11, local copies, waits for them, and re-layouts: 7.55 us -> 1.66 us
    pallas_call x2 -> x3, Pallas kernels: 0.15 us -> 4.68 us  [the longest x1 4.61 us: load_basis(): pl.pallas_call(load_kernel, out_shape=pltpu.VMEM(basis.shape, basis.dtype...]
    all_to_all x1, starting transfers between devices: 7.26 us -> 8.99 us  [body(): shares = lax.all_to_all(sent, BOTH, 0, 0)]
  transfers between devices with their start and end apart: 13 -> 17, of which waited for: 6 -> 7; matrix products, arithmetic and copies ran while one was open for 1% -> 1% of each run, Pallas kernels for 6% -> 12%
where the time goes in v5:
time: 77.2 us; the launch traced here: 77 us
  starting transfers between devices  30.9 us (40%)
  Pallas kernels  26.2 us (34%)
  waiting for transfers between devices  17.4 us (23%)
  local copies, waits for them, and re-layouts  1.66 us (2%)
  between operations  0.79 us (1%)
    ppermute x16, starting transfers between devices, swap(): return lax.ppermute(value, BOTH, pairs)  21.9 us
    pallas_call x2, Pallas kernels, advance(): pl.pallas_call(functools.partial(round_kernel, cx, cy, nf, steps, last),...  10.4 us
    ppermute x16, waiting for transfers between devices, swap(): return lax.ppermute(value, BOTH, pairs)  10 us
    all_to_all x1, starting transfers between devices, body(): shares = lax.all_to_all(sent, BOTH, 0, 0)  8.99 us
    pallas_call x2, Pallas kernels, project(): pl.pallas_call(functools.partial(project_kernel, cx, cy, steps, copies),...  8.95 us
    all_to_all x1, waiting for transfers between devices, body(): shares = lax.all_to_all(sent, BOTH, 0, 0)  7.38 us
    pallas_call x1, Pallas kernels, load_basis(): pl.pallas_call(load_kernel, out_shape=pltpu.VMEM(basis.shape, basis.dtype...  4.61 us
    unnamed x11, local copies, waits for them, and re-layouts  1.66 us
  transfers between devices with their start and end apart: 17, of which 7 were waited for; matrix products, arithmetic and copies ran while one was open for 1% of the time, Pallas kernels for 12%

profile of v5, /device:TPU:0, one launch (start us, length us, event | category | flops | bytes accessed | tf_op | source)
XLA Modules:
  0.0 77.0 jit_solution(12218175429375490804)
XLA Ops:
  0.6 0.0 copy-start
  0.6 0.9 %copy-done = f32[8,8,8,128]{3,2,1,0:T(8,128)S(1)} copy-done((f32[8,8,8,128]{3,2,1,0:T(8,128)S(1)}, f32[8,8,8,128]{3,2,1,0:T(8,128)}, u32[]{:S(2)}) %copy-start) | copy-done | bytes 262168
  1.6 0.2 to_columns.1
  1.8 3.0 %collective-permute-start = (f32[352,128]{1,0:T(8,128)S(1)}, f32[352,128]{1,0:T(8,128)S(1)}, u32[]{:S(2)}, u32[]{:S(2)}) collective-permute-start(f32[352,128]{1,0:T(8,128)S(1)} %get-tuple-element.32), channel_id=1, source_target_pairs={{0,4},{1,5},{2,6},{3,7},{8,12},{9,13},{10,14},{11,15},{16,20},{17,... | collective-permute-start | bytes 540680 | tf_op jit(solution)/shard_map/ppermute | solution.py:530
  4.8 0.0 collective-permute-start.1
  4.8 1.6 %collective-permute-start.5 = (f32[512,128]{1,0:T(8,128)S(1)}, f32[512,128]{1,0:T(8,128)S(1)}, u32[]{:S(2)}, u32[]{:S(2)}) collective-permute-start(f32[512,128]{1,0:T(8,128)S(1)} %get-tuple-element.31.after_ref.own_ref), channel_id=1, source_target_pairs={{1,2},{5,6},{9,10},{13,14},{17,18},{21,22},{25,26},{29,30},{0,3},{... | collective-permute-start | bytes 786440 | tf_op jit(solution)/shard_map/ppermute | solution.py:530
  6.4 0.0 collective-permute-start.4
  6.5 4.6 %load_basis.1.basis_ref = bf16[96,8,64,128]{3,2,1,0:T(8,128)(2,1)S(1)} custom-call(bf16[96,8,64,128]{3,2,1,0:T(8,128)(2,1)} %bitcast.7), custom_call_target="tpu_custom_call" | custom-call | tf_op jit(solution)/shard_map/load_basis/pallas_call | solution.py:175
  11.1 0.0 copy-done.3
  11.1 0.6 field_factors.1.factors_ref
  11.7 0.8 %collective-permute-done.xa_ref.a1_ref = f32[352,128]{1,0:T(8,128)S(1)} collective-permute-done((f32[352,128]{1,0:T(8,128)S(1)}, f32[352,128]{1,0:T(8,128)S(1)}, u32[]{:S(2)}, u32[]{:S(2)}) %collective-permute-start) | collective-permute-done | bytes 180256 | tf_op jit(solution)/shard_map/ppermute | solution.py:530
  12.5 0.0 collective-permute-done.1.xb_ref.b1_ref
  12.5 0.1 collective-permute-start.6
  12.6 2.6 %collective-permute-start.7 = (f32[448,128]{1,0:T(8,128)S(1)}, f32[448,128]{1,0:T(8,128)S(1)}, u32[]{:S(2)}, u32[]{:S(2)}) collective-permute-start(f32[448,128]{1,0:T(8,128)S(1)} %get-tuple-element.39), channel_id=1, source_target_pairs={{1,2},{5,6},{9,10},{13,14},{17,18},{21,22},{25,26},{29,30},{0,8},{... | collective-permute-start | bytes 688136 | tf_op jit(solution)/shard_map/ppermute | solution.py:530
  15.2 1.5 %collective-permute-start.2 = (f32[160,128]{1,0:T(8,128)S(1)}, f32[160,128]{1,0:T(8,128)S(1)}, u32[]{:S(2)}, u32[]{:S(2)}) collective-permute-start(f32[160,128]{1,0:T(8,128)S(1)} %get-tuple-element.36), channel_id=1, source_target_pairs={{0,4},{1,5},{2,6},{3,7},{8,12},{9,13},{10,14},{11,15},{16,20},{17,... | collective-permute-start | bytes 245768 | tf_op jit(solution)/shard_map/ppermute | solution.py:530
  16.7 3.0 %collective-permute-done.2.a2_ref = f32[160,128]{1,0:T(8,128)S(1)} collective-permute-done((f32[160,128]{1,0:T(8,128)S(1)}, f32[160,128]{1,0:T(8,128)S(1)}, u32[]{:S(2)}, u32[]{:S(2)}) %collective-permute-start.2) | collective-permute-done | bytes 81952 | tf_op jit(solution)/shard_map/ppermute | solution.py:530
  19.7 0.0 collective-permute-start.3
  19.7 1.3 %collective-permute-done.3.b2_ref = f32[160,128]{1,0:T(8,128)S(1)} collective-permute-done((f32[160,128]{1,0:T(8,128)S(1)}, f32[160,128]{1,0:T(8,128)S(1)}, u32[]{:S(2)}, u32[]{:S(2)}) %collective-permute-start.3) | collective-permute-done | bytes 81952 | tf_op jit(solution)/shard_map/ppermute | solution.py:530
  21.0 0.0 collective-permute-done.5.yb_ref
  21.0 0.0 collective-permute-done.4.ya_ref
  21.0 0.0 collective-permute-done.6.ca_ref
  21.0 0.0 collective-permute-done.7.cb_ref
  21.0 5.1 %advance.2 = (f32[512,128]{1,0:T(8,128)S(1)}, f32[64,32,128]{2,1,0:T(8,128)S(1)}, f32[352,128]{1,0:T(8,128)S(1)}, f32[352,128]{1,0:T(8,128)S(1)}, f32[160,128]{1,0:T(8,128)S(1)}, /*index=5*/f32[160,128]{1,0:T(8,128)S(1)}) custom-call(f32[512,128]{1,0:T(8,128)S(1)} %get-tuple-element.31.after_ref.own_ref, f32[352,128]{1,0:T(8,128)S(1)} %collective-permute-done.xa_ref.a1_ref, ...), custom_call_target="tpu_custom_call" | custom-call | tf_op jit(solution)/shard_map/advance/pallas_call | solution.py:355
  26.1 6.7 %collective-permute-start.8 = (f32[352,128]{1,0:T(8,128)S(1)}, f32[352,128]{1,0:T(8,128)S(1)}, u32[]{:S(2)}, u32[]{:S(2)}) collective-permute-start(f32[352,128]{1,0:T(8,128)S(1)} %get-tuple-element.42), channel_id=1, source_target_pairs={{0,4},{1,5},{2,6},{3,7},{8,12},{9,13},{10,14},{11,15},{16,20},{17,... | collective-permute-start | bytes 540680 | tf_op jit(solution)/shard_map/ppermute | solution.py:530
  32.9 0.0 collective-permute-start.9
  32.9 1.2 %collective-permute-start.13 = (f32[512,128]{1,0:T(8,128)S(1)}, f32[512,128]{1,0:T(8,128)S(1)}, u32[]{:S(2)}, u32[]{:S(2)}) collective-permute-start(f32[512,128]{1,0:T(8,128)S(1)} %get-tuple-element.41.own_ref), channel_id=1, source_target_pairs={{1,2},{5,6},{9,10},{13,14},{17,18},{21,22},{25,26},{29,30},{0,3},{... | collective-permute-start | bytes 786440 | tf_op jit(solution)/shard_map/ppermute | solution.py:530
  34.1 0.0 collective-permute-start.12
  34.1 4.1 %project.2.refs_0_ = f32[4,96]{1,0:T(4,128)S(1)} custom-call(bf16[96,8,64,128]{3,2,1,0:T(8,128)(2,1)S(1)} %load_basis.1.basis_ref, f32[64,32,128]{2,1,0:T(8,128)S(1)} %get-tuple-element.45.snap_ref), custom_call_target="tpu_custom_call" | custom-call | tf_op jit(solution)/shard_map/project/pallas_call | solution.py:440
  38.2 0.7 collective-permute-done.8.xa_ref.a1_ref
  39.0 0.0 collective-permute-done.9.xb_ref.b1_ref
  39.0 0.1 collective-permute-start.14
  39.1 3.6 %collective-permute-start.15 = (f32[448,128]{1,0:T(8,128)S(1)}, f32[448,128]{1,0:T(8,128)S(1)}, u32[]{:S(2)}, u32[]{:S(2)}) collective-permute-start(f32[448,128]{1,0:T(8,128)S(1)} %get-tuple-element.51), channel_id=1, source_target_pairs={{1,2},{5,6},{9,10},{13,14},{17,18},{21,22},{25,26},{29,30},{0,8},{... | collective-permute-start | bytes 688136 | tf_op jit(solution)/shard_map/ppermute | solution.py:530
  42.6 1.5 %collective-permute-start.10 = (f32[160,128]{1,0:T(8,128)S(1)}, f32[160,128]{1,0:T(8,128)S(1)}, u32[]{:S(2)}, u32[]{:S(2)}) collective-permute-start(f32[160,128]{1,0:T(8,128)S(1)} %get-tuple-element.48), channel_id=1, source_target_pairs={{0,4},{1,5},{2,6},{3,7},{8,12},{9,13},{10,14},{11,15},{16,20},{17,... | collective-permute-start | bytes 245768 | tf_op jit(solution)/shard_map/ppermute | solution.py:530
  44.1 3.0 %collective-permute-done.10.a2_ref = f32[160,128]{1,0:T(8,128)S(1)} collective-permute-done((f32[160,128]{1,0:T(8,128)S(1)}, f32[160,128]{1,0:T(8,128)S(1)}, u32[]{:S(2)}, u32[]{:S(2)}) %collective-permute-start.10) | collective-permute-done | bytes 81952 | tf_op jit(solution)/shard_map/ppermute | solution.py:530
  47.1 0.0 collective-permute-start.11
  47.1 1.3 %collective-permute-done.11.b2_ref = f32[160,128]{1,0:T(8,128)S(1)} collective-permute-done((f32[160,128]{1,0:T(8,128)S(1)}, f32[160,128]{1,0:T(8,128)S(1)}, u32[]{:S(2)}, u32[]{:S(2)}) %collective-permute-start.11) | collective-permute-done | bytes 81952 | tf_op jit(solution)/shard_map/ppermute | solution.py:530
  48.4 0.0 collective-permute-done.13.yb_ref
  48.4 0.0 collective-permute-done.12.ya_ref
  48.4 0.0 collective-permute-done.14.ca_ref
  48.4 0.0 collective-permute-done.15.cb_ref
  48.4 5.3 %advance.3 = (f32[512,128]{1,0:T(8,128)S(1)}, f32[64,32,128]{2,1,0:T(8,128)S(1)}) custom-call(f32[512,128]{1,0:T(8,128)S(1)} %get-tuple-element.41.own_ref, f32[352,128]{1,0:T(8,128)S(1)} %collective-permute-done.8.xa_ref.a1_ref, f32[352,128]{1,0:T(8,128)S(1)} %collective-permute-done.9.xb_ref.b1_ref, f32[160,128]{1,0:T(8,128)S(1)} %collective-permute-done.10.a2_ref, ...), custom_call_target="tpu_custom_call" | custom-call | tf_op jit(solution)/shard_map/advance/pallas_call | solution.py:355
  53.6 4.8 %project.3.after_ref = f32[32,8,96]{2,1,0:T(8,128)} custom-call(bf16[96,8,64,128]{3,2,1,0:T(8,128)(2,1)S(1)} %load_basis.1.basis_ref, f32[64,32,128]{2,1,0:T(8,128)S(1)} %get-tuple-element.53.snap_ref, f32[4,96]{1,0:T(4,128)S(1)} %project.2.refs_0_), custom_call_target="tpu_custom_call" | custom-call | tf_op jit(solution)/shard_map/project/pallas_call | solution.py:440
  58.5 9.0 %all-to-all-start = ((f32[32,8,96]{2,1,0:T(8,128)}), f32[32,8,96]{2,1,0:T(8,128)S(1)}, u32[]{:S(2)}, u32[]{:S(2)}) async-start(f32[32,8,96]{2,1,0:T(8,128)} %project.3.after_ref), calls=%async_computation | async-start | bytes 262144 | tf_op jit(solution)/shard_map/all_to_all | solution.py:558
  67.5 0.7 copy.10
  68.2 0.1 pick_matrices.1.picks_ref
  68.3 7.4 %all-to-all-done.shares_ref = f32[32,8,96]{2,1,0:T(8,128)S(1)} async-done(((f32[32,8,96]{2,1,0:T(8,128)}), f32[32,8,96]{2,1,0:T(8,128)S(1)}, u32[]{:S(2)}, u32[]{:S(2)}) %all-to-all-start) | async-done | bytes 98336 | tf_op jit(solution)/shard_map/all_to_all | solution.py:558
  75.7 0.0 copy-done.1
  75.7 1.3 %infer.1 = (f32[8,96]{1,0:T(8,128)}, f32[96,96]{1,0:T(8,128)}, f32[96,1188]{1,0:T(8,128)}) custom-call(f32[32,8,96]{2,1,0:T(8,128)S(1)} %all-to-all-done.shares_ref, f32[96,96]{1,0:T(8,128)S(1)} %copy-done.1, bf16[128,2560]{1,0:T(8,128)(2,1)S(1)} %pick_matrices.1.picks_ref), custom_call_target="tpu_custom_call" | custom-call | tf_op jit(solution)/shard_map/infer/pallas_call | solution.py:514
  (8 shorter events, 0.1 us)
Async XLA Ops:
  0.6 1.0 %copy-start = (f32[8,8,8,128]{3,2,1,0:T(8,128)S(1)}, f32[8,8,8,128]{3,2,1,0:T(8,128)}, u32[]{:S(2)}) copy-start(f32[8,8,8,128]{3,2,1,0:T(8,128)} %param.6) | copy-start | bytes 786436
  1.8 10.7 %collective-permute-start = (f32[352,128]{1,0:T(8,128)S(1)}, f32[352,128]{1,0:T(8,128)S(1)}, u32[]{:S(2)}, u32[]{:S(2)}) collective-permute-start(f32[352,128]{1,0:T(8,128)S(1)} %get-tuple-element.32), channel_id=1, source_target_pairs={{0,4},{1,5},{2,6},{3,7},{8,12},{9,13},{10,14},{11,15},{16,20},{17,... | collective-permute-start | bytes 540680 | tf_op jit(solution)/shard_map/ppermute | solution.py:530
  4.8 7.7 %collective-permute-start.1 = (f32[352,128]{1,0:T(8,128)S(1)}, f32[352,128]{1,0:T(8,128)S(1)}, u32[]{:S(2)}, u32[]{:S(2)}) collective-permute-start(f32[352,128]{1,0:T(8,128)S(1)} %get-tuple-element.33), channel_id=1, source_target_pairs={{4,8},{5,9},{6,10},{7,11},{12,16},{13,17},{14,18},{15,19},{20,24},... | collective-permute-start | bytes 540680 | tf_op jit(solution)/shard_map/ppermute | solution.py:530
  4.8 16.1 %collective-permute-start.5 = (f32[512,128]{1,0:T(8,128)S(1)}, f32[512,128]{1,0:T(8,128)S(1)}, u32[]{:S(2)}, u32[]{:S(2)}) collective-permute-start(f32[512,128]{1,0:T(8,128)S(1)} %get-tuple-element.31.after_ref.own_ref), channel_id=1, source_target_pairs={{1,2},{5,6},{9,10},{13,14},{17,18},{21,22},{25,26},{29,30},{0,3},{... | collective-permute-start | bytes 786440 | tf_op jit(solution)/shard_map/ppermute | solution.py:530
  6.4 14.5 %collective-permute-start.4 = (f32[512,128]{1,0:T(8,128)S(1)}, f32[512,128]{1,0:T(8,128)S(1)}, u32[]{:S(2)}, u32[]{:S(2)}) collective-permute-start(f32[512,128]{1,0:T(8,128)S(1)} %get-tuple-element.31.after_ref.own_ref), channel_id=1, source_target_pairs={{0,1},{2,3},{4,5},{6,7},{8,9},{10,11},{12,13},{14,15},{16,17},{18,... | collective-permute-start | bytes 786440 | tf_op jit(solution)/shard_map/ppermute | solution.py:530
  6.5 4.6 %copy-start.3 = (f32[8]{0:T(128)S(1)}, f32[8]{0:T(128)}, u32[]{:S(2)}) copy-start(f32[8]{0:T(128)} %dif_ref.1) | copy-start | bytes 100
  6.5 4.6 %copy-start.4 = (f32[8]{0:T(128)S(1)}, f32[8]{0:T(128)}, u32[]{:S(2)}) copy-start(f32[8]{0:T(128)} %sto_ref.1) | copy-start | bytes 100
  12.5 8.4 %collective-permute-start.6 = (f32[448,128]{1,0:T(8,128)S(1)}, f32[448,128]{1,0:T(8,128)S(1)}, u32[]{:S(2)}, u32[]{:S(2)}) collective-permute-start(f32[448,128]{1,0:T(8,128)S(1)} %get-tuple-element.38), channel_id=1, source_target_pairs={{0,1},{2,3},{4,5},{6,7},{8,9},{10,11},{12,13},{14,15},{16,17},{18,... | collective-permute-start | bytes 688136 | tf_op jit(solution)/shard_map/ppermute | solution.py:530
  12.6 8.4 %collective-permute-start.7 = (f32[448,128]{1,0:T(8,128)S(1)}, f32[448,128]{1,0:T(8,128)S(1)}, u32[]{:S(2)}, u32[]{:S(2)}) collective-permute-start(f32[448,128]{1,0:T(8,128)S(1)} %get-tuple-element.39), channel_id=1, source_target_pairs={{1,2},{5,6},{9,10},{13,14},{17,18},{21,22},{25,26},{29,30},{0,8},{... | collective-permute-start | bytes 688136 | tf_op jit(solution)/shard_map/ppermute | solution.py:530
  15.2 4.4 %collective-permute-start.2 = (f32[160,128]{1,0:T(8,128)S(1)}, f32[160,128]{1,0:T(8,128)S(1)}, u32[]{:S(2)}, u32[]{:S(2)}) collective-permute-start(f32[160,128]{1,0:T(8,128)S(1)} %get-tuple-element.36), channel_id=1, source_target_pairs={{0,4},{1,5},{2,6},{3,7},{8,12},{9,13},{10,14},{11,15},{16,20},{17,... | collective-permute-start | bytes 245768 | tf_op jit(solution)/shard_map/ppermute | solution.py:530
  19.7 1.3 %collective-permute-start.3 = (f32[160,128]{1,0:T(8,128)S(1)}, f32[160,128]{1,0:T(8,128)S(1)}, u32[]{:S(2)}, u32[]{:S(2)}) collective-permute-start(f32[160,128]{1,0:T(8,128)S(1)} %get-tuple-element.37), channel_id=1, source_target_pairs={{4,8},{5,9},{6,10},{7,11},{12,16},{13,17},{14,18},{15,19},{20,24},... | collective-permute-start | bytes 245768 | tf_op jit(solution)/shard_map/ppermute | solution.py:530
  26.1 12.8 %collective-permute-start.8 = (f32[352,128]{1,0:T(8,128)S(1)}, f32[352,128]{1,0:T(8,128)S(1)}, u32[]{:S(2)}, u32[]{:S(2)}) collective-permute-start(f32[352,128]{1,0:T(8,128)S(1)} %get-tuple-element.42), channel_id=1, source_target_pairs={{0,4},{1,5},{2,6},{3,7},{8,12},{9,13},{10,14},{11,15},{16,20},{17,... | collective-permute-start | bytes 540680 | tf_op jit(solution)/shard_map/ppermute | solution.py:530
  32.9 6.1 %collective-permute-start.9 = (f32[352,128]{1,0:T(8,128)S(1)}, f32[352,128]{1,0:T(8,128)S(1)}, u32[]{:S(2)}, u32[]{:S(2)}) collective-permute-start(f32[352,128]{1,0:T(8,128)S(1)} %get-tuple-element.43), channel_id=1, source_target_pairs={{4,8},{5,9},{6,10},{7,11},{12,16},{13,17},{14,18},{15,19},{20,24},... | collective-permute-start | bytes 540680 | tf_op jit(solution)/shard_map/ppermute | solution.py:530
  32.9 15.5 %collective-permute-start.13 = (f32[512,128]{1,0:T(8,128)S(1)}, f32[512,128]{1,0:T(8,128)S(1)}, u32[]{:S(2)}, u32[]{:S(2)}) collective-permute-start(f32[512,128]{1,0:T(8,128)S(1)} %get-tuple-element.41.own_ref), channel_id=1, source_target_pairs={{1,2},{5,6},{9,10},{13,14},{17,18},{21,22},{25,26},{29,30},{0,3},{... | collective-permute-start | bytes 786440 | tf_op jit(solution)/shard_map/ppermute | solution.py:530
  34.1 14.3 %collective-permute-start.12 = (f32[512,128]{1,0:T(8,128)S(1)}, f32[512,128]{1,0:T(8,128)S(1)}, u32[]{:S(2)}, u32[]{:S(2)}) collective-permute-start(f32[512,128]{1,0:T(8,128)S(1)} %get-tuple-element.41.own_ref), channel_id=1, source_target_pairs={{0,1},{2,3},{4,5},{6,7},{8,9},{10,11},{12,13},{14,15},{16,17},{18,... | collective-permute-start | bytes 786440 | tf_op jit(solution)/shard_map/ppermute | solution.py:530
  34.1 34.1 %copy-start.2 = (s32[4,2560]{1,0:T(4,128)S(1)}, s32[4,2560]{1,0:T(4,128)}, u32[]{:S(2)}) copy-start(s32[4,2560]{1,0:T(4,128)} %constant.2.clone.tables_ref) | copy-start | bytes 122884
  34.1 41.6 %copy-start.1 = (f32[96,96]{1,0:T(8,128)S(1)}, f32[96,96]{1,0:T(8,128)}, u32[]{:S(2)}) copy-start(f32[96,96]{1,0:T(8,128)} %gram_ref.1) | copy-start | bytes 110596
  39.0 9.4 %collective-permute-start.14 = (f32[448,128]{1,0:T(8,128)S(1)}, f32[448,128]{1,0:T(8,128)S(1)}, u32[]{:S(2)}, u32[]{:S(2)}) collective-permute-start(f32[448,128]{1,0:T(8,128)S(1)} %get-tuple-element.50), channel_id=1, source_target_pairs={{0,1},{2,3},{4,5},{6,7},{8,9},{10,11},{12,13},{14,15},{16,17},{18,... | collective-permute-start | bytes 688136 | tf_op jit(solution)/shard_map/ppermute | solution.py:530
  39.1 9.3 %collective-permute-start.15 = (f32[448,128]{1,0:T(8,128)S(1)}, f32[448,128]{1,0:T(8,128)S(1)}, u32[]{:S(2)}, u32[]{:S(2)}) collective-permute-start(f32[448,128]{1,0:T(8,128)S(1)} %get-tuple-element.51), channel_id=1, source_target_pairs={{1,2},{5,6},{9,10},{13,14},{17,18},{21,22},{25,26},{29,30},{0,8},{... | collective-permute-start | bytes 688136 | tf_op jit(solution)/shard_map/ppermute | solution.py:530
  42.6 4.4 %collective-permute-start.10 = (f32[160,128]{1,0:T(8,128)S(1)}, f32[160,128]{1,0:T(8,128)S(1)}, u32[]{:S(2)}, u32[]{:S(2)}) collective-permute-start(f32[160,128]{1,0:T(8,128)S(1)} %get-tuple-element.48), channel_id=1, source_target_pairs={{0,4},{1,5},{2,6},{3,7},{8,12},{9,13},{10,14},{11,15},{16,20},{17,... | collective-permute-start | bytes 245768 | tf_op jit(solution)/shard_map/ppermute | solution.py:530
  47.1 1.3 %collective-permute-start.11 = (f32[160,128]{1,0:T(8,128)S(1)}, f32[160,128]{1,0:T(8,128)S(1)}, u32[]{:S(2)}, u32[]{:S(2)}) collective-permute-start(f32[160,128]{1,0:T(8,128)S(1)} %get-tuple-element.49), channel_id=1, source_target_pairs={{4,8},{5,9},{6,10},{7,11},{12,16},{13,17},{14,18},{15,19},{20,24},... | collective-permute-start | bytes 245768 | tf_op jit(solution)/shard_map/ppermute | solution.py:530
  58.5 17.2 %all-to-all-start = ((f32[32,8,96]{2,1,0:T(8,128)}), f32[32,8,96]{2,1,0:T(8,128)S(1)}, u32[]{:S(2)}, u32[]{:S(2)}) async-start(f32[32,8,96]{2,1,0:T(8,128)} %project.3.after_ref), calls=%async_computation | async-start | bytes 262144 | tf_op jit(solution)/shard_map/all_to_all | solution.py:558

commit v6 on v5

--- a/solution.py
+++ b/solution.py
@@ -137,7 +137,8 @@
     )(diffusivity, stoich, after)
 
 
-def pack_kernel(cx, cy, nf, xa_ref, xb_ref, to_a_ref, to_b_ref):
+def pack_kernel(cx, cy, nf, xa_ref, xb_ref, after_ref, to_a_ref, to_b_ref):
+    del after_ref
     runs, size = corner_runs(cx)
 
     def copy(l_is_even):
@@ -151,18 +152,18 @@
     each_case(lax.rem(lax.axis_index("learn"), 2) == 0, copy)
 
 
-def pack_corners(xa, xb, cx, cy, nf):
+def pack_corners(xa, xb, after, cx, cy, nf):
     nz = xa.shape[1]
     size = 2 * corner_runs(cx)[1]
     shape = pltpu.VMEM((size * nf, nz), jnp.float32)
     return pl.pallas_call(
         functools.partial(pack_kernel, cx, cy, nf),
         out_shape=(shape, shape),
-        in_specs=[VMEM] * 2,
+        in_specs=[VMEM, VMEM, pl.BlockSpec(memory_space=pl.ANY)],
         out_specs=(VMEM, VMEM),
         compiler_params=pltpu.CompilerParams(vmem_limit_bytes=MIB),
         name="pack_corners",
-    )(*in_vmem(xa, xb))
+    )(*in_vmem(xa, xb), after)
 
 
 def load_kernel(source_ref, out_ref, sem):
@@ -378,11 +379,11 @@
     return high, middle, (rest - middle.astype(jnp.float32)).astype(jnp.bfloat16)
 
 
-def project_kernel(cx, cy, steps, copies, basis_ref, snap_ref, *refs):
-    earlier_ref, out_ref, acc_ref = refs if copies else (None, *refs)
-    modes, nf, _, nz = basis_ref.shape
+def project_kernel(cx, cy, steps, first, end, copies, basis_ref, snap_ref, *refs):
+    earlier_ref, out_ref, acc_ref = refs if len(refs) == 3 else (None, *refs)
+    modes, _, _, nz = basis_ref.shape
     pair = 2
-    for g in range(nf // pair):
+    for g in range(first // pair, end // pair):
         total = None
         for p in range(cx // 2):
             left, right = [], []
@@ -397,7 +398,7 @@
                 preferred_element_type=jnp.float32,
             )
             total = term if total is None else total + term
-        acc_ref[...] = total if g == 0 else acc_ref[...] + total
+        acc_ref[...] = total if g == first // pair else acc_ref[...] + total
 
     lanes = 8 * 2 * cy
     blocks = modes * 2 * cy // lanes
@@ -427,24 +428,24 @@
         for n in range(copies):
             out_ref[n] = both
     else:
-        out_ref[...] = result
-
-
-def project(basis, snaps, cx, cy, steps, earlier=None, copies=0):
+        out_ref[...] = result if earlier_ref is None else earlier_ref[...] + result
+
+
+def project(basis, snaps, cx, cy, steps, fields, earlier=None, copies=0):
     modes = basis.shape[0]
     shape = (steps, modes)
     operands = in_vmem(snaps)
     if copies:
         shape = (copies, earlier.shape[0] + steps, modes)
+    if earlier is not None:
         operands += in_vmem(earlier)
     return pl.pallas_call(
-        functools.partial(project_kernel, cx, cy, steps, copies),
+        functools.partial(project_kernel, cx, cy, steps, *fields, copies),
         out_shape=jax.ShapeDtypeStruct(shape, jnp.float32) if copies else pltpu.VMEM(shape, jnp.float32),
         in_specs=[VMEM] * (1 + len(operands)),
         out_specs=VMEM,
         scratch_shapes=[pltpu.VMEM((2 * steps * cy, modes * 2 * cy), jnp.float32)],
         compiler_params=pltpu.CompilerParams(vmem_limit_bytes=8 * MIB),
-        name="project",
     )(basis, *operands)
 
 
@@ -530,6 +531,22 @@
     return lax.ppermute(value, BOTH, pairs)
 
 
+def mark_kernel(after_ref, out_ref):
+    del after_ref
+    out_ref[...] = jnp.zeros_like(out_ref)
+
+
+def mark(after):
+    return pl.pallas_call(
+        mark_kernel,
+        out_shape=pltpu.VMEM((8, after.shape[1]), after.dtype),
+        in_specs=[pl.BlockSpec(memory_space=pl.ANY)],
+        out_specs=VMEM,
+        compiler_params=pltpu.CompilerParams(vmem_limit_bytes=MIB),
+        name="mark",
+    )(after)
+
+
 def body(fields, diffusivity, stoich, basis, gram_old):
     nf, cx, cy, nz = fields.shape
     ns, nl = lax.axis_size("sim"), lax.axis_size("learn")
@@ -537,7 +554,6 @@
     rounds = STEPS // steps
     x_even, x_odd, y_even, y_odd, y_far = swaps(ns, nl)
     state, *cuts = to_columns(fields)
-    factors = field_factors(diffusivity, stoich, nz, state)
     share = None
     for n in range(rounds):
         a1, b1 = swap(cuts[0], x_even), swap(cuts[1], x_odd)
@@ -545,16 +561,18 @@
         a2, b2 = swap(cuts[2], x_even), swap(cuts[3], x_odd)
         if n == 0:
             basis = load_basis(basis.reshape(basis.shape[0], nf, cx * cy, nz))
-            a1, b1, basis, factors = lax.optimization_barrier((a1, b1, basis, factors))
         else:
-            part = project(basis, snaps, cx, cy, steps)
-            a1, b1, part = lax.optimization_barrier((a1, b1, part))
+            part = project(basis, snaps, cx, cy, steps, (0, nf // 2))
+        to_a, to_b = pack_corners(a1, b1, mark(state), cx, cy, nf)
+        ca, cb = swap(to_a, y_even), swap(to_b, y_far)
+        if n == 0:
+            factors = field_factors(diffusivity, stoich, nz, to_b)
+        else:
+            part = project(basis, snaps, cx, cy, steps, (nf // 2, nf), part)
             share = part if share is None else jnp.concatenate([share, part], axis=0)
-        to_a, to_b = pack_corners(a1, b1, cx, cy, nf)
-        ca, cb = swap(to_a, y_even), swap(to_b, y_far)
         operands = (state, a1, b1, a2, b2, ya, yb, ca, cb, factors)
         state, snaps, *cuts = advance(operands, cx, cy, nf, steps, n == rounds - 1)
-    sent = project(basis, snaps, cx, cy, steps, share, ns * nl)
+    sent = project(basis, snaps, cx, cy, steps, (0, nf), share, ns * nl)
     shares = lax.all_to_all(sent, BOTH, 0, 0)
     block, picks = pick_matrices(gram_old.shape[0], nl, sent)
     reduced, pod_gram, rhs_block = infer(shares, gram_old, picks, block)

time: 77.2 us -> 82.5 us (1.069)
  waiting for transfers between devices: 17.4 us -> 24.2 us
  starting transfers between devices: 30.9 us -> 27.6 us
  local copies, waits for them, and re-layouts: 1.66 us -> 2.97 us
    ppermute x16, waiting for transfers between devices: 10 us -> 16.9 us  [swap(): return lax.ppermute(value, BOTH, pairs)]
    all_to_all x1, starting transfers between devices: 8.99 us -> 6.37 us  [body(): shares = lax.all_to_all(sent, BOTH, 0, 0)]
    unnamed x11, local copies, waits for them, and re-layouts: 1.66 us -> 2.97 us
    pallas_call x2 -> x5, Pallas kernels: 8.95 us -> 9.35 us  [the longest x3 9.34 us: project(): pl.pallas_call(functools.partial(project_kernel, cx, cy, steps, *fields,...]
  transfers between devices with their start and end apart: 17 -> 17, of which waited for: 7 -> 5; matrix products, arithmetic and copies ran while one was open for 1% -> 1% of each run, Pallas kernels for 12% -> 12%
where the time goes in v6:
time: 82.5 us; the launch traced here: 82.3 us
  starting transfers between devices  27.6 us (33%)
  Pallas kernels  26.6 us (32%)
  waiting for transfers between devices  24.2 us (29%)
  local copies, waits for them, and re-layouts  2.97 us (4%)
  between operations  0.85 us (1%)
    ppermute x16, starting transfers between devices, swap(): return lax.ppermute(value, BOTH, pairs)  21.3 us
    ppermute x16, waiting for transfers between devices, swap(): return lax.ppermute(value, BOTH, pairs)  16.9 us
    pallas_call x2, Pallas kernels, advance(): pl.pallas_call(functools.partial(round_kernel, cx, cy, nf, steps, last),...  10.4 us
    pallas_call x3, Pallas kernels, project(): pl.pallas_call(functools.partial(project_kernel, cx, cy, steps, *fields,...  9.34 us
    all_to_all x1, waiting for transfers between devices, body(): shares = lax.all_to_all(sent, BOTH, 0, 0)  7.38 us
    all_to_all x1, starting transfers between devices, body(): shares = lax.all_to_all(sent, BOTH, 0, 0)  6.37 us
    pallas_call x1, Pallas kernels, load_basis(): pl.pallas_call(load_kernel, out_shape=pltpu.VMEM(basis.shape, basis.dtype...  4.58 us
    unnamed x11, local copies, waits for them, and re-layouts  2.97 us
  transfers between devices with their start and end apart: 17, of which 5 were waited for; matrix products, arithmetic and copies ran while one was open for 1% of the time, Pallas kernels for 12%

profile of v6, /device:TPU:0, one launch (start us, length us, event | category | flops | bytes accessed | tf_op | source)
XLA Modules:
  0.0 82.3 jit_solution(14550964626070685420)
XLA Ops:
  0.6 0.9 %copy-done = f32[8,8,8,128]{3,2,1,0:T(8,128)S(1)} copy-done((f32[8,8,8,128]{3,2,1,0:T(8,128)S(1)}, f32[8,8,8,128]{3,2,1,0:T(8,128)}, u32[]{:S(2)}) %copy-start) | copy-done | bytes 262168
  1.6 0.2 to_columns.1
  1.8 3.0 %collective-permute-start = (f32[352,128]{1,0:T(8,128)S(1)}, f32[352,128]{1,0:T(8,128)S(1)}, u32[]{:S(2)}, u32[]{:S(2)}) collective-permute-start(f32[352,128]{1,0:T(8,128)S(1)} %get-tuple-element.25), channel_id=1, source_target_pairs={{0,4},{1,5},{2,6},{3,7},{8,12},{9,13},{10,14},{11,15},{16,20},{17,... | collective-permute-start | bytes 540680 | tf_op jit(solution)/shard_map/ppermute | solution.py:531
  4.8 0.0 collective-permute-start.1
  4.8 1.6 %collective-permute-start.5 = (f32[512,128]{1,0:T(8,128)S(1)}, f32[512,128]{1,0:T(8,128)S(1)}, u32[]{:S(2)}, u32[]{:S(2)}) collective-permute-start(f32[512,128]{1,0:T(8,128)S(1)} %get-tuple-element.24.after_ref.own_ref), channel_id=1, source_target_pairs={{1,2},{5,6},{9,10},{13,14},{17,18},{21,22},{25,26},{29,30},{0,3},{... | collective-permute-start | bytes 786440 | tf_op jit(solution)/shard_map/ppermute | solution.py:531
  6.4 0.0 collective-permute-start.4
  6.5 6.0 %collective-permute-done.xa_ref.a1_ref = f32[352,128]{1,0:T(8,128)S(1)} collective-permute-done((f32[352,128]{1,0:T(8,128)S(1)}, f32[352,128]{1,0:T(8,128)S(1)}, u32[]{:S(2)}, u32[]{:S(2)}) %collective-permute-start) | collective-permute-done | bytes 180256 | tf_op jit(solution)/shard_map/ppermute | solution.py:531
  12.5 0.0 collective-permute-done.1.xb_ref.b1_ref
  12.5 0.1 collective-permute-start.6
  12.6 2.6 %collective-permute-start.7 = (f32[448,128]{1,0:T(8,128)S(1)}, f32[448,128]{1,0:T(8,128)S(1)}, u32[]{:S(2)}, u32[]{:S(2)}) collective-permute-start(f32[448,128]{1,0:T(8,128)S(1)} %get-tuple-element.30.after_ref), channel_id=1, source_target_pairs={{1,2},{5,6},{9,10},{13,14},{17,18},{21,22},{25,26},{29,30},{0,8},{... | collective-permute-start | bytes 688136 | tf_op jit(solution)/shard_map/ppermute | solution.py:531
  15.2 1.5 %collective-permute-start.2 = (f32[160,128]{1,0:T(8,128)S(1)}, f32[160,128]{1,0:T(8,128)S(1)}, u32[]{:S(2)}, u32[]{:S(2)}) collective-permute-start(f32[160,128]{1,0:T(8,128)S(1)} %get-tuple-element.27), channel_id=1, source_target_pairs={{0,4},{1,5},{2,6},{3,7},{8,12},{9,13},{10,14},{11,15},{16,20},{17,... | collective-permute-start | bytes 245768 | tf_op jit(solution)/shard_map/ppermute | solution.py:531
  16.7 3.0 %collective-permute-done.2.a2_ref = f32[160,128]{1,0:T(8,128)S(1)} collective-permute-done((f32[160,128]{1,0:T(8,128)S(1)}, f32[160,128]{1,0:T(8,128)S(1)}, u32[]{:S(2)}, u32[]{:S(2)}) %collective-permute-start.2) | collective-permute-done | bytes 81952 | tf_op jit(solution)/shard_map/ppermute | solution.py:531
  19.7 0.0 collective-permute-start.3
  19.7 0.7 copy-done.3
  20.3 0.7 copy-done.4
  21.0 0.6 field_factors.1.factors_ref
  21.6 0.0 collective-permute-done.3.b2_ref
  21.6 0.0 collective-permute-done.5.yb_ref
  21.6 0.0 collective-permute-done.4.ya_ref
  21.6 0.0 collective-permute-done.6.ca_ref
  21.6 0.0 collective-permute-done.7.cb_ref
  21.6 5.1 %advance.2 = (f32[512,128]{1,0:T(8,128)S(1)}, f32[64,32,128]{2,1,0:T(8,128)S(1)}, f32[352,128]{1,0:T(8,128)S(1)}, f32[352,128]{1,0:T(8,128)S(1)}, f32[160,128]{1,0:T(8,128)S(1)}, /*index=5*/f32[160,128]{1,0:T(8,128)S(1)}) custom-call(f32[512,128]{1,0:T(8,128)S(1)} %get-tuple-element.24.after_ref.own_ref, f32[352,128]{1,0:T(8,128)S(1)} %collective-permute-done.xa_ref.a1_ref, ...), custom_call_target="tpu_custom_call" | custom-call | tf_op jit(solution)/shard_map/advance/pallas_call | solution.py:356
  26.8 6.1 %collective-permute-start.8 = (f32[352,128]{1,0:T(8,128)S(1)}, f32[352,128]{1,0:T(8,128)S(1)}, u32[]{:S(2)}, u32[]{:S(2)}) collective-permute-start(f32[352,128]{1,0:T(8,128)S(1)} %get-tuple-element.32), channel_id=1, source_target_pairs={{0,4},{1,5},{2,6},{3,7},{8,12},{9,13},{10,14},{11,15},{16,20},{17,... | collective-permute-start | bytes 540680 | tf_op jit(solution)/shard_map/ppermute | solution.py:531
  32.9 0.0 collective-permute-start.9
  32.9 1.2 %collective-permute-start.13 = (f32[512,128]{1,0:T(8,128)S(1)}, f32[512,128]{1,0:T(8,128)S(1)}, u32[]{:S(2)}, u32[]{:S(2)}) collective-permute-start(f32[512,128]{1,0:T(8,128)S(1)} %get-tuple-element.31.after_ref.own_ref), channel_id=1, source_target_pairs={{1,2},{5,6},{9,10},{13,14},{17,18},{21,22},{25,26},{29,30},{0,3},{... | collective-permute-start | bytes 786440 | tf_op jit(solution)/shard_map/ppermute | solution.py:531
  34.1 0.0 collective-permute-start.12
  34.1 4.9 %collective-permute-done.8.xa_ref.a1_ref = f32[352,128]{1,0:T(8,128)S(1)} collective-permute-done((f32[352,128]{1,0:T(8,128)S(1)}, f32[352,128]{1,0:T(8,128)S(1)}, u32[]{:S(2)}, u32[]{:S(2)}) %collective-permute-start.8) | collective-permute-done | bytes 180256 | tf_op jit(solution)/shard_map/ppermute | solution.py:531
  39.0 0.0 collective-permute-done.9.xb_ref.b1_ref
  39.0 0.1 collective-permute-start.14
  39.1 3.6 %collective-permute-start.15 = (f32[448,128]{1,0:T(8,128)S(1)}, f32[448,128]{1,0:T(8,128)S(1)}, u32[]{:S(2)}, u32[]{:S(2)}) collective-permute-start(f32[448,128]{1,0:T(8,128)S(1)} %get-tuple-element.37), channel_id=1, source_target_pairs={{1,2},{5,6},{9,10},{13,14},{17,18},{21,22},{25,26},{29,30},{0,8},{... | collective-permute-start | bytes 688136 | tf_op jit(solution)/shard_map/ppermute | solution.py:531
  42.6 1.5 %collective-permute-start.10 = (f32[160,128]{1,0:T(8,128)S(1)}, f32[160,128]{1,0:T(8,128)S(1)}, u32[]{:S(2)}, u32[]{:S(2)}) collective-permute-start(f32[160,128]{1,0:T(8,128)S(1)} %get-tuple-element.34), channel_id=1, source_target_pairs={{0,4},{1,5},{2,6},{3,7},{8,12},{9,13},{10,14},{11,15},{16,20},{17,... | collective-permute-start | bytes 245768 | tf_op jit(solution)/shard_map/ppermute | solution.py:531
  44.1 3.0 %collective-permute-done.10.a2_ref = f32[160,128]{1,0:T(8,128)S(1)} collective-permute-done((f32[160,128]{1,0:T(8,128)S(1)}, f32[160,128]{1,0:T(8,128)S(1)}, u32[]{:S(2)}, u32[]{:S(2)}) %collective-permute-start.10) | collective-permute-done | bytes 81952 | tf_op jit(solution)/shard_map/ppermute | solution.py:531
  47.1 4.6 %load_basis.1.basis_ref = bf16[96,8,64,128]{3,2,1,0:T(8,128)(2,1)S(1)} custom-call(bf16[96,8,64,128]{3,2,1,0:T(8,128)(2,1)} %bitcast.7), custom_call_target="tpu_custom_call" | custom-call | tf_op jit(solution)/shard_map/load_basis/pallas_call | solution.py:176
  51.7 2.3 %shard_map.93.refs_0_ = f32[4,96]{1,0:T(4,128)S(1)} custom-call(bf16[96,8,64,128]{3,2,1,0:T(8,128)(2,1)S(1)} %load_basis.1.basis_ref, f32[64,32,128]{2,1,0:T(8,128)S(1)} %get-tuple-element.40.snap_ref), custom_call_target="tpu_custom_call" | custom-call | tf_op jit(solution)/shard_map/pallas_call | solution.py:442
  53.9 0.0 copy-start.2
  54.0 0.0 copy-start.1
  54.0 2.3 %shard_map.94.refs_0_ = f32[4,96]{1,0:T(4,128)S(1)} custom-call(bf16[96,8,64,128]{3,2,1,0:T(8,128)(2,1)S(1)} %load_basis.1.basis_ref, f32[64,32,128]{2,1,0:T(8,128)S(1)} %get-tuple-element.40.snap_ref, f32[4,96]{1,0:T(4,128)S(1)} %shard_map.93.refs_0_), custom_call_target="tpu_custom_call" | custom-call | tf_op jit(solution)/shard_map/pallas_call | solution.py:442
  56.2 0.0 collective-permute-done.11.b2_ref
  56.3 0.0 collective-permute-done.13.yb_ref
  56.3 0.0 collective-permute-done.14.ca_ref
  56.3 0.0 collective-permute-done.15.cb_ref
  56.3 5.3 %advance.3 = (f32[512,128]{1,0:T(8,128)S(1)}, f32[64,32,128]{2,1,0:T(8,128)S(1)}) custom-call(f32[512,128]{1,0:T(8,128)S(1)} %get-tuple-element.31.after_ref.own_ref, f32[352,128]{1,0:T(8,128)S(1)} %collective-permute-done.8.xa_ref.a1_ref, f32[352,128]{1,0:T(8,128)S(1)} %collective-permute-done.9.xb_ref.b1_ref, ...), custom_call_target="tpu_custom_call" | custom-call | tf_op jit(solution)/shard_map/advance/pallas_call | solution.py:356
  61.6 4.8 %shard_map.95.after_ref = f32[32,8,96]{2,1,0:T(8,128)} custom-call(bf16[96,8,64,128]{3,2,1,0:T(8,128)(2,1)S(1)} %load_basis.1.basis_ref, f32[64,32,128]{2,1,0:T(8,128)S(1)} %get-tuple-element.39.snap_ref, f32[4,96]{1,0:T(4,128)S(1)} %shard_map.94.refs_0_), custom_call_target="tpu_custom_call" | custom-call | tf_op jit(solution)/shard_map/pallas_call | solution.py:442
  66.4 6.4 %all-to-all-start = ((f32[32,8,96]{2,1,0:T(8,128)}), f32[32,8,96]{2,1,0:T(8,128)S(1)}, u32[]{:S(2)}, u32[]{:S(2)}) async-start(f32[32,8,96]{2,1,0:T(8,128)} %shard_map.95.after_ref), calls=%async_computation | async-start | bytes 262144 | tf_op jit(solution)/shard_map/all_to_all | solution.py:576
  72.8 0.7 copy.10
  73.5 0.1 pick_matrices.1.picks_ref
  73.6 7.4 %all-to-all-done.shares_ref = f32[32,8,96]{2,1,0:T(8,128)S(1)} async-done(((f32[32,8,96]{2,1,0:T(8,128)}), f32[32,8,96]{2,1,0:T(8,128)S(1)}, u32[]{:S(2)}, u32[]{:S(2)}) %all-to-all-start) | async-done | bytes 98336 | tf_op jit(solution)/shard_map/all_to_all | solution.py:576
  81.0 1.3 %infer.1 = (f32[8,96]{1,0:T(8,128)}, f32[96,96]{1,0:T(8,128)}, f32[96,1188]{1,0:T(8,128)}) custom-call(f32[32,8,96]{2,1,0:T(8,128)S(1)} %all-to-all-done.shares_ref, f32[96,96]{1,0:T(8,128)S(1)} %copy-done.1, bf16[128,2560]{1,0:T(8,128)(2,1)S(1)} %pick_matrices.1.picks_ref), custom_call_target="tpu_custom_call" | custom-call | tf_op jit(solution)/shard_map/infer/pallas_call | solution.py:515
  (11 shorter events, 0.1 us)
Async XLA Ops:
  0.6 1.0 %copy-start = (f32[8,8,8,128]{3,2,1,0:T(8,128)S(1)}, f32[8,8,8,128]{3,2,1,0:T(8,128)}, u32[]{:S(2)}) copy-start(f32[8,8,8,128]{3,2,1,0:T(8,128)} %param.6) | copy-start | bytes 786436
  1.8 10.7 %collective-permute-start = (f32[352,128]{1,0:T(8,128)S(1)}, f32[352,128]{1,0:T(8,128)S(1)}, u32[]{:S(2)}, u32[]{:S(2)}) collective-permute-start(f32[352,128]{1,0:T(8,128)S(1)} %get-tuple-element.25), channel_id=1, source_target_pairs={{0,4},{1,5},{2,6},{3,7},{8,12},{9,13},{10,14},{11,15},{16,20},{17,... | collective-permute-start | bytes 540680 | tf_op jit(solution)/shard_map/ppermute | solution.py:531
  4.8 7.7 %collective-permute-start.1 = (f32[352,128]{1,0:T(8,128)S(1)}, f32[352,128]{1,0:T(8,128)S(1)}, u32[]{:S(2)}, u32[]{:S(2)}) collective-permute-start(f32[352,128]{1,0:T(8,128)S(1)} %get-tuple-element.26), channel_id=1, source_target_pairs={{4,8},{5,9},{6,10},{7,11},{12,16},{13,17},{14,18},{15,19},{20,24},... | collective-permute-start | bytes 540680 | tf_op jit(solution)/shard_map/ppermute | solution.py:531
  4.8 16.8 %collective-permute-start.5 = (f32[512,128]{1,0:T(8,128)S(1)}, f32[512,128]{1,0:T(8,128)S(1)}, u32[]{:S(2)}, u32[]{:S(2)}) collective-permute-start(f32[512,128]{1,0:T(8,128)S(1)} %get-tuple-element.24.after_ref.own_ref), channel_id=1, source_target_pairs={{1,2},{5,6},{9,10},{13,14},{17,18},{21,22},{25,26},{29,30},{0,3},{... | collective-permute-start | bytes 786440 | tf_op jit(solution)/shard_map/ppermute | solution.py:531
  6.4 15.1 %collective-permute-start.4 = (f32[512,128]{1,0:T(8,128)S(1)}, f32[512,128]{1,0:T(8,128)S(1)}, u32[]{:S(2)}, u32[]{:S(2)}) collective-permute-start(f32[512,128]{1,0:T(8,128)S(1)} %get-tuple-element.24.after_ref.own_ref), channel_id=1, source_target_pairs={{0,1},{2,3},{4,5},{6,7},{8,9},{10,11},{12,13},{14,15},{16,17},{18,... | collective-permute-start | bytes 786440 | tf_op jit(solution)/shard_map/ppermute | solution.py:531
  12.5 9.1 %collective-permute-start.6 = (f32[448,128]{1,0:T(8,128)S(1)}, f32[448,128]{1,0:T(8,128)S(1)}, u32[]{:S(2)}, u32[]{:S(2)}) collective-permute-start(f32[448,128]{1,0:T(8,128)S(1)} %get-tuple-element.29), channel_id=1, source_target_pairs={{0,1},{2,3},{4,5},{6,7},{8,9},{10,11},{12,13},{14,15},{16,17},{18,... | collective-permute-start | bytes 688136 | tf_op jit(solution)/shard_map/ppermute | solution.py:531
  12.6 9.0 %collective-permute-start.7 = (f32[448,128]{1,0:T(8,128)S(1)}, f32[448,128]{1,0:T(8,128)S(1)}, u32[]{:S(2)}, u32[]{:S(2)}) collective-permute-start(f32[448,128]{1,0:T(8,128)S(1)} %get-tuple-element.30.after_ref), channel_id=1, source_target_pairs={{1,2},{5,6},{9,10},{13,14},{17,18},{21,22},{25,26},{29,30},{0,8},{... | collective-permute-start | bytes 688136 | tf_op jit(solution)/shard_map/ppermute | solution.py:531
  15.2 4.4 %collective-permute-start.2 = (f32[160,128]{1,0:T(8,128)S(1)}, f32[160,128]{1,0:T(8,128)S(1)}, u32[]{:S(2)}, u32[]{:S(2)}) collective-permute-start(f32[160,128]{1,0:T(8,128)S(1)} %get-tuple-element.27), channel_id=1, source_target_pairs={{0,4},{1,5},{2,6},{3,7},{8,12},{9,13},{10,14},{11,15},{16,20},{17,... | collective-permute-start | bytes 245768 | tf_op jit(solution)/shard_map/ppermute | solution.py:531
  19.7 1.9 %collective-permute-start.3 = (f32[160,128]{1,0:T(8,128)S(1)}, f32[160,128]{1,0:T(8,128)S(1)}, u32[]{:S(2)}, u32[]{:S(2)}) collective-permute-start(f32[160,128]{1,0:T(8,128)S(1)} %get-tuple-element.28), channel_id=1, source_target_pairs={{4,8},{5,9},{6,10},{7,11},{12,16},{13,17},{14,18},{15,19},{20,24},... | collective-permute-start | bytes 245768 | tf_op jit(solution)/shard_map/ppermute | solution.py:531
  19.7 0.7 copy-start.3
  20.3 0.7 copy-start.4
  26.8 12.2 %collective-permute-start.8 = (f32[352,128]{1,0:T(8,128)S(1)}, f32[352,128]{1,0:T(8,128)S(1)}, u32[]{:S(2)}, u32[]{:S(2)}) collective-permute-start(f32[352,128]{1,0:T(8,128)S(1)} %get-tuple-element.32), channel_id=1, source_target_pairs={{0,4},{1,5},{2,6},{3,7},{8,12},{9,13},{10,14},{11,15},{16,20},{17,... | collective-permute-start | bytes 540680 | tf_op jit(solution)/shard_map/ppermute | solution.py:531
  32.9 6.1 %collective-permute-start.9 = (f32[352,128]{1,0:T(8,128)S(1)}, f32[352,128]{1,0:T(8,128)S(1)}, u32[]{:S(2)}, u32[]{:S(2)}) collective-permute-start(f32[352,128]{1,0:T(8,128)S(1)} %get-tuple-element.33), channel_id=1, source_target_pairs={{4,8},{5,9},{6,10},{7,11},{12,16},{13,17},{14,18},{15,19},{20,24},... | collective-permute-start | bytes 540680 | tf_op jit(solution)/shard_map/ppermute | solution.py:531
  32.9 23.4 %collective-permute-start.13 = (f32[512,128]{1,0:T(8,128)S(1)}, f32[512,128]{1,0:T(8,128)S(1)}, u32[]{:S(2)}, u32[]{:S(2)}) collective-permute-start(f32[512,128]{1,0:T(8,128)S(1)} %get-tuple-element.31.after_ref.own_ref), channel_id=1, source_target_pairs={{1,2},{5,6},{9,10},{13,14},{17,18},{21,22},{25,26},{29,30},{0,3},{... | collective-permute-start | bytes 786440 | tf_op jit(solution)/shard_map/ppermute | solution.py:531
  34.1 22.2 %collective-permute-start.12 = (f32[512,128]{1,0:T(8,128)S(1)}, f32[512,128]{1,0:T(8,128)S(1)}, u32[]{:S(2)}, u32[]{:S(2)}) collective-permute-start(f32[512,128]{1,0:T(8,128)S(1)} %get-tuple-element.31.after_ref.own_ref), channel_id=1, source_target_pairs={{0,1},{2,3},{4,5},{6,7},{8,9},{10,11},{12,13},{14,15},{16,17},{18,... | collective-permute-start | bytes 786440 | tf_op jit(solution)/shard_map/ppermute | solution.py:531
  39.0 17.3 %collective-permute-start.14 = (f32[448,128]{1,0:T(8,128)S(1)}, f32[448,128]{1,0:T(8,128)S(1)}, u32[]{:S(2)}, u32[]{:S(2)}) collective-permute-start(f32[448,128]{1,0:T(8,128)S(1)} %get-tuple-element.36), channel_id=1, source_target_pairs={{0,1},{2,3},{4,5},{6,7},{8,9},{10,11},{12,13},{14,15},{16,17},{18,... | collective-permute-start | bytes 688136 | tf_op jit(solution)/shard_map/ppermute | solution.py:531
  39.1 17.2 %collective-permute-start.15 = (f32[448,128]{1,0:T(8,128)S(1)}, f32[448,128]{1,0:T(8,128)S(1)}, u32[]{:S(2)}, u32[]{:S(2)}) collective-permute-start(f32[448,128]{1,0:T(8,128)S(1)} %get-tuple-element.37), channel_id=1, source_target_pairs={{1,2},{5,6},{9,10},{13,14},{17,18},{21,22},{25,26},{29,30},{0,8},{... | collective-permute-start | bytes 688136 | tf_op jit(solution)/shard_map/ppermute | solution.py:531
  42.6 4.4 %collective-permute-start.10 = (f32[160,128]{1,0:T(8,128)S(1)}, f32[160,128]{1,0:T(8,128)S(1)}, u32[]{:S(2)}, u32[]{:S(2)}) collective-permute-start(f32[160,128]{1,0:T(8,128)S(1)} %get-tuple-element.34), channel_id=1, source_target_pairs={{0,4},{1,5},{2,6},{3,7},{8,12},{9,13},{10,14},{11,15},{16,20},{17,... | collective-permute-start | bytes 245768 | tf_op jit(solution)/shard_map/ppermute | solution.py:531
  47.1 9.2 %collective-permute-start.11 = (f32[160,128]{1,0:T(8,128)S(1)}, f32[160,128]{1,0:T(8,128)S(1)}, u32[]{:S(2)}, u32[]{:S(2)}) collective-permute-start(f32[160,128]{1,0:T(8,128)S(1)} %get-tuple-element.35), channel_id=1, source_target_pairs={{4,8},{5,9},{6,10},{7,11},{12,16},{13,17},{14,18},{15,19},{20,24},... | collective-permute-start | bytes 245768 | tf_op jit(solution)/shard_map/ppermute | solution.py:531
  53.9 19.5 %copy-start.2 = (s32[4,2560]{1,0:T(4,128)S(1)}, s32[4,2560]{1,0:T(4,128)}, u32[]{:S(2)}) copy-start(s32[4,2560]{1,0:T(4,128)} %constant.2.clone.tables_ref) | copy-start | bytes 122884
  54.0 27.0 %copy-start.1 = (f32[96,96]{1,0:T(8,128)S(1)}, f32[96,96]{1,0:T(8,128)}, u32[]{:S(2)}) copy-start(f32[96,96]{1,0:T(8,128)} %gram_ref.1) | copy-start | bytes 110596
  66.4 14.6 %all-to-all-start = ((f32[32,8,96]{2,1,0:T(8,128)}), f32[32,8,96]{2,1,0:T(8,128)S(1)}, u32[]{:S(2)}, u32[]{:S(2)}) async-start(f32[32,8,96]{2,1,0:T(8,128)} %shard_map.95.after_ref), calls=%async_computation | async-start | bytes 262144 | tf_op jit(solution)/shard_map/all_to_all | solution.py:576

commit v7 on v6

--- a/solution.py
+++ b/solution.py
@@ -379,11 +379,11 @@
     return high, middle, (rest - middle.astype(jnp.float32)).astype(jnp.bfloat16)
 
 
-def project_kernel(cx, cy, steps, first, end, copies, basis_ref, snap_ref, *refs):
-    earlier_ref, out_ref, acc_ref = refs if len(refs) == 3 else (None, *refs)
-    modes, _, _, nz = basis_ref.shape
+def project_kernel(cx, cy, steps, copies, basis_ref, snap_ref, *refs):
+    earlier_ref, out_ref, acc_ref = refs if copies else (None, *refs)
+    modes, nf, _, nz = basis_ref.shape
     pair = 2
-    for g in range(first // pair, end // pair):
+    for g in range(nf // pair):
         total = None
         for p in range(cx // 2):
             left, right = [], []
@@ -398,7 +398,7 @@
                 preferred_element_type=jnp.float32,
             )
             total = term if total is None else total + term
-        acc_ref[...] = total if g == first // pair else acc_ref[...] + total
+        acc_ref[...] = total if g == 0 else acc_ref[...] + total
 
     lanes = 8 * 2 * cy
     blocks = modes * 2 * cy // lanes
@@ -428,24 +428,24 @@
         for n in range(copies):
             out_ref[n] = both
     else:
-        out_ref[...] = result if earlier_ref is None else earlier_ref[...] + result
-
-
-def project(basis, snaps, cx, cy, steps, fields, earlier=None, copies=0):
+        out_ref[...] = result
+
+
+def project(basis, snaps, cx, cy, steps, earlier=None, copies=0):
     modes = basis.shape[0]
     shape = (steps, modes)
     operands = in_vmem(snaps)
     if copies:
         shape = (copies, earlier.shape[0] + steps, modes)
-    if earlier is not None:
         operands += in_vmem(earlier)
     return pl.pallas_call(
-        functools.partial(project_kernel, cx, cy, steps, *fields, copies),
+        functools.partial(project_kernel, cx, cy, steps, copies),
         out_shape=jax.ShapeDtypeStruct(shape, jnp.float32) if copies else pltpu.VMEM(shape, jnp.float32),
         in_specs=[VMEM] * (1 + len(operands)),
         out_specs=VMEM,
         scratch_shapes=[pltpu.VMEM((2 * steps * cy, modes * 2 * cy), jnp.float32)],
         compiler_params=pltpu.CompilerParams(vmem_limit_bytes=8 * MIB),
+        name="project",
     )(basis, *operands)
 
 
@@ -562,17 +562,15 @@
         if n == 0:
             basis = load_basis(basis.reshape(basis.shape[0], nf, cx * cy, nz))
         else:
-            part = project(basis, snaps, cx, cy, steps, (0, nf // 2))
+            part = project(basis, snaps, cx, cy, steps)
+            share = part if share is None else jnp.concatenate([share, part], axis=0)
         to_a, to_b = pack_corners(a1, b1, mark(state), cx, cy, nf)
         ca, cb = swap(to_a, y_even), swap(to_b, y_far)
         if n == 0:
             factors = field_factors(diffusivity, stoich, nz, to_b)
-        else:
-            part = project(basis, snaps, cx, cy, steps, (nf // 2, nf), part)
-            share = part if share is None else jnp.concatenate([share, part], axis=0)
         operands = (state, a1, b1, a2, b2, ya, yb, ca, cb, factors)
         state, snaps, *cuts = advance(operands, cx, cy, nf, steps, n == rounds - 1)
-    sent = project(basis, snaps, cx, cy, steps, (0, nf), share, ns * nl)
+    sent = project(basis, snaps, cx, cy, steps, share, ns * nl)
     shares = lax.all_to_all(sent, BOTH, 0, 0)
     block, picks = pick_matrices(gram_old.shape[0], nl, sent)
     reduced, pod_gram, rhs_block = infer(shares, gram_old, picks, block)

time: 82.5 us -> 82.1 us (level)
    pallas_call x3 -> x2, Pallas kernels: 9.34 us -> 8.95 us  [project(): pl.pallas_call(functools.partial(project_kernel, cx, cy, steps, copies),...]
where the time goes in v7:
time: 82.1 us; the launch traced here: 81.9 us
  starting transfers between devices  27.7 us (34%)
  Pallas kernels  26.2 us (32%)
  waiting for transfers between devices  24.2 us (29%)
  local copies, waits for them, and re-layouts  2.97 us (4%)
  between operations  0.84 us (1%)
    ppermute x16, starting transfers between devices, swap(): return lax.ppermute(value, BOTH, pairs)  21.3 us
    ppermute x16, waiting for transfers between devices, swap(): return lax.ppermute(value, BOTH, pairs)  16.9 us
    pallas_call x2, Pallas kernels, advance(): pl.pallas_call(functools.partial(round_kernel, cx, cy, nf, steps, last),...  10.4 us
    pallas_call x2, Pallas kernels, project(): pl.pallas_call(functools.partial(project_kernel, cx, cy, steps, copies),...  8.95 us
    all_to_all x1, waiting for transfers between devices, body(): shares = lax.all_to_all(sent, BOTH, 0, 0)  7.38 us
    all_to_all x1, starting transfers between devices, body(): shares = lax.all_to_all(sent, BOTH, 0, 0)  6.38 us
    pallas_call x1, Pallas kernels, load_basis(): pl.pallas_call(load_kernel, out_shape=pltpu.VMEM(basis.shape, basis.dtype...  4.58 us
    unnamed x11, local copies, waits for them, and re-layouts  2.97 us
  transfers between devices with their start and end apart: 17, of which 5 were waited for; matrix products, arithmetic and copies ran while one was open for 1% of the time, Pallas kernels for 12%

profile of v7, /device:TPU:0, one launch (start us, length us, event | category | flops | bytes accessed | tf_op | source)
XLA Modules:
  0.0 81.9 jit_solution(7296467871093402421)
XLA Ops:
  0.6 0.9 %copy-done = f32[8,8,8,128]{3,2,1,0:T(8,128)S(1)} copy-done((f32[8,8,8,128]{3,2,1,0:T(8,128)S(1)}, f32[8,8,8,128]{3,2,1,0:T(8,128)}, u32[]{:S(2)}) %copy-start) | copy-done | bytes 262168
  1.6 0.2 to_columns.1
  1.8 3.0 %collective-permute-start = (f32[352,128]{1,0:T(8,128)S(1)}, f32[352,128]{1,0:T(8,128)S(1)}, u32[]{:S(2)}, u32[]{:S(2)}) collective-permute-start(f32[352,128]{1,0:T(8,128)S(1)} %get-tuple-element.25), channel_id=1, source_target_pairs={{0,4},{1,5},{2,6},{3,7},{8,12},{9,13},{10,14},{11,15},{16,20},{17,... | collective-permute-start | bytes 540680 | tf_op jit(solution)/shard_map/ppermute | solution.py:531
  4.8 0.0 collective-permute-start.1
  4.8 1.6 %collective-permute-start.5 = (f32[512,128]{1,0:T(8,128)S(1)}, f32[512,128]{1,0:T(8,128)S(1)}, u32[]{:S(2)}, u32[]{:S(2)}) collective-permute-start(f32[512,128]{1,0:T(8,128)S(1)} %get-tuple-element.24.after_ref.own_ref), channel_id=1, source_target_pairs={{1,2},{5,6},{9,10},{13,14},{17,18},{21,22},{25,26},{29,30},{0,3},{... | collective-permute-start | bytes 786440 | tf_op jit(solution)/shard_map/ppermute | solution.py:531
  6.4 0.0 collective-permute-start.4
  6.5 6.0 %collective-permute-done.xa_ref.a1_ref = f32[352,128]{1,0:T(8,128)S(1)} collective-permute-done((f32[352,128]{1,0:T(8,128)S(1)}, f32[352,128]{1,0:T(8,128)S(1)}, u32[]{:S(2)}, u32[]{:S(2)}) %collective-permute-start) | collective-permute-done | bytes 180256 | tf_op jit(solution)/shard_map/ppermute | solution.py:531
  12.5 0.0 collective-permute-done.1.xb_ref.b1_ref
  12.5 0.1 collective-permute-start.6
  12.6 2.6 %collective-permute-start.7 = (f32[448,128]{1,0:T(8,128)S(1)}, f32[448,128]{1,0:T(8,128)S(1)}, u32[]{:S(2)}, u32[]{:S(2)}) collective-permute-start(f32[448,128]{1,0:T(8,128)S(1)} %get-tuple-element.30.after_ref), channel_id=1, source_target_pairs={{1,2},{5,6},{9,10},{13,14},{17,18},{21,22},{25,26},{29,30},{0,8},{... | collective-permute-start | bytes 688136 | tf_op jit(solution)/shard_map/ppermute | solution.py:531
  15.2 1.5 %collective-permute-start.2 = (f32[160,128]{1,0:T(8,128)S(1)}, f32[160,128]{1,0:T(8,128)S(1)}, u32[]{:S(2)}, u32[]{:S(2)}) collective-permute-start(f32[160,128]{1,0:T(8,128)S(1)} %get-tuple-element.27), channel_id=1, source_target_pairs={{0,4},{1,5},{2,6},{3,7},{8,12},{9,13},{10,14},{11,15},{16,20},{17,... | collective-permute-start | bytes 245768 | tf_op jit(solution)/shard_map/ppermute | solution.py:531
  16.7 3.0 %collective-permute-done.2.a2_ref = f32[160,128]{1,0:T(8,128)S(1)} collective-permute-done((f32[160,128]{1,0:T(8,128)S(1)}, f32[160,128]{1,0:T(8,128)S(1)}, u32[]{:S(2)}, u32[]{:S(2)}) %collective-permute-start.2) | collective-permute-done | bytes 81952 | tf_op jit(solution)/shard_map/ppermute | solution.py:531
  19.7 0.0 collective-permute-start.3
  19.7 0.7 copy-done.3
  20.3 0.7 copy-done.4
  21.0 0.6 field_factors.1.factors_ref
  21.6 0.0 collective-permute-done.3.b2_ref
  21.6 0.0 collective-permute-done.5.yb_ref
  21.6 0.0 collective-permute-done.4.ya_ref
  21.6 0.0 collective-permute-done.6.ca_ref
  21.6 0.0 collective-permute-done.7.cb_ref
  21.6 5.1 %advance.2 = (f32[512,128]{1,0:T(8,128)S(1)}, f32[64,32,128]{2,1,0:T(8,128)S(1)}, f32[352,128]{1,0:T(8,128)S(1)}, f32[352,128]{1,0:T(8,128)S(1)}, f32[160,128]{1,0:T(8,128)S(1)}, /*index=5*/f32[160,128]{1,0:T(8,128)S(1)}) custom-call(f32[512,128]{1,0:T(8,128)S(1)} %get-tuple-element.24.after_ref.own_ref, f32[352,128]{1,0:T(8,128)S(1)} %collective-permute-done.xa_ref.a1_ref, ...), custom_call_target="tpu_custom_call" | custom-call | tf_op jit(solution)/shard_map/advance/pallas_call | solution.py:356
  26.8 6.1 %collective-permute-start.8 = (f32[352,128]{1,0:T(8,128)S(1)}, f32[352,128]{1,0:T(8,128)S(1)}, u32[]{:S(2)}, u32[]{:S(2)}) collective-permute-start(f32[352,128]{1,0:T(8,128)S(1)} %get-tuple-element.32), channel_id=1, source_target_pairs={{0,4},{1,5},{2,6},{3,7},{8,12},{9,13},{10,14},{11,15},{16,20},{17,... | collective-permute-start | bytes 540680 | tf_op jit(solution)/shard_map/ppermute | solution.py:531
  32.9 0.0 collective-permute-start.9
  32.9 1.2 %collective-permute-start.13 = (f32[512,128]{1,0:T(8,128)S(1)}, f32[512,128]{1,0:T(8,128)S(1)}, u32[]{:S(2)}, u32[]{:S(2)}) collective-permute-start(f32[512,128]{1,0:T(8,128)S(1)} %get-tuple-element.31.after_ref.own_ref), channel_id=1, source_target_pairs={{1,2},{5,6},{9,10},{13,14},{17,18},{21,22},{25,26},{29,30},{0,3},{... | collective-permute-start | bytes 786440 | tf_op jit(solution)/shard_map/ppermute | solution.py:531
  34.1 0.0 collective-permute-start.12
  34.1 4.9 %collective-permute-done.8.xa_ref.a1_ref = f32[352,128]{1,0:T(8,128)S(1)} collective-permute-done((f32[352,128]{1,0:T(8,128)S(1)}, f32[352,128]{1,0:T(8,128)S(1)}, u32[]{:S(2)}, u32[]{:S(2)}) %collective-permute-start.8) | collective-permute-done | bytes 180256 | tf_op jit(solution)/shard_map/ppermute | solution.py:531
  39.0 0.0 collective-permute-done.9.xb_ref.b1_ref
  39.0 0.1 collective-permute-start.14
  39.1 3.6 %collective-permute-start.15 = (f32[448,128]{1,0:T(8,128)S(1)}, f32[448,128]{1,0:T(8,128)S(1)}, u32[]{:S(2)}, u32[]{:S(2)}) collective-permute-start(f32[448,128]{1,0:T(8,128)S(1)} %get-tuple-element.37), channel_id=1, source_target_pairs={{1,2},{5,6},{9,10},{13,14},{17,18},{21,22},{25,26},{29,30},{0,8},{... | collective-permute-start | bytes 688136 | tf_op jit(solution)/shard_map/ppermute | solution.py:531
  42.6 1.5 %collective-permute-start.10 = (f32[160,128]{1,0:T(8,128)S(1)}, f32[160,128]{1,0:T(8,128)S(1)}, u32[]{:S(2)}, u32[]{:S(2)}) collective-permute-start(f32[160,128]{1,0:T(8,128)S(1)} %get-tuple-element.34), channel_id=1, source_target_pairs={{0,4},{1,5},{2,6},{3,7},{8,12},{9,13},{10,14},{11,15},{16,20},{17,... | collective-permute-start | bytes 245768 | tf_op jit(solution)/shard_map/ppermute | solution.py:531
  44.1 3.0 %collective-permute-done.10.a2_ref = f32[160,128]{1,0:T(8,128)S(1)} collective-permute-done((f32[160,128]{1,0:T(8,128)S(1)}, f32[160,128]{1,0:T(8,128)S(1)}, u32[]{:S(2)}, u32[]{:S(2)}) %collective-permute-start.10) | collective-permute-done | bytes 81952 | tf_op jit(solution)/shard_map/ppermute | solution.py:531
  47.1 0.0 collective-permute-start.11
  47.1 4.6 %load_basis.1.basis_ref = bf16[96,8,64,128]{3,2,1,0:T(8,128)(2,1)S(1)} custom-call(bf16[96,8,64,128]{3,2,1,0:T(8,128)(2,1)} %bitcast.7), custom_call_target="tpu_custom_call" | custom-call | tf_op jit(solution)/shard_map/load_basis/pallas_call | solution.py:176
  51.7 0.0 copy-start.2
  51.7 0.0 copy-start.1
  51.7 4.1 %project.2.refs_0_ = f32[4,96]{1,0:T(4,128)S(1)} custom-call(bf16[96,8,64,128]{3,2,1,0:T(8,128)(2,1)S(1)} %load_basis.1.basis_ref, f32[64,32,128]{2,1,0:T(8,128)S(1)} %get-tuple-element.40.snap_ref), custom_call_target="tpu_custom_call" | custom-call | tf_op jit(solution)/shard_map/project/pallas_call | solution.py:441
  55.8 0.0 collective-permute-done.11.b2_ref
  55.9 0.0 collective-permute-done.13.yb_ref
  55.9 0.0 collective-permute-done.14.ca_ref
  55.9 0.0 collective-permute-done.15.cb_ref
  55.9 5.3 %advance.3 = (f32[512,128]{1,0:T(8,128)S(1)}, f32[64,32,128]{2,1,0:T(8,128)S(1)}) custom-call(f32[512,128]{1,0:T(8,128)S(1)} %get-tuple-element.31.after_ref.own_ref, f32[352,128]{1,0:T(8,128)S(1)} %collective-permute-done.8.xa_ref.a1_ref, f32[352,128]{1,0:T(8,128)S(1)} %collective-permute-done.9.xb_ref.b1_ref, ...), custom_call_target="tpu_custom_call" | custom-call | tf_op jit(solution)/shard_map/advance/pallas_call | solution.py:356
  61.2 4.8 %project.3.after_ref = f32[32,8,96]{2,1,0:T(8,128)} custom-call(bf16[96,8,64,128]{3,2,1,0:T(8,128)(2,1)S(1)} %load_basis.1.basis_ref, f32[64,32,128]{2,1,0:T(8,128)S(1)} %get-tuple-element.39.snap_ref, f32[4,96]{1,0:T(4,128)S(1)} %project.2.refs_0_), custom_call_target="tpu_custom_call" | custom-call | tf_op jit(solution)/shard_map/project/pallas_call | solution.py:441
  66.0 6.4 %all-to-all-start = ((f32[32,8,96]{2,1,0:T(8,128)}), f32[32,8,96]{2,1,0:T(8,128)S(1)}, u32[]{:S(2)}, u32[]{:S(2)}) async-start(f32[32,8,96]{2,1,0:T(8,128)} %project.3.after_ref), calls=%async_computation | async-start | bytes 262144 | tf_op jit(solution)/shard_map/all_to_all | solution.py:574
  72.4 0.7 copy.10
  73.1 0.1 pick_matrices.1.picks_ref
  73.2 7.4 %all-to-all-done.shares_ref = f32[32,8,96]{2,1,0:T(8,128)S(1)} async-done(((f32[32,8,96]{2,1,0:T(8,128)}), f32[32,8,96]{2,1,0:T(8,128)S(1)}, u32[]{:S(2)}, u32[]{:S(2)}) %all-to-all-start) | async-done | bytes 98336 | tf_op jit(solution)/shard_map/all_to_all | solution.py:574
  80.6 1.3 %infer.1 = (f32[8,96]{1,0:T(8,128)}, f32[96,96]{1,0:T(8,128)}, f32[96,1188]{1,0:T(8,128)}) custom-call(f32[32,8,96]{2,1,0:T(8,128)S(1)} %all-to-all-done.shares_ref, f32[96,96]{1,0:T(8,128)S(1)} %copy-done.1, bf16[128,2560]{1,0:T(8,128)(2,1)S(1)} %pick_matrices.1.picks_ref), custom_call_target="tpu_custom_call" | custom-call | tf_op jit(solution)/shard_map/infer/pallas_call | solution.py:515
  (10 shorter events, 0.1 us)
Async XLA Ops:
  0.6 1.0 %copy-start = (f32[8,8,8,128]{3,2,1,0:T(8,128)S(1)}, f32[8,8,8,128]{3,2,1,0:T(8,128)}, u32[]{:S(2)}) copy-start(f32[8,8,8,128]{3,2,1,0:T(8,128)} %param.6) | copy-start | bytes 786436
  1.8 10.7 %collective-permute-start = (f32[352,128]{1,0:T(8,128)S(1)}, f32[352,128]{1,0:T(8,128)S(1)}, u32[]{:S(2)}, u32[]{:S(2)}) collective-permute-start(f32[352,128]{1,0:T(8,128)S(1)} %get-tuple-element.25), channel_id=1, source_target_pairs={{0,4},{1,5},{2,6},{3,7},{8,12},{9,13},{10,14},{11,15},{16,20},{17,... | collective-permute-start | bytes 540680 | tf_op jit(solution)/shard_map/ppermute | solution.py:531
  4.8 7.7 %collective-permute-start.1 = (f32[352,128]{1,0:T(8,128)S(1)}, f32[352,128]{1,0:T(8,128)S(1)}, u32[]{:S(2)}, u32[]{:S(2)}) collective-permute-start(f32[352,128]{1,0:T(8,128)S(1)} %get-tuple-element.26), channel_id=1, source_target_pairs={{4,8},{5,9},{6,10},{7,11},{12,16},{13,17},{14,18},{15,19},{20,24},... | collective-permute-start | bytes 540680 | tf_op jit(solution)/shard_map/ppermute | solution.py:531
  4.8 16.8 %collective-permute-start.5 = (f32[512,128]{1,0:T(8,128)S(1)}, f32[512,128]{1,0:T(8,128)S(1)}, u32[]{:S(2)}, u32[]{:S(2)}) collective-permute-start(f32[512,128]{1,0:T(8,128)S(1)} %get-tuple-element.24.after_ref.own_ref), channel_id=1, source_target_pairs={{1,2},{5,6},{9,10},{13,14},{17,18},{21,22},{25,26},{29,30},{0,3},{... | collective-permute-start | bytes 786440 | tf_op jit(solution)/shard_map/ppermute | solution.py:531
  6.4 15.1 %collective-permute-start.4 = (f32[512,128]{1,0:T(8,128)S(1)}, f32[512,128]{1,0:T(8,128)S(1)}, u32[]{:S(2)}, u32[]{:S(2)}) collective-permute-start(f32[512,128]{1,0:T(8,128)S(1)} %get-tuple-element.24.after_ref.own_ref), channel_id=1, source_target_pairs={{0,1},{2,3},{4,5},{6,7},{8,9},{10,11},{12,13},{14,15},{16,17},{18,... | collective-permute-start | bytes 786440 | tf_op jit(solution)/shard_map/ppermute | solution.py:531
  12.5 9.1 %collective-permute-start.6 = (f32[448,128]{1,0:T(8,128)S(1)}, f32[448,128]{1,0:T(8,128)S(1)}, u32[]{:S(2)}, u32[]{:S(2)}) collective-permute-start(f32[448,128]{1,0:T(8,128)S(1)} %get-tuple-element.29), channel_id=1, source_target_pairs={{0,1},{2,3},{4,5},{6,7},{8,9},{10,11},{12,13},{14,15},{16,17},{18,... | collective-permute-start | bytes 688136 | tf_op jit(solution)/shard_map/ppermute | solution.py:531
  12.6 9.0 %collective-permute-start.7 = (f32[448,128]{1,0:T(8,128)S(1)}, f32[448,128]{1,0:T(8,128)S(1)}, u32[]{:S(2)}, u32[]{:S(2)}) collective-permute-start(f32[448,128]{1,0:T(8,128)S(1)} %get-tuple-element.30.after_ref), channel_id=1, source_target_pairs={{1,2},{5,6},{9,10},{13,14},{17,18},{21,22},{25,26},{29,30},{0,8},{... | collective-permute-start | bytes 688136 | tf_op jit(solution)/shard_map/ppermute | solution.py:531
  15.2 4.4 %collective-permute-start.2 = (f32[160,128]{1,0:T(8,128)S(1)}, f32[160,128]{1,0:T(8,128)S(1)}, u32[]{:S(2)}, u32[]{:S(2)}) collective-permute-start(f32[160,128]{1,0:T(8,128)S(1)} %get-tuple-element.27), channel_id=1, source_target_pairs={{0,4},{1,5},{2,6},{3,7},{8,12},{9,13},{10,14},{11,15},{16,20},{17,... | collective-permute-start | bytes 245768 | tf_op jit(solution)/shard_map/ppermute | solution.py:531
  19.7 1.9 %collective-permute-start.3 = (f32[160,128]{1,0:T(8,128)S(1)}, f32[160,128]{1,0:T(8,128)S(1)}, u32[]{:S(2)}, u32[]{:S(2)}) collective-permute-start(f32[160,128]{1,0:T(8,128)S(1)} %get-tuple-element.28), channel_id=1, source_target_pairs={{4,8},{5,9},{6,10},{7,11},{12,16},{13,17},{14,18},{15,19},{20,24},... | collective-permute-start | bytes 245768 | tf_op jit(solution)/shard_map/ppermute | solution.py:531
  19.7 0.7 copy-start.3
  20.3 0.7 copy-start.4
  26.8 12.2 %collective-permute-start.8 = (f32[352,128]{1,0:T(8,128)S(1)}, f32[352,128]{1,0:T(8,128)S(1)}, u32[]{:S(2)}, u32[]{:S(2)}) collective-permute-start(f32[352,128]{1,0:T(8,128)S(1)} %get-tuple-element.32), channel_id=1, source_target_pairs={{0,4},{1,5},{2,6},{3,7},{8,12},{9,13},{10,14},{11,15},{16,20},{17,... | collective-permute-start | bytes 540680 | tf_op jit(solution)/shard_map/ppermute | solution.py:531
  32.9 6.1 %collective-permute-start.9 = (f32[352,128]{1,0:T(8,128)S(1)}, f32[352,128]{1,0:T(8,128)S(1)}, u32[]{:S(2)}, u32[]{:S(2)}) collective-permute-start(f32[352,128]{1,0:T(8,128)S(1)} %get-tuple-element.33), channel_id=1, source_target_pairs={{4,8},{5,9},{6,10},{7,11},{12,16},{13,17},{14,18},{15,19},{20,24},... | collective-permute-start | bytes 540680 | tf_op jit(solution)/shard_map/ppermute | solution.py:531
  32.9 23.0 %collective-permute-start.13 = (f32[512,128]{1,0:T(8,128)S(1)}, f32[512,128]{1,0:T(8,128)S(1)}, u32[]{:S(2)}, u32[]{:S(2)}) collective-permute-start(f32[512,128]{1,0:T(8,128)S(1)} %get-tuple-element.31.after_ref.own_ref), channel_id=1, source_target_pairs={{1,2},{5,6},{9,10},{13,14},{17,18},{21,22},{25,26},{29,30},{0,3},{... | collective-permute-start | bytes 786440 | tf_op jit(solution)/shard_map/ppermute | solution.py:531
  34.1 21.8 %collective-permute-start.12 = (f32[512,128]{1,0:T(8,128)S(1)}, f32[512,128]{1,0:T(8,128)S(1)}, u32[]{:S(2)}, u32[]{:S(2)}) collective-permute-start(f32[512,128]{1,0:T(8,128)S(1)} %get-tuple-element.31.after_ref.own_ref), channel_id=1, source_target_pairs={{0,1},{2,3},{4,5},{6,7},{8,9},{10,11},{12,13},{14,15},{16,17},{18,... | collective-permute-start | bytes 786440 | tf_op jit(solution)/shard_map/ppermute | solution.py:531
  39.0 16.9 %collective-permute-start.14 = (f32[448,128]{1,0:T(8,128)S(1)}, f32[448,128]{1,0:T(8,128)S(1)}, u32[]{:S(2)}, u32[]{:S(2)}) collective-permute-start(f32[448,128]{1,0:T(8,128)S(1)} %get-tuple-element.36), channel_id=1, source_target_pairs={{0,1},{2,3},{4,5},{6,7},{8,9},{10,11},{12,13},{14,15},{16,17},{18,... | collective-permute-start | bytes 688136 | tf_op jit(solution)/shard_map/ppermute | solution.py:531
  39.1 16.8 %collective-permute-start.15 = (f32[448,128]{1,0:T(8,128)S(1)}, f32[448,128]{1,0:T(8,128)S(1)}, u32[]{:S(2)}, u32[]{:S(2)}) collective-permute-start(f32[448,128]{1,0:T(8,128)S(1)} %get-tuple-element.37), channel_id=1, source_target_pairs={{1,2},{5,6},{9,10},{13,14},{17,18},{21,22},{25,26},{29,30},{0,8},{... | collective-permute-start | bytes 688136 | tf_op jit(solution)/shard_map/ppermute | solution.py:531
  42.6 4.4 %collective-permute-start.10 = (f32[160,128]{1,0:T(8,128)S(1)}, f32[160,128]{1,0:T(8,128)S(1)}, u32[]{:S(2)}, u32[]{:S(2)}) collective-permute-start(f32[160,128]{1,0:T(8,128)S(1)} %get-tuple-element.34), channel_id=1, source_target_pairs={{0,4},{1,5},{2,6},{3,7},{8,12},{9,13},{10,14},{11,15},{16,20},{17,... | collective-permute-start | bytes 245768 | tf_op jit(solution)/shard_map/ppermute | solution.py:531
  47.1 8.8 %collective-permute-start.11 = (f32[160,128]{1,0:T(8,128)S(1)}, f32[160,128]{1,0:T(8,128)S(1)}, u32[]{:S(2)}, u32[]{:S(2)}) collective-permute-start(f32[160,128]{1,0:T(8,128)S(1)} %get-tuple-element.35), channel_id=1, source_target_pairs={{4,8},{5,9},{6,10},{7,11},{12,16},{13,17},{14,18},{15,19},{20,24},... | collective-permute-start | bytes 245768 | tf_op jit(solution)/shard_map/ppermute | solution.py:531
  51.7 21.4 %copy-start.2 = (s32[4,2560]{1,0:T(4,128)S(1)}, s32[4,2560]{1,0:T(4,128)}, u32[]{:S(2)}) copy-start(s32[4,2560]{1,0:T(4,128)} %constant.2.clone.tables_ref) | copy-start | bytes 122884
  51.7 28.9 %copy-start.1 = (f32[96,96]{1,0:T(8,128)S(1)}, f32[96,96]{1,0:T(8,128)}, u32[]{:S(2)}) copy-start(f32[96,96]{1,0:T(8,128)} %gram_ref.1) | copy-start | bytes 110596
  66.0 14.6 %all-to-all-start = ((f32[32,8,96]{2,1,0:T(8,128)}), f32[32,8,96]{2,1,0:T(8,128)S(1)}, u32[]{:S(2)}, u32[]{:S(2)}) async-start(f32[32,8,96]{2,1,0:T(8,128)} %project.3.after_ref), calls=%async_computation | async-start | bytes 262144 | tf_op jit(solution)/shard_map/all_to_all | solution.py:574
